TPU v7x, 32 devices: a whole 2x2x4 slice. The times are simulated.
32 devices in a mesh: dp: 4 (over y, x), wide: 8 (over z, core).
Axes of the slice: x: 2, y: 2, z: 4, core: 2. Of those that a mesh axis runs over, the one named last changes fastest.
Arguments:
- tokens: bfloat16 [224, 196, 768], P(('dp', 'wide')), may hold values from -6 to 6
- norm1_gain: bfloat16 [768], replicated, may hold values from 0.5 to 1.5
- norm1_shift: bfloat16 [768], replicated, may hold values from -1.796875 to 1.796875
- qkv_weight: bfloat16 [768, 2304], replicated, may hold values from -0.21875 to 0.21875
- qv_bias: bfloat16 [2, 768], replicated, may hold values from -1.796875 to 1.796875
- rel_rows: bfloat16 [127, 64], replicated, may hold values from -0.8984375 to 0.8984375
- rel_cols: bfloat16 [127, 64], replicated, may hold values from -0.8984375 to 0.8984375
- out_weight: bfloat16 [768, 768], replicated, may hold values from -3.5 to 3.5
- out_bias: bfloat16 [768], replicated, may hold values from -1.796875 to 1.796875
- norm2_gain: bfloat16 [768], replicated, may hold values from 0.5 to 1.5
- norm2_shift: bfloat16 [768], replicated, may hold values from -1.796875 to 1.796875
- fc1_weight: bfloat16 [768, 3072], replicated, may hold values from -0.21875 to 0.21875
- fc1_bias: bfloat16 [3072], replicated, may hold values from -1.796875 to 1.796875
- fc2_weight: bfloat16 [3072, 768], replicated, may hold values from -0.109375 to 0.109375
- fc2_bias: bfloat16 [768], replicated, may hold values from -1.796875 to 1.796875
- window_place: int32 [200], P('dp'), may hold values from 0 to 55, as said below
- image_extent: int32 [8, 2], P('dp'), may hold values from 33 to 64, as said below
- box_mask: int32 [224, 196], P(('dp', 'wide')), may hold values 0 or 1
- out_grad: bfloat16 [224, 196, 768], P(('dp', 'wide')), may hold values from -6 to 6
Outputs:
- tokens_out: bfloat16 [224, 196, 768], P(('dp', 'wide'))
- tokens_grad: float32 [224, 196, 768], P(('dp', 'wide'))
- norm1_gain_grad: float32 [768], replicated
- norm1_shift_grad: float32 [768], replicated
- qkv_weight_grad: float32 [768, 2304], P('wide')
- qv_bias_grad: float32 [2, 768], replicated
- rel_rows_grad: float32 [127, 64], replicated
- rel_cols_grad: float32 [127, 64], replicated
- out_weight_grad: float32 [768, 768], P('wide')
- out_bias_grad: float32 [768], replicated
- norm2_gain_grad: float32 [768], replicated
- norm2_shift_grad: float32 [768], replicated
- fc1_weight_grad: float32 [768, 3072], P('wide')
- fc1_bias_grad: float32 [3072], replicated
- fc2_weight_grad: float32 [3072, 768], P('wide')
- fc2_bias_grad: float32 [768], replicated
Inputs may be any that keep to these rules, and one draw needn't show every extreme that they name: `window_place`: window t = n * 25 + w of group-local image n of a group sits on device (t + s) mod 8 of wide for a shift s drawn per group (s = 7 in the first group), in one of that device's 7 slots; no two windows of a group share a slot. Counting the windows on one device a whose image is that of a pair, over each run of 3 consecutive (image, head) pairs numbered head * 2 + image, gives at most 11. `image_extent`: the first image of each group has content in all its rows and columns.
All inputs are finite; a program needn't handle non-finite values. No bound on the sum of `box_mask` on one device may be relied on, other than what follows from the above.
Results may differ from a plain program's by a relative error of at most 0.012.
Values may be sent and summed in bfloat16 or wider, within the bound.
No kernel may reach another device: no remote copies, remote signals or barrier semaphores. Data moves between devices by JAX's collectives and lax.ppermute only.
A program may use at most 320 MiB of HBM per device.

v0:
```python
from functools import partial

import jax
import jax.numpy as jnp
from jax import lax
from jax.sharding import PartitionSpec as P

D = 768
HEADS = 12
HDIM = 64
GRID = 64
WIN = 14
WGRID = 5
PAIR_DEV = 3
WINS = 25
WTOK = 196


norm_eps = 1e-06
mask_fill = -1000000000.0


def product(left, right):
    return jnp.dot(left, right, preferred_element_type=jnp.float32)


def product_left(left, right):
    return lax.dot_general(
        left, right, (((0,), (0,)), ((), ())), preferred_element_type=jnp.float32
    )


def product_right(left, right):
    return lax.dot_general(
        left, right, (((1,), (1,)), ((), ())), preferred_element_type=jnp.float32
    )


def head_major(matrix):
    rows = matrix.shape[0]
    return matrix.reshape(rows, 3, HEADS, HDIM).transpose(0, 2, 1, 3).reshape(rows, 3 * D)


def part_major(matrix):
    rows = matrix.shape[0]
    return matrix.reshape(rows, HEADS, 3, HDIM).transpose(0, 2, 1, 3).reshape(rows, 3 * D)


def norm_rows(values, gain, shift):
    centre = values - jnp.mean(values, axis=-1, keepdims=True)
    spread = lax.rsqrt(jnp.mean(centre * centre, axis=-1, keepdims=True) + norm_eps)
    scaled = centre * spread
    return (scaled * gain + shift, scaled, spread)


def norm_back(grad_rows, scaled, spread, gain):
    weighted = grad_rows * gain
    return spread * (
        weighted
        - jnp.mean(weighted, axis=-1, keepdims=True)
        - scaled * jnp.mean(weighted * scaled, axis=-1, keepdims=True)
    )


def send_plan(window_place, slot_count, image_count, wide_index, capacity, wide_count):
    window_total = window_place.shape[0]
    owners = window_place // slot_count
    placed = window_place % slot_count
    window_ids = jnp.arange(window_total, dtype=jnp.int32)
    slot_ids = jnp.arange(slot_count, dtype=jnp.int32)
    matches = (owners[None, :] == wide_index) & (placed[None, :] == slot_ids[:, None])
    occupied = jnp.any(matches, axis=1)
    window_of = jnp.sum(jnp.where(matches, window_ids[None, :], 0), axis=1)
    pair_of = (
        jnp.arange(HEADS, dtype=jnp.int32)[None, :] * image_count + (window_of // WINS)[:, None]
    )
    targets = (pair_of // PAIR_DEV).reshape(-1)
    ordering = (pair_of * window_total + window_of[:, None]).reshape(-1)
    live_items = jnp.repeat(occupied, HEADS)
    earlier = (
        live_items[None, :]
        & (targets[None, :] == targets[:, None])
        & (ordering[None, :] < ordering[:, None])
    )
    ranking = jnp.sum(earlier.astype(jnp.int32), axis=1)
    position = jnp.where(live_items, targets * capacity + ranking, wide_count * capacity)
    return (occupied, window_of, live_items, position)


def receive_plan(window_place, slot_count, image_count, wide_index, capacity):
    window_total = window_place.shape[0]
    owners = window_place // slot_count
    pair_ids = wide_index * PAIR_DEV + jnp.arange(PAIR_DEV, dtype=jnp.int32)
    pair_image = pair_ids % image_count
    window_of = (pair_image[:, None] * WINS + jnp.arange(WINS, dtype=jnp.int32)[None, :]).reshape(
        -1
    )
    picked = window_of[:, None] == jnp.arange(window_total, dtype=jnp.int32)[None, :]
    sender = jnp.sum(jnp.where(picked, owners[None, :], 0), axis=1)
    ordering = jnp.repeat(pair_ids, WINS) * window_total + window_of
    earlier = (sender[None, :] == sender[:, None]) & (ordering[None, :] < ordering[:, None])
    ranking = jnp.sum(earlier.astype(jnp.int32), axis=1)
    return (sender * capacity + ranking, pair_image)


def patch_mask(occupied, window_of):
    cell_ids = jnp.arange(WTOK, dtype=jnp.int32)
    local_window = window_of % WINS
    grid_row = (local_window // WGRID)[:, None] * WIN + (cell_ids // WIN)[None, :]
    grid_col = (local_window % WGRID)[:, None] * WIN + (cell_ids % WIN)[None, :]
    inside = occupied[:, None] & (grid_row < GRID) & (grid_col < GRID)
    return inside.astype(jnp.float32)


def to_items(values, slot_count, part_count):
    shaped = values.reshape(slot_count, WTOK, HEADS, part_count * HDIM).transpose(0, 2, 1, 3)
    return shaped.reshape(slot_count * HEADS, WTOK * part_count * HDIM)


def from_items(item_rows, slot_count, part_count):
    shaped = item_rows.reshape(slot_count, HEADS, WTOK, part_count * HDIM).transpose(0, 2, 1, 3)
    return shaped.reshape(slot_count * WTOK, HEADS * part_count * HDIM)


def pack_items(item_rows, targets, length, wide_count):
    blank_rows = jnp.zeros((length, item_rows.shape[1]), item_rows.dtype)
    filled = blank_rows.at[targets].set(item_rows, mode="drop")
    return filled.reshape(wide_count, length // wide_count, item_rows.shape[1])


def unpack_items(arrived, position, live_items, length):
    flattened = arrived.reshape(length, -1)
    picked = flattened[jnp.minimum(position, length - 1)]
    return jnp.where(live_items[:, None], picked, jnp.zeros_like(picked))


def grid_from_items(item_rows, pair_count, part_count):
    padded_side = WGRID * WIN
    shaped = item_rows.reshape(pair_count, WGRID, WGRID, WIN, WIN, part_count * HDIM)
    shaped = shaped.transpose(0, 1, 3, 2, 4, 5).reshape(
        pair_count, padded_side, padded_side, part_count * HDIM
    )
    return shaped[:, :GRID, :GRID].reshape(pair_count, GRID * GRID, part_count, HDIM)


def items_from_grid(grid_values, pair_count):
    channels = grid_values.shape[-1]
    margin = WGRID * WIN - GRID
    padded = jnp.pad(
        grid_values.reshape(pair_count, GRID, GRID, channels),
        ((0, 0), (0, margin), (0, margin), (0, 0)),
    )
    shaped = padded.reshape(pair_count, WGRID, WIN, WGRID, WIN, channels).transpose(
        0, 1, 3, 2, 4, 5
    )
    return shaped.reshape(pair_count * WINS, WTOK * channels)


def offset_table():
    offsets = (
        jnp.arange(GRID, dtype=jnp.int32)[:, None]
        - jnp.arange(GRID, dtype=jnp.int32)[None, :]
        + GRID
        - 1
    )
    return offsets.reshape(-1)[:, None] == jnp.arange(2 * GRID - 1, dtype=jnp.int32)[None, :]


def key_bias(pair_image, image_extent):
    image_count = image_extent.shape[0]
    chosen = pair_image[:, None] == jnp.arange(image_count, dtype=jnp.int32)[None, :]
    extent_rows = jnp.sum(jnp.where(chosen, image_extent[None, :, 0], 0), axis=1)
    extent_cols = jnp.sum(jnp.where(chosen, image_extent[None, :, 1], 0), axis=1)
    grid_ids = jnp.arange(GRID, dtype=jnp.int32)[None, :]
    row_bias_terms = jnp.where(grid_ids < extent_rows[:, None], 0.0, mask_fill).astype(jnp.float32)
    column_bias_terms = jnp.where(grid_ids < extent_cols[:, None], 0.0, mask_fill).astype(
        jnp.float32
    )
    return (row_bias_terms, column_bias_terms)


def rel_terms(
    queries, row_position_table, column_position_table, row_bias_terms, column_bias_terms
):
    pair_count = queries.shape[0]
    grid_queries = queries.reshape(pair_count, GRID, GRID, HDIM)
    row_partial = jnp.einsum(
        "jrcd,rkd->jrck", grid_queries, row_position_table, preferred_element_type=jnp.float32
    )
    column_partial = jnp.einsum(
        "jrcd,ckd->jrck", grid_queries, column_position_table, preferred_element_type=jnp.float32
    )
    row_partial = row_partial + row_bias_terms[:, None, None, :]
    column_partial = column_partial + column_bias_terms[:, None, None, :]
    return (
        row_partial.reshape(pair_count, GRID * GRID, GRID),
        column_partial.reshape(pair_count, GRID * GRID, GRID),
    )


def block_scores(query_tile_rows, key_rows, row_block_terms, column_block_terms, score_scale):
    pair_count, block_rows = (query_tile_rows.shape[0], query_tile_rows.shape[1])
    raw_scores = (
        jnp.einsum("jbd,jnd->jbn", query_tile_rows, key_rows, preferred_element_type=jnp.float32)
        * score_scale
    )
    raw_scores = raw_scores.reshape(pair_count, block_rows, GRID, GRID)
    raw_scores = raw_scores + row_block_terms[:, :, :, None] + column_block_terms[:, :, None, :]
    return raw_scores.reshape(pair_count, block_rows, GRID * GRID)


def attention_forward(queries, key_rows, values, rel_rows_part, rel_cols_part):
    pair_count, patch_count = (queries.shape[0], queries.shape[1])
    block_rows = min(512, patch_count)
    score_scale = HDIM ** (-0.5)

    def one_block(block_id, carry):
        out_buffer, total_buffer = carry
        first_row = block_id * block_rows
        query_tile_rows = lax.dynamic_slice_in_dim(queries, first_row, block_rows, 1)
        row_block_terms = lax.dynamic_slice_in_dim(rel_rows_part, first_row, block_rows, 1)
        column_block_terms = lax.dynamic_slice_in_dim(rel_cols_part, first_row, block_rows, 1)
        scores = block_scores(
            query_tile_rows, key_rows, row_block_terms, column_block_terms, score_scale
        )
        highest = jnp.max(scores, axis=-1, keepdims=True)
        totals = highest + jnp.log(jnp.sum(jnp.exp(scores - highest), axis=-1, keepdims=True))
        weights_low = jnp.exp(scores - totals).astype(jnp.bfloat16)
        outputs = jnp.einsum(
            "jbn,jnd->jbd", weights_low, values, preferred_element_type=jnp.float32
        )
        out_buffer = lax.dynamic_update_slice_in_dim(
            out_buffer, outputs.astype(jnp.bfloat16), first_row, 1
        )
        total_buffer = lax.dynamic_update_slice_in_dim(total_buffer, totals[:, :, 0], first_row, 1)
        return (out_buffer, total_buffer)

    initial = (
        jnp.zeros((pair_count, patch_count, HDIM), jnp.bfloat16),
        jnp.zeros((pair_count, patch_count), jnp.float32),
    )
    return lax.fori_loop(0, patch_count // block_rows, one_block, initial)


def attention_backward(queries, key_rows, values, rel_rows_part, rel_cols_part, totals, grad_pairs):
    pair_count, patch_count = (queries.shape[0], queries.shape[1])
    block_rows = min(512, patch_count)
    score_scale = HDIM ** (-0.5)

    def one_block(block_id, running):
        grad_keys, grad_values, query_buffer, rows_buffer, cols_buffer = running
        first_row = block_id * block_rows
        query_tile_rows = lax.dynamic_slice_in_dim(queries, first_row, block_rows, 1)
        row_block_terms = lax.dynamic_slice_in_dim(rel_rows_part, first_row, block_rows, 1)
        column_block_terms = lax.dynamic_slice_in_dim(rel_cols_part, first_row, block_rows, 1)
        total_block = lax.dynamic_slice_in_dim(totals, first_row, block_rows, 1)
        grad_block = lax.dynamic_slice_in_dim(grad_pairs, first_row, block_rows, 1)
        scores = block_scores(
            query_tile_rows, key_rows, row_block_terms, column_block_terms, score_scale
        )
        weights = jnp.exp(scores - total_block[:, :, None])
        grad_weights = jnp.einsum(
            "jbd,jnd->jbn", grad_block, values, preferred_element_type=jnp.float32
        )
        inner = jnp.sum(weights * grad_weights, axis=-1, keepdims=True)
        grad_scores = (weights * (grad_weights - inner)).astype(jnp.bfloat16)
        grad_keys = grad_keys + score_scale * jnp.einsum(
            "jbn,jbd->jnd", grad_scores, query_tile_rows, preferred_element_type=jnp.float32
        )
        grad_values = grad_values + jnp.einsum(
            "jbn,jbd->jnd",
            weights.astype(jnp.bfloat16),
            grad_block,
            preferred_element_type=jnp.float32,
        )
        grad_query = score_scale * jnp.einsum(
            "jbn,jnd->jbd", grad_scores, key_rows, preferred_element_type=jnp.float32
        )
        folded = grad_scores.astype(jnp.float32).reshape(pair_count, block_rows, GRID, GRID)
        query_buffer = lax.dynamic_update_slice_in_dim(query_buffer, grad_query, first_row, 1)
        rows_buffer = lax.dynamic_update_slice_in_dim(
            rows_buffer, jnp.sum(folded, axis=3), first_row, 1
        )
        cols_buffer = lax.dynamic_update_slice_in_dim(
            cols_buffer, jnp.sum(folded, axis=2), first_row, 1
        )
        return (grad_keys, grad_values, query_buffer, rows_buffer, cols_buffer)

    initial = (
        jnp.zeros((pair_count, patch_count, HDIM), jnp.float32),
        jnp.zeros((pair_count, patch_count, HDIM), jnp.float32),
        jnp.zeros((pair_count, patch_count, HDIM), jnp.float32),
        jnp.zeros((pair_count, patch_count, GRID), jnp.float32),
        jnp.zeros((pair_count, patch_count, GRID), jnp.float32),
    )
    grad_keys, grad_values, grad_query, grad_rows, grad_cols = lax.fori_loop(
        0, patch_count // block_rows, one_block, initial
    )
    return (grad_query, grad_keys, grad_values, grad_rows, grad_cols)


def rel_back(queries, row_position_table, column_position_table, grad_rows, grad_cols, picks):
    pair_count = queries.shape[0]
    exact_result = lax.Precision.HIGHEST
    grid_queries = queries.astype(jnp.float32).reshape(pair_count, GRID, GRID, HDIM)
    rows_four = grad_rows.reshape(pair_count, GRID, GRID, GRID)
    cols_four = grad_cols.reshape(pair_count, GRID, GRID, GRID)
    rel_query = jnp.einsum(
        "jrck,rkd->jrcd", rows_four, row_position_table.astype(jnp.float32), precision=exact_result
    )
    rel_query = rel_query + jnp.einsum(
        "jrck,ckd->jrcd",
        cols_four,
        column_position_table.astype(jnp.float32),
        precision=exact_result,
    )
    table_rows = jnp.einsum(
        "jrck,jrcd->rkd", rows_four, grid_queries, precision=exact_result
    ).reshape(GRID * GRID, HDIM)
    table_cols = jnp.einsum(
        "jrck,jrcd->ckd", cols_four, grid_queries, precision=exact_result
    ).reshape(GRID * GRID, HDIM)
    pick_values = picks.astype(jnp.float32)
    rows_grad = lax.dot_general(
        pick_values,
        table_rows,
        (((0,), (0,)), ((), ())),
        precision=exact_result,
        preferred_element_type=jnp.float32,
    )
    cols_grad = lax.dot_general(
        pick_values,
        table_cols,
        (((0,), (0,)), ((), ())),
        precision=exact_result,
        preferred_element_type=jnp.float32,
    )
    return (rel_query.reshape(pair_count, GRID * GRID, HDIM), rows_grad, cols_grad)


def shards(
    tokens,
    norm1_gain,
    norm1_shift,
    qkv_weight,
    qv_bias,
    rel_rows,
    rel_cols,
    out_weight,
    out_bias,
    norm2_gain,
    norm2_shift,
    fc1_weight,
    fc1_bias,
    fc2_weight,
    fc2_bias,
    window_place,
    image_extent,
    box_mask,
    out_grad,
):
    wide_count = lax.axis_size("wide")
    wide_index = lax.axis_index("wide")
    capacity = max(2, 88 // wide_count)
    length = wide_count * capacity
    slot_count = tokens.shape[0]
    image_count = image_extent.shape[0]
    row_count = slot_count * WTOK
    occupied, window_of, live_items, position = send_plan(
        window_place, slot_count, image_count, wide_index, capacity, wide_count
    )
    gather_index, pair_image = receive_plan(
        window_place, slot_count, image_count, wide_index, capacity
    )
    present = patch_mask(occupied, window_of).reshape(row_count, 1)
    qkv_heads = head_major(qkv_weight)
    inputs = tokens.reshape(row_count, D).astype(jnp.float32)
    normed1, scaled1, spread1 = norm_rows(
        inputs, norm1_gain.astype(jnp.float32), norm1_shift.astype(jnp.float32)
    )
    normed1 = normed1.astype(jnp.bfloat16)
    bias_rows = jnp.stack([qv_bias[0], jnp.zeros((D,), qv_bias.dtype), qv_bias[1]]).astype(
        jnp.float32
    )
    bias_full = head_major(bias_rows.reshape(1, 3 * D))[0]
    qkv_values = (product(normed1, qkv_heads) + bias_full).astype(jnp.bfloat16)
    qkv_packed = pack_items(to_items(qkv_values, slot_count, 3), position, length, wide_count)
    arrived_qkv = lax.all_to_all(qkv_packed, "wide", split_axis=0, concat_axis=0, tiled=True)
    pair_grid = grid_from_items(arrived_qkv.reshape(length, -1)[gather_index], PAIR_DEV, 3)
    queries, key_rows, values = (pair_grid[:, :, 0], pair_grid[:, :, 1], pair_grid[:, :, 2])
    picks = offset_table()
    row_position_table = (
        product(picks.astype(jnp.bfloat16), rel_rows).astype(jnp.bfloat16).reshape(GRID, GRID, HDIM)
    )
    column_position_table = (
        product(picks.astype(jnp.bfloat16), rel_cols).astype(jnp.bfloat16).reshape(GRID, GRID, HDIM)
    )
    row_bias_terms, column_bias_terms = key_bias(pair_image, image_extent)
    rel_rows_part, rel_cols_part = rel_terms(
        queries, row_position_table, column_position_table, row_bias_terms, column_bias_terms
    )
    attended_pairs, totals = attention_forward(
        queries, key_rows, values, rel_rows_part, rel_cols_part
    )
    out_packed = pack_items(
        items_from_grid(attended_pairs, PAIR_DEV), gather_index, length, wide_count
    )
    returned = lax.all_to_all(out_packed, "wide", split_axis=0, concat_axis=0, tiled=True)
    attended = from_items(unpack_items(returned, position, live_items, length), slot_count, 1)
    branch = product(attended, out_weight) + out_bias.astype(jnp.float32)
    middle = inputs + branch
    normed2, scaled2, spread2 = norm_rows(
        middle, norm2_gain.astype(jnp.float32), norm2_shift.astype(jnp.float32)
    )
    normed2 = normed2.astype(jnp.bfloat16)
    before = product(normed2, fc1_weight) + fc1_bias.astype(jnp.float32)
    activated, gelu_pull = jax.vjp(partial(jax.nn.gelu, approximate=False), before)
    act_low = activated.astype(jnp.bfloat16)
    result = middle + product(act_low, fc2_weight) + fc2_bias.astype(jnp.float32)
    tokens_out = (result * present).astype(jnp.bfloat16).reshape(tokens.shape)
    row_weight = box_mask.reshape(row_count, 1).astype(jnp.float32) * present
    grad_result = out_grad.reshape(row_count, D).astype(jnp.float32) * row_weight
    grad_low = grad_result.astype(jnp.bfloat16)
    fc2_weight_grad = product_left(act_low, grad_low)
    fc2_bias_grad = jnp.sum(grad_result, axis=0)
    grad_before = gelu_pull(product_right(grad_low, fc2_weight))[0].astype(jnp.bfloat16)
    fc1_weight_grad = product_left(normed2, grad_before)
    fc1_bias_grad = jnp.sum(grad_before.astype(jnp.float32), axis=0)
    grad_normed2 = product_right(grad_before, fc1_weight)
    norm2_gain_grad = jnp.sum(grad_normed2 * scaled2, axis=0)
    norm2_shift_grad = jnp.sum(grad_normed2, axis=0)
    grad_middle = grad_result + norm_back(
        grad_normed2, scaled2, spread2, norm2_gain.astype(jnp.float32)
    )
    grad_branch = grad_middle.astype(jnp.bfloat16)
    out_weight_grad = product_left(attended, grad_branch)
    out_bias_grad = jnp.sum(grad_branch.astype(jnp.float32), axis=0)
    grad_attended = product_right(grad_branch, out_weight).astype(jnp.bfloat16)
    grad_packed = pack_items(to_items(grad_attended, slot_count, 1), position, length, wide_count)
    resent_qkv, grad_arrived = (
        lax.all_to_all(qkv_packed, "wide", split_axis=0, concat_axis=0, tiled=True),
        lax.all_to_all(grad_packed, "wide", split_axis=0, concat_axis=0, tiled=True),
    )
    resent_grid = grid_from_items(resent_qkv.reshape(length, -1)[gather_index], PAIR_DEV, 3)
    queries, key_rows, values = (resent_grid[:, :, 0], resent_grid[:, :, 1], resent_grid[:, :, 2])
    grad_pairs = grid_from_items(grad_arrived.reshape(length, -1)[gather_index], PAIR_DEV, 1)[
        :, :, 0
    ]
    grad_query_part, grad_keys, grad_values, grad_rows, grad_cols = attention_backward(
        queries, key_rows, values, rel_rows_part, rel_cols_part, totals, grad_pairs
    )
    rel_query, rel_rows_grad, rel_cols_grad = rel_back(
        queries, row_position_table, column_position_table, grad_rows, grad_cols, picks
    )
    grad_query = (grad_query_part + rel_query).astype(jnp.bfloat16)
    stacked = jnp.concatenate(
        [grad_query, grad_keys.astype(jnp.bfloat16), grad_values.astype(jnp.bfloat16)], axis=2
    )
    back_packed = pack_items(items_from_grid(stacked, PAIR_DEV), gather_index, length, wide_count)
    grad_returned = lax.all_to_all(back_packed, "wide", split_axis=0, concat_axis=0, tiled=True)
    grad_qkv = from_items(unpack_items(grad_returned, position, live_items, length), slot_count, 3)
    qkv_weight_grad = part_major(product_left(normed1, grad_qkv))
    bias_sums = jnp.sum(grad_qkv.astype(jnp.float32), axis=0).reshape(HEADS, 3, HDIM)
    qv_bias_grad = jnp.stack([bias_sums[:, 0].reshape(D), bias_sums[:, 2].reshape(D)])
    grad_normed1 = product_right(grad_qkv, qkv_heads)
    norm1_gain_grad = jnp.sum(grad_normed1 * scaled1, axis=0)
    norm1_shift_grad = jnp.sum(grad_normed1, axis=0)
    grad_inputs = (
        grad_middle + norm_back(grad_normed1, scaled1, spread1, norm1_gain.astype(jnp.float32))
    ) * present
    tokens_grad = grad_inputs.reshape(tokens.shape)
    large_grads = (qkv_weight_grad, out_weight_grad, fc1_weight_grad, fc2_weight_grad)
    shares = (
        lax.psum_scatter(large_grads[0], "wide", scatter_dimension=0, tiled=True),
        lax.psum_scatter(large_grads[1], "wide", scatter_dimension=0, tiled=True),
        lax.psum_scatter(large_grads[2], "wide", scatter_dimension=0, tiled=True),
        lax.psum_scatter(large_grads[3], "wide", scatter_dimension=0, tiled=True),
    )
    shares = lax.psum((shares[0], shares[1], shares[2], shares[3]), "dp")
    small_grads = lax.psum(
        (
            norm1_gain_grad,
            norm1_shift_grad,
            qv_bias_grad,
            rel_rows_grad,
            rel_cols_grad,
            out_bias_grad,
            norm2_gain_grad,
            norm2_shift_grad,
            fc1_bias_grad,
            fc2_bias_grad,
        ),
        ("dp", "wide"),
    )
    return (
        tokens_out,
        tokens_grad,
        small_grads[0],
        small_grads[1],
        shares[0],
        small_grads[2],
        small_grads[3],
        small_grads[4],
        shares[1],
        small_grads[5],
        small_grads[6],
        small_grads[7],
        shares[2],
        small_grads[8],
        shares[3],
        small_grads[9],
    )


def solution(mesh):
    placed = (
        P(("dp", "wide"), None, None),
        P(),
        P(),
        P(),
        P(),
        P(),
        P(),
        P(),
        P(),
        P(),
        P(),
        P(),
        P(),
        P(),
        P(),
        P("dp"),
        P("dp", None),
        P(("dp", "wide"), None),
        P(("dp", "wide"), None, None),
    )
    return jax.shard_map(
        shards,
        mesh=mesh,
        in_specs=placed,
        out_specs=(
            P(("dp", "wide"), None, None),
            P(("dp", "wide"), None, None),
            P(),
            P(),
            P("wide", None),
            P(),
            P(),
            P(),
            P("wide", None),
            P(),
            P(),
            P(),
            P("wide", None),
            P(),
            P("wide", None),
            P(),
        ),
        check_vma=False,
    )
```

profile of v0, /device:TPU:0, one launch (start us, length us, event | category | flops | bytes accessed | tf_op | source)
XLA Modules:
  0.0 4604.6 jit_solution(16657492129168396268)
XLA Ops:
  132.1 202.9 %all-to-all-done = bf16[8,11,37632]{2,1,0:T(8,128)(2,1)} async-done(((bf16[8,11,37632]{2,1,0:T(8,128)(2,1)}), bf16[8,11,37632]{2,1,0:T(8,128)(2,1)}, u32[]{:S(2)}, u32[]{:S(2)}) %all-to-all-start) | async-done | bytes 6623264 | tf_op jit(solution)/shard_map/all_to_all | solution.py:388
  487.7 976.9 %while.37 = (s32[]{:T(128)}, bf16[3,4096,64]{1,2,0:T(8,128)(2,1)}, f32[3,4096]{1,0:T(4,128)S(1)}, bf16[3,4096,64]{1,2,0:T(8,128)(2,1)}, bf16[3,4096,64]{1,2,0:T(...) while((s32[]{:T(128)}, bf16[3,4096,64]{1,2,0:T(8,128)(2,1)}, ...), condition=%wide.region_13.14_spmd, body=%wide.region_10.13_spmd.sunk | while | flops 1661041152 | bytes 289071296 | solution.py:242
  684.3 26.2 fusion.142
  806.4 26.2 fusion.142
  1050.6 26.2 fusion.142
  1416.8 26.2 fusion.142
  1512.5 65.2 %all-to-all-done.1 = bf16[8,11,12544]{2,1,0:T(8,128)(2,1)} async-done(((bf16[8,11,12544]{2,1,0:T(8,128)(2,1)}), bf16[8,11,12544]{2,1,0:T(8,128)(2,1)}, u32[]{:S(2)}, u32[]{:S(2)}) %all-to-all-start.1) | async-done | bytes 2207776 | tf_op jit(solution)/shard_map/all_to_all | solution.py:408
  1612.2 49.0 %multiply_convert_fusion.1 = (bf16[1372,3072]{1,0:T(8,128)(2,1)}, f32[1372,3072]{1,0:T(8,128)}, f32[1372,3072]{1,0:T(8,128)}) fusion(f32[3072]{0:T(1024)S(1)} %convert_element_type.194, bf16[768,3072]{1,0:T(8,128)(2,1)} %param.34, f32[1372,768]{1,0:T(8,128)S(1)} %get-tuple-element.654, f32[768]{0:T(1024)S(1)} %convert_element_type.192, ...), kind=kOutput, calls=%fused_computation.51 | convolution fusion | flops 6757352448 | bytes 51110624 | tf_op jit(solution)/shard_map/dot_general | solution.py:24
  1740.6 72.9 %all-to-all-done.2 = bf16[8,11,12544]{2,1,0:T(8,128)(2,1)} async-done(((bf16[8,11,12544]{2,1,0:T(8,128)(2,1)}), bf16[8,11,12544]{2,1,0:T(8,128)(2,1)}, u32[]{:S(2)}, u32[]{:S(2)}) %all-to-all-start.2) | async-done | bytes 2207776 | tf_op jit(solution)/shard_map/all_to_all | solution.py:442
  1853.2 1717.0 %while.38 = (s32[]{:T(128)}, f32[3,4096,64]{1,2,0:T(8,128)}, f32[3,4096,64]{1,2,0:T(8,128)}, f32[3,4096,64]{1,2,0:T(8,128)}, f32[3,4096,64]{1,2,0:T(8,128)}, /*i...) while((s32[]{:T(128)}, f32[3,4096,64]{1,2,0:T(8,128)}, ...), condition=%wide.region_24.25_spmd.clone, body=%wide.region_20.24_spmd.clone.sunk | while | flops 4105861632 | bytes 501381312 | solution.py:296
  1942.8 34.2 multiply_reduce_fusion.11
  2155.8 34.2 multiply_reduce_fusion.11
  2370.5 34.2 multiply_reduce_fusion.11
  2585.4 34.2 multiply_reduce_fusion.11
  2800.1 34.2 multiply_reduce_fusion.11
  3014.9 34.2 multiply_reduce_fusion.11
  3229.7 34.2 multiply_reduce_fusion.11
  3444.5 34.2 multiply_reduce_fusion.11
  3723.6 208.7 %all-to-all-done.3 = bf16[8,11,37632]{2,1,0:T(8,128)(2,1)} async-done(((bf16[8,11,37632]{2,1,0:T(8,128)(2,1)}), bf16[8,11,37632]{2,1,0:T(8,128)(2,1)}, u32[]{:S(2)}, u32[]{:S(2)}) %all-to-all-start.3) | async-done | bytes 6623264 | tf_op jit(solution)/shard_map/all_to_all | solution.py:460
  4108.7 35.0 reduce-scatter.7.cloned.1.call-done
  4143.7 101.1 %reduce-scatter.11.cloned.1.call-done = f32[384,768]{1,0:T(8,128)} async-done(((f32[3072,768]{1,0:T(8,128)}), f32[384,768]{1,0:T(8,128)}) %reduce-scatter.11.cloned.1.call-update) | async-done | bytes 1179664 | tf_op jit(solution)/shard_map/reduce_scatter | solution.py:477
  4244.8 100.1 %reduce-scatter.9.cloned.1.call-done = f32[96,3072]{1,0:T(8,128)} async-done(((f32[768,3072]{1,0:T(8,128)}), f32[96,3072]{1,0:T(8,128)}) %reduce-scatter.9.cloned.1.call-update) | async-done | bytes 1179664 | tf_op jit(solution)/shard_map/reduce_scatter | solution.py:476
  4386.6 59.9 %all-reduce.9.cloned.1.call-done = (f32[96,2304]{0,1:T(8,128)}, f32[96,768]{1,0:T(8,128)}, f32[96,3072]{1,0:T(8,128)}, f32[384,768]{1,0:T(8,128)}) async-done(((f32[96,2304]{0,1:T(8,128)}, f32[96,768]{1,0:T(8,128)}, f32[96,3072]{1,0:T(8,128)}, f32[384,768]{1,0:T(8,128)}), (f32[96,2304]{0,1:T(8,128)}, f32[96,768]{1,0:T(8,128)}, f32[96,3072]{1,0:T(8,128)}, f32[384,768]{1,0:T(8,128)})) %all-reduce.9.cloned.1.call-update) | async-done | bytes 3538960 | tf_op jit(solution)/shard_map/psum | solution.py:479
  4449.1 131.0 %all-reduce.7.cloned.1.call-done = (f32[768]{0:T(1024)}, f32[768]{0:T(1024)}, f32[2,768]{1,0:T(2,128)}, f32[127,64]{0,1:T(8,128)}, f32[127,64]{0,1:T(8,128)}, /*...) async-done(((f32[768]{0:T(1024)}, f32[768]{0:T(1024)}, f32[2,768]{1,0:T(2,128)}, f32[127,64]{0,1:T(8,128)}, f32[127,64]{0,1:T(8,128)}, ...) | async-done | bytes 101904 | tf_op jit(solution)/shard_map/psum | solution.py:480
  (570 shorter events, 3184.2 us)
Async XLA Ops:
  7.2 1599.4 %copy-start = (bf16[768,768]{1,0:T(8,128)(2,1)S(1)}, bf16[768,768]{1,0:T(8,128)(2,1)}, u32[]{:S(2)}) copy-start(bf16[768,768]{1,0:T(8,128)(2,1)} %param.30) | copy-start | bytes 3538948
  13.8 80.0 %copy-start.68 = (s32[84]{0:T(128)}, s32[84]{0:T(128)S(1)}, u32[]{:S(2)}) copy-start(s32[84]{0:T(128)S(1)} %fusion.72) | copy-start | bytes 1012
  117.9 217.1 %all-to-all-start = ((bf16[8,11,37632]{2,1,0:T(8,128)(2,1)}), bf16[8,11,37632]{2,1,0:T(8,128)(2,1)}, u32[]{:S(2)}, u32[]{:S(2)}) async-start(bf16[8,11,37632]{2,1,0:T(8,128)(2,1)} %reshape.878), calls=%async_computation | async-start | bytes 19267584 | tf_op jit(solution)/shard_map/all_to_all | solution.py:388
  124.8 219.5 %copy-start.22 = (s32[4096]{0:T(1024)}, s32[4096]{0:T(1024)S(1)}, u32[]{:S(2)}) copy-start(s32[4096]{0:T(1024)S(1)} %sub.223) | copy-start | bytes 49156
  131.6 212.7 %copy-start.49 = (s32[1024]{0:T(1024)}, s32[1024]{0:T(1024)S(1)}, u32[]{:S(2)}) copy-start(s32[1024]{0:T(1024)S(1)} %pad_clamp_fusion.1) | copy-start | bytes 12292
  1500.2 77.5 %all-to-all-start.1 = ((bf16[8,11,12544]{2,1,0:T(8,128)(2,1)}), bf16[8,11,12544]{2,1,0:T(8,128)(2,1)}, u32[]{:S(2)}, u32[]{:S(2)}) async-start(bf16[8,11,12544]{2,1,0:T(8,128)(2,1)} %reshape.890), calls=%async_computation.1 | async-start | bytes 6422528 | tf_op jit(solution)/shard_map/all_to_all | solution.py:408
  1507.4 191.9 %copy-start.38 = (f32[768]{0:T(1024)}, f32[768]{0:T(1024)S(1)}, u32[]{:S(2)}) copy-start(f32[768]{0:T(1024)S(1)} %convert_element_type.191) | copy-start | bytes 9220
  1507.4 104.8 %copy-start.53 = (f32[768]{0:T(1024)}, f32[768]{0:T(1024)S(1)}, u32[]{:S(2)}) copy-start(f32[768]{0:T(1024)S(1)} %convert_element_type.192) | copy-start | bytes 9220
  1512.5 71.4 %copy-start.48 = (s32[1024]{0:T(1024)}, s32[1024]{0:T(1024)S(1)}, u32[]{:S(2)}) copy-start(s32[1024]{0:T(1024)S(1)} %pad_clamp_fusion) | copy-start | bytes 12292
  1611.6 49.6 %copy-start.8 = (f32[1372,768]{1,0:T(8,128)}, f32[1372,768]{1,0:T(8,128)S(1)}, u32[]{:S(2)}) copy-start(f32[1372,768]{1,0:T(8,128)S(1)} %get-tuple-element.654) | copy-start | bytes 12644356
  1611.6 87.7 %copy-start.26 = (f32[1372]{0:T(1024)}, f32[1372]{0:T(1024)S(1)}, u32[]{:S(2)}) copy-start(f32[1372]{0:T(1024)S(1)} %broadcast_multiply_fusion.4) | copy-start | bytes 16468
  1612.2 87.1 %copy-start.36 = (f32[1372]{0:T(1024)}, f32[1372]{0:T(1024)S(1)}, u32[]{:S(2)}) copy-start(f32[1372]{0:T(1024)S(1)} %add_rsqrt_fusion) | copy-start | bytes 16468
  1612.2 49.0 %copy-start.34 = (f32[1372]{0:T(1024)S(1)}, f32[1372]{0:T(1024)}, u32[]{:S(2)}) copy-start(f32[1372]{0:T(1024)} %reshape.921) | copy-start | bytes 16468
  1736.1 77.4 %all-to-all-start.2 = ((bf16[8,11,12544]{2,1,0:T(8,128)(2,1)}), bf16[8,11,12544]{2,1,0:T(8,128)(2,1)}, u32[]{:S(2)}, u32[]{:S(2)}) async-start(bf16[8,11,12544]{2,1,0:T(8,128)(2,1)} %reshape.896), calls=%async_computation.2 | async-start | bytes 6422528 | tf_op jit(solution)/shard_map/all_to_all | solution.py:442
  3716.6 215.8 %all-to-all-start.3 = ((bf16[8,11,37632]{2,1,0:T(8,128)(2,1)}), bf16[8,11,37632]{2,1,0:T(8,128)(2,1)}, u32[]{:S(2)}, u32[]{:S(2)}) async-start(bf16[8,11,37632]{2,1,0:T(8,128)(2,1)} %reshape.906), calls=%async_computation.3 | async-start | bytes 19267584 | tf_op jit(solution)/shard_map/all_to_all | solution.py:460
  3721.8 384.4 %reduce-scatter.13.cloned.1.call-start = ((), (), s32[]{:S(2)}) async-start(), calls=%async_computation.11 | async-start | bytes 7962624
  4029.8 113.9 %reduce-scatter.7.cloned.1.call-start = ((), (), s32[]{:S(2)}) async-start(), calls=%async_computation.8 | async-start | bytes 2654208 | tf_op jit(solution)/shard_map/reduce_scatter | solution.py:475
  4037.0 207.7 %reduce-scatter.11.cloned.1.call-start = ((), (), s32[]{:S(2)}) async-start(), calls=%async_computation.10 | async-start | bytes 10616832 | tf_op jit(solution)/shard_map/reduce_scatter | solution.py:477
  4051.0 293.8 %reduce-scatter.9.cloned.1.call-start = ((), (), s32[]{:S(2)}) async-start(), calls=%async_computation.9 | async-start | bytes 10616832 | tf_op jit(solution)/shard_map/reduce_scatter | solution.py:476
  4066.0 380.5 %all-reduce.9.cloned.1.call-start = ((), (), s32[]{:S(2)}) async-start(), calls=%async_computation.13 | async-start | bytes 7667712 | tf_op jit(solution)/shard_map/psum | solution.py:479
  4344.9 235.2 %all-reduce.7.cloned.1.call-start = ((), (), s32[]{:S(2)}) async-start(), calls=%async_computation.12 | async-start | bytes 217088 | tf_op jit(solution)/shard_map/psum | solution.py:480
  4381.3 216.1 %copy-start.1 = (bf16[768,768]{1,0:T(8,128)(2,1)S(1)}, bf16[768,768]{1,0:T(8,128)(2,1)}, u32[]{:S(2)}) copy-start(bf16[768,768]{1,0:T(8,128)(2,1)} %param.30) | copy-start | bytes 3538948
  4446.5 149.4 %copy-start.20 = (f32[384,768]{1,0:T(8,128)S(1)}, f32[384,768]{1,0:T(8,128)}, u32[]{:S(2)}) copy-start(f32[384,768]{1,0:T(8,128)} %get-tuple-element.916) | copy-start | bytes 3538948
  4580.1 16.8 copy-start.56
  (62 other events, 349.7 us)
Sparse Core Ops, SparseCore 0:
  4029.9 76.1 reduce-scatter.12
  4109.1 34.5 reduce-scatter.6
  4146.0 98.7 reduce-scatter.10
  4246.9 97.8 reduce-scatter.8
  4348.7 97.7 all-reduce.8
  4453.9 126.1 all-reduce.6
where the time goes:
time: 4640 us; the launch traced here: 4600 us
  local copies, waits for them, and re-layouts  1950 us (42%)
  matrix products  1170 us (25%)
  waiting for transfers between devices  991 us (21%)
  other arithmetic  457 us (10%)
    add x64, local copies, waits for them, and re-layouts, block_scores(): raw_scores + row_block_terms[:, :, :, None]  1170 us
    dot_general x16, matrix products, block_scores(): jnp.einsum('jbd,jnd->jbn', query_tile_rows, key_rows, preferred_element_t...  483 us
    all_to_all x1, waiting for transfers between devices, shards(): lax.all_to_all(back_packed, 'wide', split_axis=0, concat_axis=0, tiled=True)  209 us
    all_to_all x1, waiting for transfers between devices, shards(): lax.all_to_all(qkv_packed, 'wide', split_axis=0, concat_axis=0, tiled=True)  203 us
    convert_element_type x8, other arithmetic, one_block(): grad_scores = (weights * (grad_weights - inner)).astype(jnp.bfloat16)  172 us
    reshape x8, local copies, waits for them, and re-layouts, one_block(): grad_scores.astype(jnp.float32).reshape(pair_count, block_rows, GRID, GRID)  142 us
    psum x1, waiting for transfers between devices, shards(): lax.psum((norm1_gain_grad, norm1_shift_grad, qv_bias_grad, rel_rows_grad,...  131 us
    dot_general x8, matrix products, one_block(): jnp.einsum('jbd,jnd->jbn', grad_block, values, preferred_element_type=jnp...  107 us
  transfers between devices with their start and end apart: 10, of which 10 were waited for; matrix products, arithmetic and copies ran while one was open for 3% of the time, Pallas kernels for 0%

commit v1 on v0

--- a/solution.py
+++ b/solution.py
@@ -1,9 +1,17 @@
 from functools import partial
 
+import functools
 import jax
 import jax.numpy as jnp
 from jax import lax
+from jax.experimental import pallas as pl
+from jax.experimental.pallas import tpu as pltpu
 from jax.sharding import PartitionSpec as P
+
+F32 = jnp.float32
+BF = jnp.bfloat16
+N = 4096
+NEG = -1e9
 
 D = 768
 HEADS = 12
@@ -17,7 +25,6 @@
 
 
 norm_eps = 1e-06
-mask_fill = -1000000000.0
 
 
 def product(left, right):
@@ -156,186 +163,146 @@
     return shaped.reshape(pair_count * WINS, WTOK * channels)
 
 
-def offset_table():
-    offsets = (
-        jnp.arange(GRID, dtype=jnp.int32)[:, None]
-        - jnp.arange(GRID, dtype=jnp.int32)[None, :]
-        + GRID
-        - 1
-    )
-    return offsets.reshape(-1)[:, None] == jnp.arange(2 * GRID - 1, dtype=jnp.int32)[None, :]
-
-
-def key_bias(pair_image, image_extent):
-    image_count = image_extent.shape[0]
-    chosen = pair_image[:, None] == jnp.arange(image_count, dtype=jnp.int32)[None, :]
-    extent_rows = jnp.sum(jnp.where(chosen, image_extent[None, :, 0], 0), axis=1)
-    extent_cols = jnp.sum(jnp.where(chosen, image_extent[None, :, 1], 0), axis=1)
-    grid_ids = jnp.arange(GRID, dtype=jnp.int32)[None, :]
-    row_bias_terms = jnp.where(grid_ids < extent_rows[:, None], 0.0, mask_fill).astype(jnp.float32)
-    column_bias_terms = jnp.where(grid_ids < extent_cols[:, None], 0.0, mask_fill).astype(
-        jnp.float32
-    )
-    return (row_bias_terms, column_bias_terms)
-
-
-def rel_terms(
-    queries, row_position_table, column_position_table, row_bias_terms, column_bias_terms
-):
-    pair_count = queries.shape[0]
-    grid_queries = queries.reshape(pair_count, GRID, GRID, HDIM)
-    row_partial = jnp.einsum(
-        "jrcd,rkd->jrck", grid_queries, row_position_table, preferred_element_type=jnp.float32
-    )
-    column_partial = jnp.einsum(
-        "jrcd,ckd->jrck", grid_queries, column_position_table, preferred_element_type=jnp.float32
-    )
-    row_partial = row_partial + row_bias_terms[:, None, None, :]
-    column_partial = column_partial + column_bias_terms[:, None, None, :]
-    return (
-        row_partial.reshape(pair_count, GRID * GRID, GRID),
-        column_partial.reshape(pair_count, GRID * GRID, GRID),
-    )
-
-
-def block_scores(query_tile_rows, key_rows, row_block_terms, column_block_terms, score_scale):
-    pair_count, block_rows = (query_tile_rows.shape[0], query_tile_rows.shape[1])
-    raw_scores = (
-        jnp.einsum("jbd,jnd->jbn", query_tile_rows, key_rows, preferred_element_type=jnp.float32)
-        * score_scale
-    )
-    raw_scores = raw_scores.reshape(pair_count, block_rows, GRID, GRID)
-    raw_scores = raw_scores + row_block_terms[:, :, :, None] + column_block_terms[:, :, None, :]
-    return raw_scores.reshape(pair_count, block_rows, GRID * GRID)
-
-
-def attention_forward(queries, key_rows, values, rel_rows_part, rel_cols_part):
-    pair_count, patch_count = (queries.shape[0], queries.shape[1])
-    block_rows = min(512, patch_count)
-    score_scale = HDIM ** (-0.5)
-
-    def one_block(block_id, carry):
-        out_buffer, total_buffer = carry
-        first_row = block_id * block_rows
-        query_tile_rows = lax.dynamic_slice_in_dim(queries, first_row, block_rows, 1)
-        row_block_terms = lax.dynamic_slice_in_dim(rel_rows_part, first_row, block_rows, 1)
-        column_block_terms = lax.dynamic_slice_in_dim(rel_cols_part, first_row, block_rows, 1)
-        scores = block_scores(
-            query_tile_rows, key_rows, row_block_terms, column_block_terms, score_scale
-        )
-        highest = jnp.max(scores, axis=-1, keepdims=True)
-        totals = highest + jnp.log(jnp.sum(jnp.exp(scores - highest), axis=-1, keepdims=True))
-        weights_low = jnp.exp(scores - totals).astype(jnp.bfloat16)
-        outputs = jnp.einsum(
-            "jbn,jnd->jbd", weights_low, values, preferred_element_type=jnp.float32
-        )
-        out_buffer = lax.dynamic_update_slice_in_dim(
-            out_buffer, outputs.astype(jnp.bfloat16), first_row, 1
-        )
-        total_buffer = lax.dynamic_update_slice_in_dim(total_buffer, totals[:, :, 0], first_row, 1)
-        return (out_buffer, total_buffer)
-
-    initial = (
-        jnp.zeros((pair_count, patch_count, HDIM), jnp.bfloat16),
-        jnp.zeros((pair_count, patch_count), jnp.float32),
-    )
-    return lax.fori_loop(0, patch_count // block_rows, one_block, initial)
-
-
-def attention_backward(queries, key_rows, values, rel_rows_part, rel_cols_part, totals, grad_pairs):
-    pair_count, patch_count = (queries.shape[0], queries.shape[1])
-    block_rows = min(512, patch_count)
-    score_scale = HDIM ** (-0.5)
-
-    def one_block(block_id, running):
-        grad_keys, grad_values, query_buffer, rows_buffer, cols_buffer = running
-        first_row = block_id * block_rows
-        query_tile_rows = lax.dynamic_slice_in_dim(queries, first_row, block_rows, 1)
-        row_block_terms = lax.dynamic_slice_in_dim(rel_rows_part, first_row, block_rows, 1)
-        column_block_terms = lax.dynamic_slice_in_dim(rel_cols_part, first_row, block_rows, 1)
-        total_block = lax.dynamic_slice_in_dim(totals, first_row, block_rows, 1)
-        grad_block = lax.dynamic_slice_in_dim(grad_pairs, first_row, block_rows, 1)
-        scores = block_scores(
-            query_tile_rows, key_rows, row_block_terms, column_block_terms, score_scale
-        )
-        weights = jnp.exp(scores - total_block[:, :, None])
-        grad_weights = jnp.einsum(
-            "jbd,jnd->jbn", grad_block, values, preferred_element_type=jnp.float32
-        )
-        inner = jnp.sum(weights * grad_weights, axis=-1, keepdims=True)
-        grad_scores = (weights * (grad_weights - inner)).astype(jnp.bfloat16)
-        grad_keys = grad_keys + score_scale * jnp.einsum(
-            "jbn,jbd->jnd", grad_scores, query_tile_rows, preferred_element_type=jnp.float32
-        )
-        grad_values = grad_values + jnp.einsum(
-            "jbn,jbd->jnd",
-            weights.astype(jnp.bfloat16),
-            grad_block,
-            preferred_element_type=jnp.float32,
-        )
-        grad_query = score_scale * jnp.einsum(
-            "jbn,jnd->jbd", grad_scores, key_rows, preferred_element_type=jnp.float32
-        )
-        folded = grad_scores.astype(jnp.float32).reshape(pair_count, block_rows, GRID, GRID)
-        query_buffer = lax.dynamic_update_slice_in_dim(query_buffer, grad_query, first_row, 1)
-        rows_buffer = lax.dynamic_update_slice_in_dim(
-            rows_buffer, jnp.sum(folded, axis=3), first_row, 1
-        )
-        cols_buffer = lax.dynamic_update_slice_in_dim(
-            cols_buffer, jnp.sum(folded, axis=2), first_row, 1
-        )
-        return (grad_keys, grad_values, query_buffer, rows_buffer, cols_buffer)
-
-    initial = (
-        jnp.zeros((pair_count, patch_count, HDIM), jnp.float32),
-        jnp.zeros((pair_count, patch_count, HDIM), jnp.float32),
-        jnp.zeros((pair_count, patch_count, HDIM), jnp.float32),
-        jnp.zeros((pair_count, patch_count, GRID), jnp.float32),
-        jnp.zeros((pair_count, patch_count, GRID), jnp.float32),
-    )
-    grad_keys, grad_values, grad_query, grad_rows, grad_cols = lax.fori_loop(
-        0, patch_count // block_rows, one_block, initial
-    )
-    return (grad_query, grad_keys, grad_values, grad_rows, grad_cols)
-
-
-def rel_back(queries, row_position_table, column_position_table, grad_rows, grad_cols, picks):
-    pair_count = queries.shape[0]
-    exact_result = lax.Precision.HIGHEST
-    grid_queries = queries.astype(jnp.float32).reshape(pair_count, GRID, GRID, HDIM)
-    rows_four = grad_rows.reshape(pair_count, GRID, GRID, GRID)
-    cols_four = grad_cols.reshape(pair_count, GRID, GRID, GRID)
-    rel_query = jnp.einsum(
-        "jrck,rkd->jrcd", rows_four, row_position_table.astype(jnp.float32), precision=exact_result
-    )
-    rel_query = rel_query + jnp.einsum(
-        "jrck,ckd->jrcd",
-        cols_four,
-        column_position_table.astype(jnp.float32),
-        precision=exact_result,
-    )
-    table_rows = jnp.einsum(
-        "jrck,jrcd->rkd", rows_four, grid_queries, precision=exact_result
-    ).reshape(GRID * GRID, HDIM)
-    table_cols = jnp.einsum(
-        "jrck,jrcd->ckd", cols_four, grid_queries, precision=exact_result
-    ).reshape(GRID * GRID, HDIM)
-    pick_values = picks.astype(jnp.float32)
-    rows_grad = lax.dot_general(
-        pick_values,
-        table_rows,
-        (((0,), (0,)), ((), ())),
-        precision=exact_result,
-        preferred_element_type=jnp.float32,
-    )
-    cols_grad = lax.dot_general(
-        pick_values,
-        table_cols,
-        (((0,), (0,)), ((), ())),
-        precision=exact_result,
-        preferred_element_type=jnp.float32,
-    )
-    return (rel_query.reshape(pair_count, GRID * GRID, HDIM), rows_grad, cols_grad)
+def dot(a,b): return jnp.dot(a,b,preferred_element_type=F32)
+def dotT(a,b): return lax.dot_general(a,b,(((1,),(1,)),((),())),preferred_element_type=F32)
+
+def split(x):
+    hi=x.astype(BF); lo=(x-hi.astype(F32)).astype(BF)
+    return hi,lo
+
+def onehots():
+    f=lax.broadcasted_iota(jnp.int32,(192,2048),0)
+    j=lax.broadcasted_iota(jnp.int32,(192,2048),1)
+    col=(f%64)==(j%64)
+    row=((f-128)%32)==(j//64)
+    return jnp.where(f<128, col.astype(F32), row.astype(F32)).astype(BF)
+
+def rel_feats(q, rel, ext_r, ext_c, row0, groups, sub=None):
+    fr=dotT(q, rel[...])
+    outs_r=[];outs_c=[]
+    lane=lax.broadcasted_iota(jnp.int32,(64,128),1)
+    mr=jnp.where(lane<ext_r,0.0,NEG); mc=jnp.where(lane<ext_c,0.0,NEG)
+    for g in range(groups):
+        r=row0+g
+        a=pltpu.roll(fr[g*64:(g+1)*64,:128], (r+65)%128, 1)+mr
+        c=pltpu.roll(fr[g*64:(g+1)*64,128:], 65, 1, stride=1, stride_axis=0)+mc
+        outs_r.append(a); outs_c.append(c)
+    R=jnp.concatenate(outs_r,0); C=jnp.concatenate(outs_c,0)
+    return R,C
+
+def make_lhs(q,R,C):
+    rh,rl=split(R[:,:64]); ch,cl=split(C[:,:64])
+    qs=(q.astype(F32)*0.125).astype(BF)
+    A=jnp.concatenate([qs,ch,cl,rh[:,:32],rl[:,:32]],1)
+    B=jnp.concatenate([qs,ch,cl,rh[:,32:],rl[:,32:]],1)
+    return A,B
+
+def fwd_kernel(ext_ref,q_ref,k_ref,v_ref,rel_ref,o_ref,oa_ref,kt,va,*,TQ):
+    p=pl.program_id(0); t=pl.program_id(1)
+    @pl.when((p==0)&(t==0))
+    def _():
+        oh=onehots()
+        kt[64:,:2048]=oh; kt[64:,2048:]=oh
+        va[:,64:]=jnp.where(lax.broadcasted_iota(jnp.int32,(N,64),1)==0,1.0,0.0).astype(BF)
+    @pl.when(t==0)
+    def _():
+        kt[:64,:]=k_ref[0].astype(F32).T.astype(BF)
+        va[:,:64]=v_ref[0]
+    q=q_ref[0]
+    R,C=rel_feats(q,rel_ref,ext_ref[p,0],ext_ref[p,1],t*(TQ//64),TQ//64)
+    A,B=make_lhs(q,R,C)
+    SA=dot(A,kt[:,:2048]); SB=dot(B,kt[:,2048:])
+    m=jnp.maximum(jnp.max(SA,1,keepdims=True),jnp.max(SB,1,keepdims=True))
+    PA=jnp.exp(SA-m).astype(BF); PB=jnp.exp(SB-m).astype(BF)
+    acc=dot(PA,va[:2048,:])+dot(PB,va[2048:,:])
+    l=acc[:,64:65]
+    o=acc*(1.0/l)
+    L=m+jnp.log(l)
+    lane=lax.broadcasted_iota(jnp.int32,(TQ,128),1)
+    oa_ref[0]=jnp.where(lane<64,o,L)
+    o_ref[0]=o[:,:64].astype(BF)
+
+def attn_fwd(ext, q, k, v, rel, TQ=256):
+    Pn=q.shape[0]
+    return pl.pallas_call(functools.partial(fwd_kernel,TQ=TQ),
+      out_shape=(jax.ShapeDtypeStruct((Pn,N,64),BF),jax.ShapeDtypeStruct((Pn,N,128),F32)),
+      grid_spec=pltpu.PrefetchScalarGridSpec(num_scalar_prefetch=1,grid=(Pn,N//TQ),
+        in_specs=[pl.BlockSpec((1,TQ,64),lambda p,t,*_:(p,t,0)),
+                  pl.BlockSpec((1,N,64),lambda p,t,*_:(p,0,0)),
+                  pl.BlockSpec((1,N,64),lambda p,t,*_:(p,0,0)),
+                  pl.BlockSpec((256,64),lambda p,t,*_:(0,0))],
+        out_specs=[pl.BlockSpec((1,TQ,64),lambda p,t,*_:(p,t,0)),pl.BlockSpec((1,TQ,128),lambda p,t,*_:(p,t,0))],
+        scratch_shapes=[pltpu.VMEM((256,N),BF),pltpu.VMEM((N,128),BF)]),
+      compiler_params=pltpu.CompilerParams(dimension_semantics=("arbitrary","arbitrary"),vmem_limit_bytes=56<<20))(ext,q,k,v,rel)
+
+def bwd_kernel(ext_ref,q_ref,k_ref,v_ref,oa_ref,do_ref,rel_ref,relb_ref,dq_ref,dkt_ref,dvt_ref,drel_ref,kt,vt,ka,*,TQ):
+    p=pl.program_id(0); t=pl.program_id(1)
+    H=2048
+    @pl.when((p==0)&(t==0))
+    def _():
+        oh=onehots()
+        kt[64:,:H]=oh; kt[64:,H:]=oh
+        vt[64:,:]=jnp.where(lax.broadcasted_iota(jnp.int32,(64,N),0)<2,-1.0,0.0).astype(BF)
+        j=lax.broadcasted_iota(jnp.int32,(N,128),0); f=lax.broadcasted_iota(jnp.int32,(N,128),1)
+        ka[:,64:192]=jnp.where(f<64,((63-f)==j%64).astype(F32),((f-64)==j//64).astype(F32)).astype(BF)
+        ka[:,192:]=jnp.zeros((N,64),BF)
+        drel_ref[...]=jnp.zeros_like(drel_ref)
+    @pl.when(t==0)
+    def _():
+        kf=k_ref[0]
+        kt[:64,:]=kf.astype(F32).T.astype(BF)
+        ka[:,:64]=(kf.astype(F32)*0.125).astype(BF)
+        vt[:64,:]=v_ref[0].astype(F32).T.astype(BF)
+        dkt_ref[...]=jnp.zeros_like(dkt_ref); dvt_ref[...]=jnp.zeros_like(dvt_ref)
+    q=q_ref[0]; do=do_ref[0]; oa=oa_ref[0]
+    L=oa[:,64:65]
+    D=jnp.sum(do.astype(F32)*oa[:,:64],1,keepdims=True)
+    g=TQ//64; row0=t*g
+    R,C=rel_feats(q,rel_ref,ext_ref[p,0],ext_ref[p,1],row0,g)
+    A,B=make_lhs(q,R-L,C)
+    dh,dl=split(D)
+    lane=lax.broadcasted_iota(jnp.int32,(TQ,64),1)
+    dd=jnp.where(lane==0,dh.astype(F32),jnp.where(lane==1,dl.astype(F32),0.0)).astype(BF)
+    doa=jnp.concatenate([do,dd],1)
+    qt=(q.astype(F32)*0.125).T.astype(BF)
+    dot_=do.astype(F32).T.astype(BF)
+    dqa=None
+    for h,lhs in ((0,A),(1,B)):
+        sl=slice(h*H,(h+1)*H)
+        P=jnp.exp(dot(lhs,kt[:,sl]))
+        dS=(P*dot(doa,vt[:,sl])).astype(BF)
+        dvt_ref[0,:,sl]+=dot(dot_,P.astype(BF))
+        dkt_ref[0,:,sl]+=dot(qt,dS)
+        x=dot(dS,ka[sl,:])
+        dqa=x if dqa is None else dqa+x
+    z64=jnp.zeros((64,64),F32)
+    outs=[]
+    for i in range(g):
+        rs=slice(i*64,(i+1)*64)
+        dC=jnp.concatenate([dqa[rs,64:128],z64],1)
+        dR=jnp.concatenate([dqa[rs,128:192],z64],1)
+        fR=pltpu.roll(dR,(63-(row0+i))%128,1)
+        fC=pltpu.roll(dC,0,1,stride=1,stride_axis=0)
+        outs.append(jnp.concatenate([fR,fC],1))
+    f=jnp.concatenate(outs,0)
+    fh,fl=split(f)
+    relv=relb_ref[...]
+    dq=dqa[:,:64]+dot(fh,relv)+dot(fl,relv)
+    dq_ref[0]=dq.astype(BF)
+    q8=q.astype(F32).T.astype(BF)
+    drel_ref[...]+=dot(q8,fh)+dot(q8,fl)
+
+def attn_bwd(ext, q, k, v, oa, do, rel, TQ=256):
+    Pn=q.shape[0]
+    full=lambda w:pl.BlockSpec((1,N,w),lambda p,t,*_:(p,0,0))
+    tile=lambda w:pl.BlockSpec((1,TQ,w),lambda p,t,*_:(p,t,0))
+    return pl.pallas_call(functools.partial(bwd_kernel,TQ=TQ),
+      out_shape=(jax.ShapeDtypeStruct((Pn,N,64),BF),jax.ShapeDtypeStruct((Pn,64,N),F32),jax.ShapeDtypeStruct((Pn,64,N),F32),jax.ShapeDtypeStruct((64,256),F32)),
+      grid_spec=pltpu.PrefetchScalarGridSpec(num_scalar_prefetch=1,grid=(Pn,N//TQ),
+        in_specs=[tile(64),full(64),full(64),tile(128),tile(64),pl.BlockSpec((256,64),lambda p,t,*_:(0,0)),pl.BlockSpec((256,64),lambda p,t,*_:(0,0))],
+        out_specs=[tile(64),pl.BlockSpec((1,64,N),lambda p,t,*_:(p,0,0)),pl.BlockSpec((1,64,N),lambda p,t,*_:(p,0,0)),pl.BlockSpec((64,256),lambda p,t,*_:(0,0))],
+        scratch_shapes=[pltpu.VMEM((256,N),BF),pltpu.VMEM((128,N),BF),pltpu.VMEM((N,256),BF)]),
+      compiler_params=pltpu.CompilerParams(dimension_semantics=("arbitrary","arbitrary"),vmem_limit_bytes=56<<20))(ext,q,k,v,oa,do,rel,jnp.concatenate([rel[:128],rel[128:255][::-1],rel[255:]],0))
 
 
 def shards(
@@ -388,20 +355,10 @@
     arrived_qkv = lax.all_to_all(qkv_packed, "wide", split_axis=0, concat_axis=0, tiled=True)
     pair_grid = grid_from_items(arrived_qkv.reshape(length, -1)[gather_index], PAIR_DEV, 3)
     queries, key_rows, values = (pair_grid[:, :, 0], pair_grid[:, :, 1], pair_grid[:, :, 2])
-    picks = offset_table()
-    row_position_table = (
-        product(picks.astype(jnp.bfloat16), rel_rows).astype(jnp.bfloat16).reshape(GRID, GRID, HDIM)
-    )
-    column_position_table = (
-        product(picks.astype(jnp.bfloat16), rel_cols).astype(jnp.bfloat16).reshape(GRID, GRID, HDIM)
-    )
-    row_bias_terms, column_bias_terms = key_bias(pair_image, image_extent)
-    rel_rows_part, rel_cols_part = rel_terms(
-        queries, row_position_table, column_position_table, row_bias_terms, column_bias_terms
-    )
-    attended_pairs, totals = attention_forward(
-        queries, key_rows, values, rel_rows_part, rel_cols_part
-    )
+    blank = jnp.zeros((1, HDIM), BF)
+    rel = jnp.concatenate([rel_rows[::-1], blank, rel_cols[::-1], blank], 0)
+    extents = image_extent[pair_image]
+    attended_pairs, saved = attn_fwd(extents, queries, key_rows, values, rel)
     out_packed = pack_items(
         items_from_grid(attended_pairs, PAIR_DEV), gather_index, length, wide_count
     )
@@ -437,22 +394,18 @@
     out_bias_grad = jnp.sum(grad_branch.astype(jnp.float32), axis=0)
     grad_attended = product_right(grad_branch, out_weight).astype(jnp.bfloat16)
     grad_packed = pack_items(to_items(grad_attended, slot_count, 1), position, length, wide_count)
-    resent_qkv, grad_arrived = (
-        lax.all_to_all(qkv_packed, "wide", split_axis=0, concat_axis=0, tiled=True),
-        lax.all_to_all(grad_packed, "wide", split_axis=0, concat_axis=0, tiled=True),
-    )
-    resent_grid = grid_from_items(resent_qkv.reshape(length, -1)[gather_index], PAIR_DEV, 3)
-    queries, key_rows, values = (resent_grid[:, :, 0], resent_grid[:, :, 1], resent_grid[:, :, 2])
+    grad_arrived = lax.all_to_all(grad_packed, "wide", split_axis=0, concat_axis=0, tiled=True)
     grad_pairs = grid_from_items(grad_arrived.reshape(length, -1)[gather_index], PAIR_DEV, 1)[
         :, :, 0
     ]
-    grad_query_part, grad_keys, grad_values, grad_rows, grad_cols = attention_backward(
-        queries, key_rows, values, rel_rows_part, rel_cols_part, totals, grad_pairs
-    )
-    rel_query, rel_rows_grad, rel_cols_grad = rel_back(
-        queries, row_position_table, column_position_table, grad_rows, grad_cols, picks
-    )
-    grad_query = (grad_query_part + rel_query).astype(jnp.bfloat16)
+    grad_query, grad_keys, grad_values, rel_grads = attn_bwd(
+        extents, queries, key_rows, values, saved, grad_pairs, rel
+    )
+    rel_grads = rel_grads.T
+    rel_rows_grad = rel_grads[:127][::-1]
+    rel_cols_grad = rel_grads[128:255]
+    grad_keys = grad_keys.transpose(0, 2, 1)
+    grad_values = grad_values.transpose(0, 2, 1)
     stacked = jnp.concatenate(
         [grad_query, grad_keys.astype(jnp.bfloat16), grad_values.astype(jnp.bfloat16)], axis=2
     )

time: 4640 us -> 2140 us (0.46)
  local copies, waits for them, and re-layouts: 1950 us -> 534 us
  matrix products: 1170 us -> 170 us
  other arithmetic: 457 us -> 42.3 us
  Pallas kernels: 0 us -> 319 us
  blocking collectives: 0 us -> 77.5 us
    add x67 -> x0, local copies, waits for them, and re-layouts: 1190 us -> none  [the longest x64 1170 us: block_scores(): raw_scores + row_block_terms[:, :, :, None]]
    dot_general x64 -> x0, matrix products: 993 us -> none  [the longest x16 483 us: block_scores(): jnp.einsum('jbd,jnd->jbn', query_tile_rows, key_rows, preferred_element_t...]
    pallas_call x0 -> x2, Pallas kernels: none -> 319 us  [the longest x1 200 us: attn_bwd(): pl.pallas_call(functools.partial(bwd_kernel, TQ=TQ), out_shape=(jax.Shape...]
    reduce_sum x25 -> x0, other arithmetic: 236 us -> none  [the longest x8 84.5 us: one_block(): jnp.sum(jnp.exp(scores - highest), axis=-1, keepdims=True)]
    reshape x17 -> x0, local copies, waits for them, and re-layouts: 187 us -> none  [the longest x8 142 us: one_block(): grad_scores.astype(jnp.float32).reshape(pair_count, block_rows, GRID, GRID)]
    convert_element_type x9 -> x0, other arithmetic: 175 us -> none  [the longest x8 172 us: one_block(): grad_scores = (weights * (grad_weights - inner)).astype(jnp.bfloat16)]
    all_to_all x0 -> x1, blocking collectives: none -> 77.5 us  [shards(): lax.all_to_all(grad_packed, 'wide', split_axis=0, concat_axis=0, tiled=True)]
    all_to_all x1 -> x0, waiting for transfers between devices: 72.9 us -> none  [shards(): lax.all_to_all(grad_packed, 'wide', split_axis=0, concat_axis=0, tiled=True)]
  transfers between devices with their start and end apart: 10 -> 9, of which waited for: 10 -> 9; matrix products, arithmetic and copies ran while one was open for 3% -> 4% of each run, Pallas kernels for 0% -> 0%
where the time goes in v1:
time: 2140 us; the launch traced here: 2120 us
  waiting for transfers between devices  945 us (44%)
  local copies, waits for them, and re-layouts  534 us (25%)
  Pallas kernels  319 us (15%)
  matrix products  170 us (8%)
  blocking collectives  77.5 us (4%)
  other arithmetic  42.3 us (2%)
    all_to_all x1, waiting for transfers between devices, shards(): lax.all_to_all(back_packed, 'wide', split_axis=0, concat_axis=0, tiled=True)  209 us
    all_to_all x1, waiting for transfers between devices, shards(): lax.all_to_all(qkv_packed, 'wide', split_axis=0, concat_axis=0, tiled=True)  207 us
    pallas_call x1, Pallas kernels, attn_bwd(): pl.pallas_call(functools.partial(bwd_kernel, TQ=TQ), out_shape=(jax.Shape...  200 us
    psum x1, waiting for transfers between devices, shards(): lax.psum((norm1_gain_grad, norm1_shift_grad, qv_bias_grad, rel_rows_grad,...  131 us
    pallas_call x1, Pallas kernels, attn_fwd(): pl.pallas_call(functools.partial(fwd_kernel, TQ=TQ), out_shape=(jax.Shape...  119 us
    reduce_scatter x1, waiting for transfers between devices, shards(): lax.psum_scatter(large_grads[3], 'wide', scatter_dimension=0, tiled=True)  101 us
    reduce_scatter x1, waiting for transfers between devices, shards(): lax.psum_scatter(large_grads[2], 'wide', scatter_dimension=0, tiled=True)  100 us
    all_to_all x1, blocking collectives, shards(): lax.all_to_all(grad_packed, 'wide', split_axis=0, concat_axis=0, tiled=True)  77.5 us
  transfers between devices with their start and end apart: 9, of which 9 were waited for; matrix products, arithmetic and copies ran while one was open for 4% of the time, Pallas kernels for 0%

profile of v1, /device:TPU:0, one launch (start us, length us, event | category | flops | bytes accessed | tf_op | source)
XLA Modules:
  0.0 2122.0 jit_solution(4543289695078181005)
XLA Ops:
  49.6 18.1 reshape.769
  94.2 14.7 scatter_custom_fusion
  128.1 207.4 %all-to-all-done = bf16[8,11,37632]{2,1,0:T(8,128)(2,1)} async-done(((bf16[8,11,37632]{2,1,0:T(8,128)(2,1)}), bf16[8,11,37632]{2,1,0:T(8,128)(2,1)}, u32[]{:S(2)}, u32[]{:S(2)}) %all-to-all-start) | async-done | bytes 6623264 | tf_op jit(solution)/shard_map/all_to_all | solution.py:355
  344.8 15.4 gather_fusion.1
  400.4 23.3 %reshape.880 = bf16[3,4096,3,64]{3,2,1,0:T(4,128)(2,1)} reshape(bf16[3,64,64,192]{3,2,1,0:T(8,128)(2,1)} %slice.56) | data formatting | bytes 9437184 | tf_op jit(solution)/shard_map/reshape | solution.py:150
  423.6 26.9 %fusion.50 = (bf16[3,4096,1,64]{3,2,1,0:T(2,128)(2,1)S(1)}, bf16[3,4096,1,64]{3,2,1,0:T(2,128)(2,1)S(1)}, bf16[3,4096,1,64]{3,2,1,0:T(2,128)(2,1)S(1)}) fusion(bf16[3,4096,3,64]{3,2,1,0:T(4,128)(2,1)} %reshape.880), kind=kLoop, calls=%fused_computation.163 | loop fusion | bytes 9437184 | tf_op jit(solution)/shard_map/slice | solution.py:357
  456.7 119.3 %shard_map.306 = (bf16[3,4096,64]{2,1,0:T(8,128)(2,1)}, f32[3,4096,128]{2,1,0:T(8,128)}) custom-call(s32[3,2]{1,0:T(4,128)} %gather_fusion, bf16[3,4096,64]{2,1,0:T(8,128)(2,1)} %bitcast.103, bf16[3,4096,64]{2,1,0:T(8,128)(2,1)} %bitcast.101, bf16[3,4096,64]{2,1,0:T(8,128)(2,1)} %bitcast.99, bf16[256,64]{1,0:T(8,128)(2,1)} %get-tuple-element.120.rel_ref), custom_call_target="tpu_custom_call" | custom-call | tf_op jit(solution)/shard_map/pallas_call | solution.py:227
  622.2 64.9 %all-to-all-done.1 = bf16[8,11,12544]{2,1,0:T(8,128)(2,1)} async-done(((bf16[8,11,12544]{2,1,0:T(8,128)(2,1)}), bf16[8,11,12544]{2,1,0:T(8,128)(2,1)}, u32[]{:S(2)}, u32[]{:S(2)}) %all-to-all-start.1) | async-done | bytes 2207776 | tf_op jit(solution)/shard_map/all_to_all | solution.py:365
  721.7 49.1 %multiply_convert_fusion = (bf16[1372,3072]{1,0:T(8,128)(2,1)}, f32[1372,3072]{1,0:T(8,128)}, f32[1372,3072]{1,0:T(8,128)}) fusion(f32[3072]{0:T(1024)S(1)} %convert_element_type.150, bf16[768,3072]{1,0:T(8,128)(2,1)} %param.30, f32[1372,768]{1,0:T(8,128)S(1)} %get-tuple-element.125, f32[768]{0:T(1024)S(1)} %convert_element_type.148, ...), kind=kOutput, calls=%fused_computation.14 | convolution fusion | flops 6757352448 | bytes 51110624 | tf_op jit(solution)/shard_map/dot_general | solution.py:31
  770.8 23.4 %convert_reduce_fusion.1 = (f32[3072]{0:T(1024)}, bf16[1372,3072]{1,0:T(8,128)(2,1)}) fusion(f32[1372,3072]{1,0:T(8,128)} %get-tuple-element.109, bf16[3072,768]{1,0:T(8,128)(2,1)} %param.32, f32[1372,768]{1,0:T(8,128)} %reshape.801, f32[1372]{0:T(1024)S(1)} %copy-done.27, f32[1372,3072]{1,0:T(8,128)} %get-tuple-element.126, f32[3072]{0:T(1024)S(1)} %convert_element_type.150), kind=kOutput, calls=%fused_computation.12 | convolution fusion | flops 6547663872 | bytes 51111280 | tf_op jit(solution)/shard_map/dot_general | solution.py:41
  794.2 15.1 multiply_reduce_fusion.2
  845.8 77.5 %all_to_all.20 = bf16[8,11,12544]{2,1,0:T(8,128)(2,1)} all-to-all(bf16[8,11,12544]{2,1,0:T(8,128)(2,1)} %reshape.785), channel_id=1, replica_groups=mesh['dp'=4,'wide'=8] {'wide'}, dimensions={0} | all-to-all | bytes 4415488 | tf_op jit(solution)/shard_map/all_to_all | solution.py:397
  952.6 200.0 %shard_map.307 = (bf16[3,4096,64]{2,1,0:T(8,128)(2,1)}, f32[3,64,4096]{2,1,0:T(8,128)}, f32[3,64,4096]{2,1,0:T(8,128)}, f32[64,256]{1,0:T(8,128)}) custom-call(s32[3,2]{1,0:T(4,128)} %gather_fusion, bf16[3,4096,64]{2,1,0:T(8,128)(2,1)} %bitcast.104, bf16[3,4096,64]{2,1,0:T(8,128)(2,1)} %bitcast.102, bf16[3,4096,64]{2,1,0:T(8,128)(2,1)} %bitcast.100, ...), custom_call_target="tpu_custom_call" | custom-call | tf_op jit(solution)/shard_map/pallas_call | solution.py:299
  1241.0 208.7 %all-to-all-done.3 = bf16[8,11,37632]{2,1,0:T(8,128)(2,1)} async-done(((bf16[8,11,37632]{2,1,0:T(8,128)(2,1)}), bf16[8,11,37632]{2,1,0:T(8,128)(2,1)}, u32[]{:S(2)}, u32[]{:S(2)}) %all-to-all-start.3) | async-done | bytes 6623264 | tf_op jit(solution)/shard_map/all_to_all | solution.py:413
  1459.0 16.7 gather_fusion.4
  1511.4 15.4 reshape.794
  1568.9 14.3 fusion.46
  1586.0 37.6 %reduce-scatter.13.cloned.1.call-done = f32[96,2304]{1,0:T(8,128)} async-done(((f32[768,2304]{1,0:T(8,128)}), f32[96,2304]{1,0:T(8,128)}) %reduce-scatter.13.cloned.1.call-update) | async-done | bytes 884752
  1626.2 35.0 %reduce-scatter.7.cloned.1.call-done = f32[96,768]{1,0:T(8,128)} async-done(((f32[768,768]{1,0:T(8,128)}), f32[96,768]{1,0:T(8,128)}) %reduce-scatter.7.cloned.1.call-update) | async-done | bytes 294928 | tf_op jit(solution)/shard_map/reduce_scatter | solution.py:428
  1661.2 101.2 %reduce-scatter.11.cloned.1.call-done = f32[384,768]{1,0:T(8,128)} async-done(((f32[3072,768]{1,0:T(8,128)}), f32[384,768]{1,0:T(8,128)}) %reduce-scatter.11.cloned.1.call-update) | async-done | bytes 1179664 | tf_op jit(solution)/shard_map/reduce_scatter | solution.py:430
  1762.3 100.1 %reduce-scatter.9.cloned.1.call-done = f32[96,3072]{1,0:T(8,128)} async-done(((f32[768,3072]{1,0:T(8,128)}), f32[96,3072]{1,0:T(8,128)}) %reduce-scatter.9.cloned.1.call-update) | async-done | bytes 1179664 | tf_op jit(solution)/shard_map/reduce_scatter | solution.py:429
  1878.1 13.9 multiply_reduce_fusion.3
  1904.8 59.3 %all-reduce.10.cloned.1.call-done = (f32[96,2304]{0,1:T(8,128)}, f32[96,768]{1,0:T(8,128)}, f32[96,3072]{1,0:T(8,128)}, f32[384,768]{1,0:T(8,128)}) async-done(((f32[96,2304]{0,1:T(8,128)}, f32[96,768]{1,0:T(8,128)}, f32[96,3072]{1,0:T(8,128)}, f32[384,768]{1,0:T(8,128)}), (f32[96,2304]{0,1:T(8,128)}, f32[96,768]{1,0:T(8,128)}, f32[96,3072]{1,0:T(8,128)}, ...) | async-done | bytes 3538960 | tf_op jit(solution)/shard_map/psum | solution.py:432
  1966.7 130.9 %all-reduce.8.cloned.1.call-done = (f32[768]{0:T(1024)}, f32[768]{0:T(1024)}, f32[2,768]{1,0:T(2,128)}, f32[127,64]{0,1:T(8,128)}, f32[127,64]{0,1:T(8,128)}, /*...) async-done(((f32[768]{0:T(1024)}, f32[768]{0:T(1024)}, f32[2,768]{1,0:T(2,128)}, f32[127,64]{0,1:T(8,128)}, f32[127,64]{0,1:T(8,128)}, ...) | async-done | bytes 101904 | tf_op jit(solution)/shard_map/psum | solution.py:433
  (295 shorter events, 518.5 us)
Async XLA Ops:
  7.2 708.8 %copy-start = (bf16[768,768]{1,0:T(8,128)(2,1)S(1)}, bf16[768,768]{1,0:T(8,128)(2,1)}, u32[]{:S(2)}) copy-start(bf16[768,768]{1,0:T(8,128)(2,1)} %param.26) | copy-start | bytes 3538948
  8.9 690.7 %copy-start.38 = (pred[7]{0:T(512)(128)(4,1)}, pred[7]{0:T(512)(128)(4,1)S(1)}, u32[]{:S(2)}) copy-start(pred[7]{0:T(512)(128)(4,1)S(1)} %fusion.25) | copy-start | bytes 25
  9.3 607.4 %copy-start.44 = (s32[7]{0:T(128)}, s32[7]{0:T(128)S(1)}, u32[]{:S(2)}) copy-start(s32[7]{0:T(128)S(1)} %get-tuple-element.106) | copy-start | bytes 88
  12.4 81.8 %copy-start.56 = (s32[84]{0:T(128)}, s32[84]{0:T(128)S(1)}, u32[]{:S(2)}) copy-start(s32[84]{0:T(128)S(1)} %fusion.36) | copy-start | bytes 1012
  118.3 217.1 %all-to-all-start = ((bf16[8,11,37632]{2,1,0:T(8,128)(2,1)}), bf16[8,11,37632]{2,1,0:T(8,128)(2,1)}, u32[]{:S(2)}, u32[]{:S(2)}) async-start(bf16[8,11,37632]{2,1,0:T(8,128)(2,1)} %reshape.771), calls=%async_computation | async-start | bytes 19267584 | tf_op jit(solution)/shard_map/all_to_all | solution.py:355
  127.3 472.4 %copy-start.55 = (s32[75]{0:T(128)}, s32[75]{0:T(128)S(1)}, u32[]{:S(2)}) copy-start(s32[75]{0:T(128)S(1)} %fusion.34) | copy-start | bytes 904
  127.3 217.4 %copy-start.42 = (s32[1024]{0:T(1024)}, s32[1024]{0:T(1024)S(1)}, u32[]{:S(2)}) copy-start(s32[1024]{0:T(1024)S(1)} %pad_clamp_fusion.1) | copy-start | bytes 12292
  609.7 77.4 %all-to-all-start.1 = ((bf16[8,11,12544]{2,1,0:T(8,128)(2,1)}), bf16[8,11,12544]{2,1,0:T(8,128)(2,1)}, u32[]{:S(2)}, u32[]{:S(2)}) async-start(bf16[8,11,12544]{2,1,0:T(8,128)(2,1)} %reshape.779), calls=%async_computation.1 | async-start | bytes 6422528 | tf_op jit(solution)/shard_map/all_to_all | solution.py:365
  616.6 192.7 %copy-start.30 = (f32[768]{0:T(1024)}, f32[768]{0:T(1024)S(1)}, u32[]{:S(2)}) copy-start(f32[768]{0:T(1024)S(1)} %convert_element_type.147) | copy-start | bytes 9220
  616.6 105.1 %copy-start.46 = (f32[768]{0:T(1024)}, f32[768]{0:T(1024)S(1)}, u32[]{:S(2)}) copy-start(f32[768]{0:T(1024)S(1)} %convert_element_type.148) | copy-start | bytes 9220
  622.1 71.2 %copy-start.41 = (s32[1024]{0:T(1024)}, s32[1024]{0:T(1024)S(1)}, u32[]{:S(2)}) copy-start(s32[1024]{0:T(1024)S(1)} %pad_clamp_fusion) | copy-start | bytes 12292
  721.0 49.8 %copy-start.3 = (f32[1372,768]{1,0:T(8,128)}, f32[1372,768]{1,0:T(8,128)S(1)}, u32[]{:S(2)}) copy-start(f32[1372,768]{1,0:T(8,128)S(1)} %get-tuple-element.125) | copy-start | bytes 12644356
  721.0 88.3 %copy-start.18 = (f32[1372]{0:T(1024)}, f32[1372]{0:T(1024)S(1)}, u32[]{:S(2)}) copy-start(f32[1372]{0:T(1024)S(1)} %broadcast_multiply_fusion.4) | copy-start | bytes 16468
  721.7 87.6 %copy-start.28 = (f32[1372]{0:T(1024)}, f32[1372]{0:T(1024)S(1)}, u32[]{:S(2)}) copy-start(f32[1372]{0:T(1024)S(1)} %add_rsqrt_fusion) | copy-start | bytes 16468
  721.7 49.1 %copy-start.27 = (f32[1372]{0:T(1024)S(1)}, f32[1372]{0:T(1024)}, u32[]{:S(2)}) copy-start(f32[1372]{0:T(1024)} %reshape.803) | copy-start | bytes 16468
  1233.9 215.8 %all-to-all-start.3 = ((bf16[8,11,37632]{2,1,0:T(8,128)(2,1)}), bf16[8,11,37632]{2,1,0:T(8,128)(2,1)}, u32[]{:S(2)}, u32[]{:S(2)}) async-start(bf16[8,11,37632]{2,1,0:T(8,128)(2,1)} %reshape.792), calls=%async_computation.3 | async-start | bytes 19267584 | tf_op jit(solution)/shard_map/all_to_all | solution.py:413
  1239.2 384.4 %reduce-scatter.13.cloned.1.call-start = ((), (), s32[]{:S(2)}) async-start(), calls=%async_computation.11 | async-start | bytes 7962624
  1547.2 114.0 %reduce-scatter.7.cloned.1.call-start = ((), (), s32[]{:S(2)}) async-start(), calls=%async_computation.8 | async-start | bytes 2654208 | tf_op jit(solution)/shard_map/reduce_scatter | solution.py:428
  1554.4 207.9 %reduce-scatter.11.cloned.1.call-start = ((), (), s32[]{:S(2)}) async-start(), calls=%async_computation.10 | async-start | bytes 10616832 | tf_op jit(solution)/shard_map/reduce_scatter | solution.py:430
  1568.2 294.2 %reduce-scatter.9.cloned.1.call-start = ((), (), s32[]{:S(2)}) async-start(), calls=%async_computation.9 | async-start | bytes 10616832 | tf_op jit(solution)/shard_map/reduce_scatter | solution.py:429
  1583.3 380.7 %all-reduce.10.cloned.1.call-start = ((), (), s32[]{:S(2)}) async-start(), calls=%async_computation.13 | async-start | bytes 7667712 | tf_op jit(solution)/shard_map/psum | solution.py:432
  1862.4 235.1 %all-reduce.8.cloned.1.call-start = ((), (), s32[]{:S(2)}) async-start(), calls=%async_computation.12 | async-start | bytes 217088 | tf_op jit(solution)/shard_map/psum | solution.py:433
  1964.0 149.3 %copy-start.14 = (f32[384,768]{1,0:T(8,128)S(1)}, f32[384,768]{1,0:T(8,128)}, u32[]{:S(2)}) copy-start(f32[384,768]{1,0:T(8,128)} %get-tuple-element.149) | copy-start | bytes 3538948
  2097.6 16.8 copy-start.48
  (42 other events, 185.3 us)
Sparse Core Ops, SparseCore 0:
  1547.3 76.2 reduce-scatter.12
  1626.5 34.6 reduce-scatter.6
  1663.5 98.8 reduce-scatter.10
  1764.5 97.8 reduce-scatter.8
  1866.3 97.7 all-reduce.9
  1971.5 126.0 all-reduce.7

commit v2 on v1

v2 whole, which is shorter than its diff:
```python
from functools import partial

import jax
import jax.numpy as jnp
from jax import lax
from jax.experimental import pallas as pl
from jax.experimental.pallas import tpu as pltpu
from jax.sharding import PartitionSpec as P

F32 = jnp.float32
BF = jnp.bfloat16
D = 768
HEADS = 12
HDIM = 64
GRID = 64
N = GRID * GRID
WIN = 14
WGRID = 5
WINS = 25
WTOK = 196
HALF = 98
GROUPS = 4
CHUNKS = 3
EPS = 1e-06
NEG = -1e9
VMEM = 60 << 20


def dot(a, b):
    return jnp.dot(a, b, preferred_element_type=F32)


def dot_t(a, b):
    return lax.dot_general(a, b, (((1,), (1,)), ((), ())), preferred_element_type=F32)


def t_dot(a, b):
    return lax.dot_general(a, b, (((0,), (0,)), ((), ())), preferred_element_type=F32)


def shape(dims, kind):
    return jax.ShapeDtypeStruct(dims, kind)


def params(*semantics):
    return pltpu.CompilerParams(
        dimension_semantics=semantics or ("arbitrary",), vmem_limit_bytes=VMEM
    )


class Plan:
    def __init__(self, wide, images):
        self.wide, self.images = wide, images
        self.corner = WINS % wide == 1 and wide < WINS
        self.full = WINS // wide if self.corner else -(-WINS // wide)
        self.slots = self.full + int(self.corner)
        used = self.full * HALF + 32 * int(self.corner)
        self.rows = max(-(-used // 16) * 16, self.start(self.full - 1) + 112)
        self.corner_at = self.full * HALF

    def start(self, m):
        return m * HALF // 16 * 16

    def turn(self, places, slot_count, image):
        return (places[0] // slot_count + WINS * image) % self.wide

    def residue(self, places, slot_count, me, image):
        return (me + 2 * WINS * self.wide - self.turn(places, slot_count, image)) % self.wide

    def slot(self, places, slot_count, me, image, m):
        w = jnp.minimum(self.residue(places, slot_count, me, image) + self.wide * m, WINS - 1)
        return places[image * WINS + w] % slot_count


def norm_rows(values):
    centre = values - jnp.mean(values, axis=-1, keepdims=True)
    spread = lax.rsqrt(jnp.mean(centre * centre, axis=-1, keepdims=True) + EPS)
    return (centre * spread, spread)


def norm_back(weighted, scaled, spread):
    return spread * (
        weighted
        - jnp.mean(weighted, axis=-1, keepdims=True)
        - scaled * jnp.mean(weighted * scaled, axis=-1, keepdims=True)
    )


def place_rows(buffer, values, plan, m):
    if m < plan.full:
        for half in range(2):
            buffer[half, m * HALF : (m + 1) * HALF, :] = values[half * HALF : (half + 1) * HALF, :]
    else:
        for row in range(8):
            at = plan.corner_at + (row % 4) * 8
            buffer[row // 4, at : at + 8, :] = values[row * WIN : row * WIN + 8, :]


def cell_mask(plan, w, live):
    cell = lax.broadcasted_iota(jnp.int32, (WTOK, 1), 0)
    row_end = jnp.where(w // WGRID == WGRID - 1, 8, WIN)
    col_end = jnp.where(w % WGRID == WGRID - 1, 8, WIN)
    return ((cell // WIN < row_end) & (cell % WIN < col_end) & live).astype(F32)


def enter_kernel(plan, places, me, *refs):
    count = plan.slots
    tokens, grads = (refs[:count], refs[count : 2 * count])
    box, weight, bias, gain, shift = refs[2 * count : 2 * count + 5]
    x_out, g_out, n_out = refs[2 * count + 5 : 2 * count + 8]
    sends = refs[2 * count + 8 : 2 * count + 11]
    xbuf, gbuf, turned = refs[2 * count + 11 :]
    image = pl.program_id(0)
    slot_count = box.shape[0]

    @pl.when(image == 0)
    def _():
        xbuf[...] = jnp.zeros_like(xbuf)
        gbuf[...] = jnp.zeros_like(gbuf)
        turned[...] = box[...].astype(F32).T

    residue = plan.residue(places, slot_count, me[0], image)
    for m in range(count):
        place_rows(xbuf, tokens[m][0].astype(F32), plan, m)
        w = residue + plan.wide * m
        slot = plan.slot(places, slot_count, me[0], image, m)
        lane = lax.broadcasted_iota(jnp.int32, (WTOK, slot_count), 1)
        inside = jnp.sum(jnp.where(lane == slot, turned[...], 0.0), axis=1, keepdims=True)
        inside = inside * cell_mask(plan, w, w < WINS)
        place_rows(gbuf, grads[m][0].astype(F32) * inside, plan, m)
    x = xbuf[...].reshape(2 * plan.rows, D)
    x_out[0] = x.astype(BF)
    g_out[0] = gbuf[...].reshape(2 * plan.rows, D).astype(BF)
    scaled, _ = norm_rows(x)
    normed = (scaled * gain[...] + shift[...]).astype(BF)
    n_out[0] = normed
    for part in range(3):
        made = dot(normed, weight[:, part * D : (part + 1) * D]) + bias[:, part * D : (part + 1) * D]
        top, low = (made[: plan.rows].astype(BF), made[plan.rows :].astype(BF))
        for h in range(CHUNKS):
            for g in range(GROUPS):
                at = (h * GROUPS + g) * HDIM
                sends[h][g, :, part * 128 : (part + 1) * 128] = jnp.concatenate(
                    [top[:, at : at + HDIM], low[:, at : at + HDIM]], axis=1
                )


def enter(plan, places, me, tokens, out_grad, box_mask, weight, bias, gain, shift):
    slot_count = tokens.shape[0]

    def window(m):
        return pl.BlockSpec(
            (1, WTOK, D), lambda i, p, a: (plan.slot(p, slot_count, a[0], i, m), 0, 0)
        )

    windows = [window(m) for m in range(plan.slots)]
    fixed = [
        pl.BlockSpec(x.shape, lambda i, p, a: (0, 0)) for x in (box_mask, weight, bias, gain, shift)
    ]
    rows = pl.BlockSpec((1, 2 * plan.rows, D), lambda i, p, a: (i, 0, 0))
    send = pl.BlockSpec((GROUPS, plan.rows, 384), lambda i, p, a: (i, 0, 0))
    working = shape((plan.images, 2 * plan.rows, D), BF)
    return pl.pallas_call(
        partial(enter_kernel, plan),
        out_shape=[working] * 3 + [shape((plan.wide, plan.rows, 384), BF)] * CHUNKS,
        grid_spec=pltpu.PrefetchScalarGridSpec(
            num_scalar_prefetch=2,
            grid=(plan.images,),
            in_specs=windows + windows + fixed,
            out_specs=[rows] * 3 + [send] * CHUNKS,
            scratch_shapes=[
                pltpu.VMEM((2, plan.rows, D), F32),
                pltpu.VMEM((2, plan.rows, D), F32),
                pltpu.VMEM((WTOK, slot_count), F32),
            ],
        ),
        compiler_params=params(),
        cost_estimate=pl.CostEstimate(flops=6 * 10**9, bytes_accessed=20 << 20, transcendentals=0),
        name="enter",
    )(
        places,
        me,
        *([tokens] * plan.slots),
        *([out_grad] * plan.slots),
        box_mask,
        weight,
        bias,
        gain,
        shift,
    )


def leave_kernel(plan, places, me, values, out):
    slot = pl.program_id(0)
    slot_count = pl.num_programs(0)
    out[...] = jnp.zeros_like(out)
    for image in range(plan.images):
        residue = plan.residue(places, slot_count, me[0], image)
        for m in range(plan.slots):
            w = residue + plan.wide * m
            held = places[image * WINS + jnp.minimum(w, WINS - 1)]
            hit = (w < WINS) & (held == me[0] * slot_count + slot)

            @pl.when(hit)
            def _(image=image, m=m, w=w):
                if m < plan.full:
                    halves = []
                    for half in range(2):
                        at = half * plan.rows + m * HALF
                        halves.append(values[image, at : at + HALF, :].astype(F32))
                    keep = cell_mask(plan, w, w < WINS)
                    out[0, :HALF, :] = (halves[0] * keep[:HALF]).astype(out.dtype)
                    out[0, HALF:, :] = (halves[1] * keep[HALF:]).astype(out.dtype)
                else:
                    for row in range(8):
                        at = (row // 4) * plan.rows + plan.corner_at + (row % 4) * 8
                        piece = values[image, at : at + 8, :]
                        out[0, row * WIN : row * WIN + 8, :] = piece.astype(out.dtype)


def leave(plan, places, me, values, slot_count):
    return pl.pallas_call(
        partial(leave_kernel, plan),
        out_shape=shape((slot_count, WTOK, D), values.dtype),
        grid_spec=pltpu.PrefetchScalarGridSpec(
            num_scalar_prefetch=2,
            grid=(slot_count,),
            in_specs=[pl.BlockSpec(values.shape, lambda j, p, a: (0, 0, 0))],
            out_specs=pl.BlockSpec((1, WTOK, D), lambda j, p, a: (j, 0, 0)),
        ),
        compiler_params=params(),
        cost_estimate=pl.CostEstimate(flops=1 << 20, bytes_accessed=12 << 20, transcendentals=0),
        name="leave",
    )(places, me, values)


def spread_matrix(plan, band, flip):
    dims = (560, 448) if flip else (448, 560)
    cell = lax.broadcasted_iota(jnp.int32, dims, 1 if flip else 0)
    item = lax.broadcasted_iota(jnp.int32, dims, 0 if flip else 1)
    row, col = (cell // GRID, cell % GRID)
    block = col // WIN
    shift = jnp.zeros(dims, jnp.int32)
    for c in range(WGRID):
        m = (band * WGRID + c) // plan.wide
        if m < plan.full:
            shift = jnp.where(block == c, m * HALF - plan.start(m), shift)
        else:
            shift = jnp.where(block == c, -10000, shift)
    return (item == block * 112 + shift + row * WIN + col % WIN).astype(F32).astype(BF)


def corner_matrix(plan, flip):
    dims = (48, 256) if flip else (256, 48)
    cell = lax.broadcasted_iota(jnp.int32, dims, 1 if flip else 0)
    item = lax.broadcasted_iota(jnp.int32, dims, 0 if flip else 1)
    row, col = (cell // GRID, cell % GRID)
    at = plan.corner_at - plan.start(plan.full)
    hit = (col >= 4 * WIN) & (item == at + row * 8 + col - 4 * WIN)
    return hit.astype(F32).astype(BF)


def gather_grid(plan, turn, arrived, band):
    pieces = []
    for c in range(WGRID):
        w = band * WGRID + c
        m = w // plan.wide
        if m < plan.full:
            source = (w % plan.wide + turn) % plan.wide
            at = plan.start(m)
        else:
            source, at = (0, 0)
        pieces.append(arrived[source, at : at + 112, :])
    found = dot(spread_matrix(plan, band, False), jnp.concatenate(pieces, axis=0))
    return found


def grid_rows(plan, turn, arrived, parts, store):
    for band in range(WGRID):
        found = gather_grid(plan, turn, arrived, band)
        last = band == WGRID - 1
        if last and plan.corner:
            source = ((WINS - 1) % plan.wide + turn) % plan.wide
            at = plan.start(plan.full)
            extra = dot(corner_matrix(plan, False), arrived[source, at : at + 48, :])
        for part in range(parts):
            top = found[:, part * 128 : part * 128 + HDIM]
            low = found[:, part * 128 + HDIM : (part + 1) * 128]
            if last:
                low = low[:GRID]
            whole = jnp.concatenate([top, low], axis=0)
            if last and plan.corner:
                more = jnp.concatenate(
                    [
                        extra[:, part * 128 : part * 128 + HDIM],
                        extra[:, part * 128 + HDIM : (part + 1) * 128],
                    ],
                    axis=0,
                )
                whole = whole + more
            store(part, band * WIN * GRID, whole)


def scatter_grid(plan, turn, out, parts, load, lane=0):
    span = slice(lane, lane + parts * 128)
    out[:, :, span] = jnp.zeros((plan.wide, plan.rows, parts * 128), BF)
    for band in range(WGRID):
        last = band == WGRID - 1
        base = band * WIN * GRID
        lanes = []
        for part in range(parts):
            top = load(part, base, 448)
            if last:
                low = load(part, base + 448, GRID)
                low = jnp.concatenate([low, jnp.zeros((448 - GRID, HDIM), BF)], axis=0)
            else:
                low = load(part, base + 448, 448)
            lanes += [top, low]
        made = dot(spread_matrix(plan, band, True), jnp.concatenate(lanes, axis=1)).astype(BF)
        for c in range(WGRID):
            w = band * WGRID + c
            m = w // plan.wide
            if m < plan.full:
                dest = (w % plan.wide + turn) % plan.wide
                at = plan.start(m)
                out[dest, at : at + 112, span] += made[c * 112 : (c + 1) * 112]
        if last and plan.corner:
            lanes = []
            for part in range(parts):
                lanes += [load(part, base, 256), load(part, base + 256, 256)]
            made = dot(corner_matrix(plan, True), jnp.concatenate(lanes, axis=1)).astype(BF)
            dest = ((WINS - 1) % plan.wide + turn) % plan.wide
            at = plan.start(plan.full)
            out[dest, at : at + 48, span] += made


def split(x):
    high = x.astype(BF)
    return (high, (x - high.astype(F32)).astype(BF))


def key_marks():
    feature = lax.broadcasted_iota(jnp.int32, (192, N // 2), 0)
    key = lax.broadcasted_iota(jnp.int32, (192, N // 2), 1)
    col = (feature % GRID) == (key % GRID)
    row = ((feature - 128) % 32) == (key // GRID)
    return jnp.where(feature < 128, col.astype(F32), row.astype(F32)).astype(BF)


def rel_terms(q, table, extent_rows, extent_cols, first_row, count):
    both = dot_t(q, table)
    lane = lax.broadcasted_iota(jnp.int32, (GRID, 128), 1)
    row_mask = jnp.where(lane < extent_rows, 0.0, NEG)
    col_mask = jnp.where(lane < extent_cols, 0.0, NEG)
    rows, cols = ([], [])
    for i in range(count):
        part = both[i * GRID : (i + 1) * GRID]
        rows.append(pltpu.roll(part[:, :128], (first_row + i + 65) % 128, 1) + row_mask)
        cols.append(pltpu.roll(part[:, 128:], 65, 1, stride=1, stride_axis=0) + col_mask)
    return (jnp.concatenate(rows, 0)[:, :GRID], jnp.concatenate(cols, 0)[:, :GRID])


def query_marks(q, rows, cols):
    rh, rl = split(rows)
    ch, cl = split(cols)
    scaled = (q.astype(F32) * 0.125).astype(BF)
    return [
        jnp.concatenate([scaled, ch, cl, rh[:, i : i + 32], rl[:, i : i + 32]], 1) for i in (0, 32)
    ]


def forward_kernel(plan, tile, slot_count, places, me, extent, arrived, table, *refs):
    earlier, (send, kept, saved, kt, va, held) = (refs[:-6], refs[-6:])
    step = pl.program_id(0)
    image = me[0] // GROUPS
    turn = plan.turn(places, slot_count, image)

    @pl.when(step == 0)
    def _():
        marks = key_marks()
        kt[HDIM:, : N // 2] = marks
        kt[HDIM:, N // 2 :] = marks
        va[:, HDIM:] = (lax.broadcasted_iota(jnp.int32, (N, HDIM), 1) == 0).astype(F32).astype(BF)

        def store(part, first, values):
            kept[part, first : first + values.shape[0], :] = values.astype(BF)

        grid_rows(plan, turn, arrived, 3, store)
        kt[:HDIM, :] = kept[1].astype(F32).T.astype(BF)
        va[:, :HDIM] = kept[2]

    here = pl.ds(pl.multiple_of(step * tile, tile), tile)
    q = kept[0, here, :]
    count = tile // GRID
    rows, cols = rel_terms(q, table[...], extent[image, 0], extent[image, 1], step * count, count)
    marks = query_marks(q, rows, cols)
    scores = [dot(marks[i], kt[:, i * (N // 2) : (i + 1) * (N // 2)]) for i in range(2)]
    top = jnp.maximum(*[jnp.max(s, axis=1, keepdims=True) for s in scores])
    total = None
    for i in range(2):
        weights = jnp.exp(scores[i] - top).astype(BF)
        x = dot(weights, va[i * (N // 2) : (i + 1) * (N // 2), :])
        total = x if total is None else total + x
    mass = total[:, HDIM : HDIM + 1]
    out = total * (1.0 / mass)
    lane = lax.broadcasted_iota(jnp.int32, (tile, 128), 1)
    saved[...] = jnp.where(lane < HDIM, out, top + jnp.log(mass))
    held[here, :] = out[:, :HDIM].astype(BF)

    @pl.when(step == pl.num_programs(0) - 1)
    def _():
        load = lambda part, first, size: held[first : first + size, :]
        scatter_grid(plan, turn, send, 1, load, 128 * len(earlier))
        for i, block in enumerate(earlier):
            send[:, :, 128 * i : 128 * (i + 1)] = block[...]


def attention_forward(plan, slot_count, places, me, extent, arrived, table, *earlier, tile=256):
    lanes = 128 * (1 + len(earlier))
    whole = lambda *dims: pl.BlockSpec(dims, lambda t, *_: (0,) * len(dims))
    return pl.pallas_call(
        partial(forward_kernel, plan, tile, slot_count),
        out_shape=(
            shape((plan.wide, plan.rows, lanes), BF),
            shape((3, N, HDIM), BF),
            shape((N, 128), F32),
        ),
        grid_spec=pltpu.PrefetchScalarGridSpec(
            num_scalar_prefetch=3,
            grid=(N // tile,),
            in_specs=[whole(*x.shape) for x in (arrived, table, *earlier)],
            out_specs=[
                whole(plan.wide, plan.rows, lanes),
                whole(3, N, HDIM),
                pl.BlockSpec((tile, 128), lambda t, *_: (t, 0)),
            ],
            scratch_shapes=[
                pltpu.VMEM((256, N), BF),
                pltpu.VMEM((N, 128), BF),
                pltpu.VMEM((N, HDIM), BF),
            ],
        ),
        compiler_params=params(),
        cost_estimate=pl.CostEstimate(
            flops=4 * N * N * 256, bytes_accessed=12 << 20, transcendentals=N * N
        ),
        name="attention_forward",
    )(places, me, extent, arrived, table, *earlier)


def backward_kernel(
    plan, tile, slot_count, places, me, extent,
    arrived, kept, saved, table, table_back,
    send, rel_grad,
    kt, vt, ka, dout, dq, dk, dv,
):
    step = pl.program_id(0)
    image = me[0] // GROUPS
    turn = plan.turn(places, slot_count, image)
    side = N // 2

    @pl.when(step == 0)
    def _():
        marks = key_marks()
        kt[HDIM:, :side] = marks
        kt[HDIM:, side:] = marks
        minus = lax.broadcasted_iota(jnp.int32, (HDIM, N), 0) < 2
        vt[HDIM:, :] = jnp.where(minus, -1.0, 0.0).astype(BF)
        key = lax.broadcasted_iota(jnp.int32, (N, 128), 0)
        mark = lax.broadcasted_iota(jnp.int32, (N, 128), 1)
        col = (GRID - 1 - mark) == key % GRID
        row = (mark - GRID) == key // GRID
        ka[:, HDIM:192] = jnp.where(mark < GRID, col.astype(F32), row.astype(F32)).astype(BF)
        ka[:, 192:] = jnp.zeros((N, HDIM), BF)
        rel_grad[...] = jnp.zeros_like(rel_grad)
        dk[...] = jnp.zeros_like(dk)
        dv[...] = jnp.zeros_like(dv)
        keys = kept[1].astype(F32)
        kt[:HDIM, :] = keys.T.astype(BF)
        ka[:, :HDIM] = (keys * 0.125).astype(BF)
        vt[:HDIM, :] = kept[2].astype(F32).T.astype(BF)

        def store(part, first, values):
            dout[first : first + values.shape[0], :] = values.astype(BF)

        grid_rows(plan, turn, arrived, 1, store)

    here = pl.ds(pl.multiple_of(step * tile, tile), tile)
    q = kept[0, here, :]
    do = dout[here, :]
    old = saved[...]
    count = tile // GRID
    inner = jnp.sum(do.astype(F32) * old[:, :HDIM], axis=1, keepdims=True)
    rows, cols = rel_terms(q, table[...], extent[image, 0], extent[image, 1], step * count, count)
    marks = query_marks(q, rows - old[:, HDIM : HDIM + 1], cols)
    high, low = split(inner)
    lane = lax.broadcasted_iota(jnp.int32, (tile, HDIM), 1)
    less = jnp.where(lane == 0, high.astype(F32), jnp.where(lane == 1, low.astype(F32), 0.0))
    do_less = jnp.concatenate([do, less.astype(BF)], 1)
    q_turned = (q.astype(F32) * 0.125).T.astype(BF)
    do_turned = do.astype(F32).T.astype(BF)
    back = None
    for i in range(2):
        part = slice(i * side, (i + 1) * side)
        weights = jnp.exp(dot(marks[i], kt[:, part]))
        dscore = (weights * dot(do_less, vt[:, part])).astype(BF)
        dv[:, part] += dot(do_turned, weights.astype(BF))
        dk[:, part] += dot(q_turned, dscore)
        x = dot(dscore, ka[part, :])
        back = x if back is None else back + x
    blank = jnp.zeros((GRID, HDIM), F32)
    offsets = []
    for i in range(count):
        own = slice(i * GRID, (i + 1) * GRID)
        row_part = jnp.concatenate([back[own, 128:192], blank], 1)
        col_part = jnp.concatenate([back[own, HDIM:128], blank], 1)
        row_part = pltpu.roll(row_part, (2 * GRID - 1 + GRID - step * count - i) % 128, 1)
        col_part = pltpu.roll(col_part, 0, 1, stride=1, stride_axis=0)
        offsets.append(jnp.concatenate([row_part, col_part], 1))
    high, low = split(jnp.concatenate(offsets, 0))
    rel = table_back[...]
    both = dot(jnp.concatenate([high, low], 1), jnp.concatenate([rel, rel], 0))
    dq[here, :] = (back[:, :HDIM] + both).astype(BF)
    q_whole = q.astype(F32).T.astype(BF)
    rel_grad[...] += dot(q_whole, high) + dot(q_whole, low)

    @pl.when(step == pl.num_programs(0) - 1)
    def _():
        def load(part, first, size):
            if part == 0:
                return dq[first : first + size, :]
            return turned[part - 1][first : first + size, :]

        turned = (dk[...].T.astype(BF), dv[...].T.astype(BF))
        scatter_grid(plan, turn, send, 3, load)


def attention_backward(
    plan, slot_count, places, me, extent, arrived, lane, kept, saved, table, table_back, tile=512
):
    whole = lambda *dims: pl.BlockSpec(dims, lambda t, *_: (0,) * len(dims))
    return pl.pallas_call(
        partial(backward_kernel, plan, tile, slot_count),
        out_shape=(shape((plan.wide, plan.rows, 384), BF), shape((HDIM, 256), F32)),
        grid_spec=pltpu.PrefetchScalarGridSpec(
            num_scalar_prefetch=3,
            grid=(N // tile,),
            in_specs=[
                pl.BlockSpec((plan.wide, plan.rows, 128), lambda t, *_: (0, 0, lane)),
                whole(3, N, HDIM),
                pl.BlockSpec((tile, 128), lambda t, *_: (t, 0)),
                whole(*table.shape),
                whole(*table_back.shape),
            ],
            out_specs=[whole(plan.wide, plan.rows, 384), whole(HDIM, 256)],
            scratch_shapes=[
                pltpu.VMEM((256, N), BF),
                pltpu.VMEM((128, N), BF),
                pltpu.VMEM((N, 256), BF),
                pltpu.VMEM((N, HDIM), BF),
                pltpu.VMEM((N, HDIM), BF),
                pltpu.VMEM((HDIM, N), F32),
                pltpu.VMEM((HDIM, N), F32),
            ],
        ),
        compiler_params=params(),
        cost_estimate=pl.CostEstimate(
            flops=10 * N * N * 256, bytes_accessed=12 << 20, transcendentals=N * N
        ),
        name="attention_backward",
    )(places, me, extent, arrived, kept, saved, table, table_back)


def join_kernel(plan, first, last, x, weight, bias, attended, middle):
    returned = (first.at[:, :, :128], first.at[:, :, 128:], last)
    for half in range(2):
        lanes = [
            returned[h][g, :, half * HDIM : (half + 1) * HDIM]
            for h in range(CHUNKS)
            for g in range(GROUPS)
        ]
        attended[0, half * plan.rows : (half + 1) * plan.rows, :] = jnp.concatenate(lanes, axis=1)
    middle[0] = x[0].astype(F32) + (dot(attended[0], weight[...]) + bias[...])


def join(plan, first, last, x, weight, bias):
    rows = pl.BlockSpec((1, 2 * plan.rows, D), lambda i: (i, 0, 0))
    block = pl.BlockSpec((GROUPS, plan.rows, 128), lambda i: (i, 0, 0))
    working = (plan.images, 2 * plan.rows, D)
    return pl.pallas_call(
        partial(join_kernel, plan),
        out_shape=(shape(working, BF), shape(working, F32)),
        grid=(plan.images,),
        in_specs=[
            pl.BlockSpec((GROUPS, plan.rows, 256), lambda i: (i, 0, 0)), block, rows]
        + [pl.BlockSpec((D, D), lambda i: (0, 0)), pl.BlockSpec((1, D), lambda i: (0, 0))],
        out_specs=[rows, rows],
        compiler_params=params(),
        cost_estimate=pl.CostEstimate(flops=2 * 10**9, bytes_accessed=10 << 20, transcendentals=0),
        name="join",
    )(first, last, x, weight, bias)


def part_kernel(plan, grad, weight, first, last):
    sends = (first, last.at[:, :, :128], last.at[:, :, 128:])
    made = dot_t(grad[0], weight[...])
    top, low = (made[: plan.rows].astype(BF), made[plan.rows :].astype(BF))
    for h in range(CHUNKS):
        for g in range(GROUPS):
            at = (h * GROUPS + g) * HDIM
            made = jnp.concatenate([top[:, at : at + HDIM], low[:, at : at + HDIM]], axis=1)
            sends[h][g, :, :] = made


def part(plan, grad, weight):
    return pl.pallas_call(
        partial(part_kernel, plan),
        out_shape=[shape((plan.wide, plan.rows, lanes), BF) for lanes in (128, 256)],
        grid=(plan.images,),
        in_specs=[
            pl.BlockSpec((1, 2 * plan.rows, D), lambda i: (i, 0, 0)),
            pl.BlockSpec((D, D), lambda i: (0, 0)),
        ],
        out_specs=[
            pl.BlockSpec((GROUPS, plan.rows, lanes), lambda i: (i, 0, 0)) for lanes in (128, 256)
        ],
        compiler_params=params(),
        cost_estimate=pl.CostEstimate(flops=2 * 10**9, bytes_accessed=6 << 20, transcendentals=0),
        name="part",
    )(grad, weight)


def collect_kernel(plan, chunk, arrived, normed, wq, wk, wv, *refs):
    before, (total, weight_grad, bias_grad, held) = (refs[:-4], refs[-4:])
    image = pl.program_id(0)

    @pl.when(image == 0)
    def _():
        held[...] = jnp.zeros_like(held)
        bias_grad[...] = jnp.zeros_like(bias_grad)

    n = normed[0]
    whole = None
    for p, weight in enumerate((wq, wk, wv)):
        halves = []
        for half in range(2):
            at = p * 128 + half * HDIM
            lanes = [arrived[g, :, at : at + HDIM] for g in range(GROUPS)]
            halves.append(jnp.concatenate(lanes, axis=1))
        y = jnp.concatenate(halves, axis=0)
        x = dot_t(y, weight[...])
        whole = x if whole is None else whole + x
        span = slice(p * 256, (p + 1) * 256)
        held[:, span] += t_dot(n, y)
        bias_grad[0:1, span] += jnp.sum(y.astype(F32), axis=0, keepdims=True)
    total[0] = whole + before[0][0] if before else whole

    @pl.when(image == pl.num_programs(0) - 1)
    def _():
        weight_grad[...] = held[...].astype(weight_grad.dtype)


def collect(plan, chunk, arrived, normed, weight, before):
    rows = pl.BlockSpec((1, 2 * plan.rows, D), lambda i: (i, 0, 0))
    columns = [pl.BlockSpec((D, 256), lambda i, p=p: (0, p * 3 + chunk)) for p in range(3)]
    extra = () if before is None else (before,)
    return pl.pallas_call(
        partial(collect_kernel, plan, chunk),
        out_shape=(
            shape((plan.images, 2 * plan.rows, D), F32),
            shape((D, D), BF),
            shape((8, D), F32),
        ),
        grid=(plan.images,),
        in_specs=[pl.BlockSpec((GROUPS, plan.rows, 384), lambda i: (i, 0, 0)), rows]
        + columns
        + [rows] * len(extra),
        out_specs=[
            rows,
            pl.BlockSpec((D, D), lambda i: (0, 0)),
            pl.BlockSpec((8, D), lambda i: (0, 0)),
        ],
        scratch_shapes=[pltpu.VMEM((D, D), F32)],
        compiler_params=params(),
        cost_estimate=pl.CostEstimate(flops=8 * 10**9, bytes_accessed=20 << 20, transcendentals=0),
        name="collect",
    )(arrived, normed, weight, weight, weight, *extra)


def tie(value, *others):
    return lax.optimization_barrier((value, *others))[0]


def exchange(blocks, axis="wide"):
    return lax.all_to_all(blocks, axis, split_axis=0, concat_axis=0, tiled=True)


def share_rows(grad, wide, groups):
    piece = grad.shape[0] // wide // groups
    return grad.astype(BF).reshape(wide, groups, piece, D).transpose(1, 0, 2, 3)


def over_groups(low):
    groups = low.shape[0]
    own = lax.axis_index("dp")
    take = lambda i: lax.dynamic_index_in_dim(low, i, 0, keepdims=False)
    got = [take(own)]
    for d in range(1, groups):
        pairs = [(i, (i + d) % groups) for i in range(groups)]
        got.append(lax.ppermute(take((own + d) % groups), "dp", pairs))
    return got


def add_groups(got):
    total = got[0].astype(F32)
    for x in got[1:]:
        total = total + x.astype(F32)
    return total


def add_wide(got):
    return jnp.sum(got.astype(F32), axis=0)


def shards(
    tokens, norm1_gain, norm1_shift, qkv_weight, qv_bias, rel_rows, rel_cols, out_weight, out_bias,
    norm2_gain, norm2_shift, fc1_weight, fc1_bias, fc2_weight, fc2_bias,
    window_place, image_extent, box_mask, out_grad,
):
    wide, groups = (lax.axis_size("wide"), lax.axis_size("dp"))
    me = lax.axis_index("wide").astype(jnp.int32).reshape(1)
    plan = Plan(wide, image_extent.shape[0])
    slots = tokens.shape[0]
    wide_f = lambda v: v.astype(F32).reshape(1, -1)
    bias = jnp.concatenate([qv_bias[0], jnp.zeros((D,), BF), qv_bias[1]])
    blank = jnp.zeros((1, HDIM), BF)
    table = jnp.concatenate([rel_rows[::-1], blank, rel_cols[::-1], blank], 0)
    table_back = jnp.concatenate([rel_rows[::-1], blank, rel_cols, blank], 0)
    x, grad_out, normed1, *sends = enter(
        plan, window_place, me, tokens, out_grad, box_mask,
        qkv_weight, wide_f(bias), wide_f(norm1_gain), wide_f(norm1_shift),
    )
    forward = []
    arrived = exchange(sends[0])
    for h in range(CHUNKS):
        if h + 1 < CHUNKS:
            following, arrived = lax.optimization_barrier((sends[h + 1], arrived))
            following = exchange(tie(following, forward[h - 1][2]) if h else following)
        else:
            first, arrived = lax.optimization_barrier((forward[1][0], arrived))
            first = exchange(first)
        earlier = (forward[0][0],) if h == 1 else ()
        forward.append(
            attention_forward(
                plan, slots, window_place, me, image_extent, arrived, table, *earlier
            )
        )
        arrived = following
    last, first = lax.optimization_barrier((forward[2][0], first))
    attended, middle = join(plan, first, exchange(last), x, out_weight, wide_f(out_bias))
    rows = plan.images * 2 * plan.rows
    attended = attended.reshape(rows, D)
    middle = middle.reshape(rows, D)
    grad_low = grad_out.reshape(rows, D)
    grad_result = grad_low.astype(F32)
    scaled2, spread2 = norm_rows(middle)
    normed2 = (scaled2 * wide_f(norm2_gain) + wide_f(norm2_shift)).astype(BF)
    before = dot(normed2, fc1_weight) + wide_f(fc1_bias)
    activated, gelu_pull = jax.vjp(partial(jax.nn.gelu, approximate=False), before)
    act_low = activated.astype(BF)
    grad_before = gelu_pull(dot_t(grad_low, fc2_weight))[0].astype(BF)
    grad_normed2 = dot_t(grad_before, fc1_weight)
    grad_middle = grad_result + norm_back(grad_normed2 * wide_f(norm2_gain), scaled2, spread2)
    grad_branch = grad_middle.astype(BF)
    grad_sends = part(plan, grad_branch.reshape(plan.images, 2 * plan.rows, D), out_weight)

    grad_arrived = exchange(grad_sends[0])
    normed2, act_low, attended, _ = lax.optimization_barrier(
        (normed2, act_low, attended, grad_sends[0])
    )
    fc1_low = t_dot(normed2, grad_before).astype(BF).reshape(D, groups, D).transpose(1, 0, 2)
    shares = jnp.concatenate(
        [
            fc1_low.reshape(groups, wide, D // wide, D),
            share_rows(t_dot(act_low, grad_low), wide, groups),
            share_rows(t_dot(attended, grad_branch), wide, groups),
        ],
        axis=2,
    )
    total = lambda v: jnp.sum(v.astype(F32), axis=0)
    early = jnp.concatenate(
        [
            total(grad_branch),
            total(grad_normed2 * scaled2),
            total(grad_normed2),
            total(grad_before),
            total(grad_result),
        ]
    )
    shares, grad_arrived, early = lax.optimization_barrier((shares, grad_arrived, early))
    shares = over_groups(shares)
    following = exchange(tie(grad_sends[1], grad_arrived))

    rel_total = None
    grad_qkv = []
    for h in range(CHUNKS):
        if h == 2:
            *shares, _ = lax.optimization_barrier((*shares, send))
            shares = add_groups(shares)
            grad_arrived, shares = lax.optimization_barrier((grad_arrived, shares))
        send, rel_grad = attention_backward(
            plan, slots, window_place, me, image_extent, grad_arrived, max(h - 1, 0),
            forward[h][1], forward[h][2], table, table_back,
        )
        if h == 0:
            send, grad_arrived = lax.optimization_barrier((send, following))
        rel_total = rel_grad if h == 0 else rel_total + rel_grad
        if h > 0:
            send = tie(send, grad_qkv[-1])
        grad_qkv.append(exchange(send))
        if h + 1 < CHUNKS and h > 0:
            grad_arrived = tie(grad_arrived, grad_qkv[-2])
    shares = lax.psum_scatter(shares, "wide", scatter_dimension=0, tiled=True)[0]
    result, act_low, _ = lax.optimization_barrier((middle, act_low, send))
    shares = tie(shares, send)
    shares = lax.all_gather(shares, "dp", axis=0, tiled=False)
    result = result + dot(act_low, fc2_weight) + wide_f(fc2_bias)
    tokens_out = leave(plan, window_place, me, result.reshape(plan.images, 2 * plan.rows, D), slots)
    tokens_out = tokens_out.astype(BF)
    grad_normed1 = None
    weight_grads, bias_grads = ([], [])
    for h in range(CHUNKS):
        arrived = grad_qkv[h]
        if h == 2:
            arrived, shares, tokens_out, _ = lax.optimization_barrier(
                (arrived, shares, tokens_out, grad_normed1)
            )
        grad_normed1, weight_grad, bias_grad = collect(
            plan, h, arrived, normed1, qkv_weight, grad_normed1
        )
        weight_grads.append(
            add_groups(over_groups(share_rows(weight_grad, wide, groups))).astype(BF)
        )
        bias_grads.append(bias_grad[0].reshape(3, 256))
    weight_grads = exchange(jnp.concatenate(weight_grads, axis=2))
    bias_grad = jnp.stack(bias_grads, axis=1).reshape(3, D)
    grad_normed1 = grad_normed1.reshape(rows, D)
    scaled1, spread1 = norm_rows(x.reshape(rows, D).astype(F32))
    grad_inputs = grad_middle + norm_back(grad_normed1 * wide_f(norm1_gain), scaled1, spread1)
    sums = jnp.concatenate(
        [
            early,
            total(grad_normed1 * scaled1),
            total(grad_normed1),
            bias_grad[0],
            bias_grad[2],
            rel_total.reshape(-1),
            jnp.zeros((512,), F32),
        ]
    ).reshape(-1, D)
    sums = jnp.sum(lax.all_gather(sums, "wide", axis=0, tiled=False), axis=0)
    share = D // wide
    piece = share // groups
    last = jnp.concatenate([add_wide(weight_grads).reshape(-1, D), sums], axis=0)
    last = lax.all_gather(last, "dp", axis=0, tiled=False)
    qkv_weight_grad = last[:, : 3 * piece].reshape(share, CHUNKS, 3, 256)
    qkv_weight_grad = qkv_weight_grad.transpose(0, 2, 1, 3).reshape(share, 3 * D)
    sums = jnp.sum(last[:, 3 * piece :], axis=0).reshape(-1)
    tokens_grad = leave(
        plan, window_place, me, grad_inputs.reshape(plan.images, 2 * plan.rows, D), slots
    )
    late = sums[8 * D : 12 * D]
    rel_total = sums[12 * D : 12 * D + HDIM * 256].reshape(HDIM, 256).T
    small = sums[: 8 * D]
    return (
        tokens_out,
        tokens_grad,
        late[:D],
        late[D : 2 * D],
        qkv_weight_grad,
        late[2 * D :].reshape(2, D),
        rel_total[:127][::-1],
        rel_total[128:255],
        shares[:, 2 * share :].reshape(share, D),
        small[:D],
        small[D : 2 * D],
        small[2 * D : 3 * D],
        shares[:, :share].transpose(1, 0, 2).reshape(share, 4 * D),
        small[3 * D : 7 * D],
        shares[:, share : 2 * share].reshape(4 * share, D),
        small[7 * D :],
    )


def solution(mesh):
    tokens = P(("dp", "wide"), None, None)
    placed = (tokens,) + (P(),) * 14 + (P("dp"), P("dp", None), P(("dp", "wide"), None), tokens)
    shared = P("wide", None)
    return jax.shard_map(
        shards,
        mesh=mesh,
        in_specs=placed,
        out_specs=(
            tokens, tokens, P(), P(), shared, P(), P(), P(), shared, P(), P(), P(), shared, P(),
            shared, P(),
        ),
        check_vma=False,
    )
```

time: 2140 us -> 861 us (0.40)
  waiting for transfers between devices: 945 us -> 51.5 us
  local copies, waits for them, and re-layouts: 534 us -> 57.4 us
  Pallas kernels: 319 us -> 406 us
  matrix products: 170 us -> 123 us
  starting transfers between devices: 17.6 us -> 62.4 us
    all_to_all x3 -> x10, waiting for transfers between devices: 481 us -> 27.9 us  [exchange(): return lax.all_to_all(blocks, axis, split_axis=0, concat_axis=0, tiled=True)]
    reduce_scatter x3 -> x1, waiting for transfers between devices: 236 us -> 7.09 us  [shards(): lax.psum_scatter(shares, 'wide', scatter_dimension=0, tiled=True)[0]]
    reshape x29 -> x9, local copies, waits for them, and re-layouts: 237 us -> 19.4 us  [the longest x1 9.74 us: shards(): t_dot(normed2, grad_before).astype(BF).reshape(D, groups, D)]
    psum x2 -> x0, waiting for transfers between devices: 190 us -> none  [the longest x1 131 us: shards(): lax.psum((norm1_gain_grad, norm1_shift_grad, qv_bias_grad, rel_rows_grad,...]
    pallas_call x2 -> x14, Pallas kernels: 319 us -> 406 us  [the longest x3 202 us: attention_backward(): pl.pallas_call(partial(backward_kernel, plan, tile, slot_count), out_shap...]
    gather x7 -> x0, local copies, waits for them, and re-layouts: 58.8 us -> none  [the longest x4 39.1 us: unpack_items(): picked = flattened[jnp.minimum(position, length - 1)]]
    transpose x8 -> x2, local copies, waits for them, and re-layouts: 58.8 us -> 0.31 us  [the longest x1 0.31 us: shards(): qkv_weight_grad.transpose(0, 2, 1, 3).reshape(share, 3 * D)]
    dot_general x12 -> x7, matrix products: 170 us -> 123 us  [the longest x2 59.2 us: dot(): return jnp.dot(a, b, preferred_element_type=F32)]
  transfers between devices with their start and end apart: 9 -> 25, of which waited for: 9 -> 8; matrix products, arithmetic and copies ran while one was open for 4% -> 13% of each run, Pallas kernels for 0% -> 44%
where the time goes in v2:
time: 861 us; the launch traced here: 850 us
  Pallas kernels  406 us (47%)
  matrix products  123 us (14%)
  blocking collectives  84.1 us (10%)
  starting transfers between devices  62.4 us (7%)
  local copies, waits for them, and re-layouts  57.4 us (7%)
  waiting for transfers between devices  51.5 us (6%)
  other arithmetic  50.7 us (6%)
  between operations  14.8 us (2%)
    pallas_call x3, Pallas kernels, attention_backward(): pl.pallas_call(partial(backward_kernel, plan, tile, slot_count), out_shap...  202 us
    pallas_call x3, Pallas kernels, attention_forward(): pl.pallas_call(partial(forward_kernel, plan, tile, slot_count), out_shape...  140 us
    dot_general x2, matrix products, dot(): return jnp.dot(a, b, preferred_element_type=F32)  59.2 us
    all_to_all x1, blocking collectives, exchange(): return lax.all_to_all(blocks, axis, split_axis=0, concat_axis=0, tiled=True)  54.8 us
    all_to_all x10, starting transfers between devices, exchange(): return lax.all_to_all(blocks, axis, split_axis=0, concat_axis=0, tiled=True)  48.1 us
    dot_general x2, matrix products, dot_t(): lax.dot_general(a, b, (((1,), (1,)), ((), ())), preferred_element_type=F32)  36.4 us
    all_gather x1, blocking collectives, shards(): sums = jnp.sum(lax.all_gather(sums, 'wide', axis=0, tiled=False), axis=0)  29.3 us
    all_to_all x10, waiting for transfers between devices, exchange(): return lax.all_to_all(blocks, axis, split_axis=0, concat_axis=0, tiled=True)  27.9 us
  transfers between devices with their start and end apart: 25, of which 8 were waited for; matrix products, arithmetic and copies ran while one was open for 13% of the time, Pallas kernels for 44%

profile of v2, /device:TPU:0, one launch (start us, length us, event | category | flops | bytes accessed | tf_op | source)
XLA Modules:
  0.0 850.3 jit_solution(11700363341048858716)
XLA Ops:
  11.1 13.8 %enter.1 = (bf16[2,672,768]{2,1,0:T(8,128)(2,1)}, bf16[2,672,768]{2,1,0:T(8,128)(2,1)}, bf16[2,672,768]{2,1,0:T(8,128)(2,1)}, bf16[8,336,384]{2,1,0:T(8,128)(2,1...) custom-call(s32[50]{0:T(128)} %places.17, s32[1]{0:T(128)} %bitcast.me, bf16[7,196,768]{2,1,0:T(8,128)(2,1)} %refs_3_.1, ...), custom_call_target="tpu_custom_call" | custom-call | flops 6000000000 | bytes 20971520 | tf_op jit(solution)/shard_map/enter/pallas_call | solution.py:163
  24.9 54.8 %all_to_all.55.arrived = bf16[8,336,384]{2,1,0:T(8,128)(2,1)} all-to-all(bf16[8,336,384]{2,1,0:T(8,128)(2,1)} %get-tuple-element.85), channel_id=1, replica_groups=mesh['dp'=4,'wide'=8] {'wide'}, dimensions={0} | all-to-all | bytes 4128768 | tf_op jit(solution)/shard_map/all_to_all | solution.py:695
  84.4 46.3 %attention_forward.3 = (bf16[8,336,128]{2,1,0:T(8,128)(2,1)}, bf16[3,4096,64]{2,1,0:T(8,128)(2,1)}, f32[4096,128]{1,0:T(8,128)}) custom-call(s32[50]{0:T(128)} %places.17, s32[1]{0:T(128)} %bitcast.me, s32[2,2]{1,0:T(2,128)} %extent.11, bf16[8,336,384]{2,1,0:T(8,128)(2,1)} %all_to_all.55.arrived, bf16[256,64]{1,0:T(8,128)(2,1)} %get-tuple-element.189.table), custom_call_target="tpu_custom_call" | custom-call | flops 17179869184 | bytes 12582912 | tf_op jit(solution)/shard_map/attention_forward/pallas_call | solution.py:421
  136.2 46.9 %attention_forward.4 = (bf16[8,336,256]{2,1,0:T(8,128)(2,1)}, bf16[3,4096,64]{2,1,0:T(8,128)(2,1)}, f32[4096,128]{1,0:T(8,128)}) custom-call(s32[50]{0:T(128)} %places.17, s32[1]{0:T(128)} %bitcast.me, s32[2,2]{1,0:T(2,128)} %extent.11, bf16[8,336,384]{2,1,0:T(8,128)(2,1)} %copy-done.11, bf16[256,64]{1,0:T(8,128)(2,1)} %get-tuple-element.189.table, ...), custom_call_target="tpu_custom_call" | custom-call | flops 17179869184 | bytes 12582912 | tf_op jit(solution)/shard_map/attention_forward/pallas_call | solution.py:421
  188.2 46.4 %attention_forward.5 = (bf16[8,336,128]{2,1,0:T(8,128)(2,1)}, bf16[3,4096,64]{2,1,0:T(8,128)(2,1)}, f32[4096,128]{1,0:T(8,128)}) custom-call(s32[50]{0:T(128)} %places.17, s32[1]{0:T(128)} %bitcast.me, s32[2,2]{1,0:T(2,128)} %extent.11, bf16[8,336,384]{2,1,0:T(8,128)(2,1)} %all-to-all-done.2.arrived, bf16[256,64]{1,0:T(8,128)(2,1)} %get-tuple-element.189.table), custom_call_target="tpu_custom_call" | custom-call | flops 17179869184 | bytes 12582912 | tf_op jit(solution)/shard_map/attention_forward/pallas_call | solution.py:421
  241.6 17.3 %all-to-all-done.4.last = bf16[8,336,128]{2,1,0:T(8,128)(2,1)} async-done(((bf16[8,336,128]{2,1,0:T(8,128)(2,1)}), bf16[8,336,128]{2,1,0:T(8,128)(2,1)}, u32[]{:S(2)}, u32[]{:S(2)}) %all-to-all-start.4) | async-done | bytes 688160 | tf_op jit(solution)/shard_map/all_to_all | solution.py:695
  273.7 47.2 %multiply_convert_fusion = (bf16[1344,3072]{1,0:T(8,128)(2,1)}, f32[1344,3072]{1,0:T(8,128)}, f32[1344,3072]{1,0:T(8,128)}) fusion(f32[3072]{0:T(1024)S(1)} %convert_element_type.151, bf16[1344,768]{1,0:T(8,128)(2,1)S(1)} %add_convert_fusion.1, bf16[768,3072]{1,0:T(8,128)(2,1)} %param.30), kind=kOutput, calls=%fused_computation.4 | convolution fusion | flops 6614286336 | bytes 48082944 | tf_op jit(solution)/shard_map/dot_general | solution.py:30
  320.9 21.1 %convert_reduce_fusion = (f32[3072]{0:T(1024)S(1)}, bf16[1344,3072]{1,0:T(8,128)(2,1)}) fusion(f32[1344,3072]{1,0:T(8,128)} %get-tuple-element.170, bf16[1344,768]{1,0:T(8,128)(2,1)S(1)} %bitcast.116, bf16[3072,768]{1,0:T(8,128)(2,1)} %param.32, f32[1344,3072]{1,0:T(8,128)} %get-tuple-element.192, f32[3072]{0:T(1024)S(1)} %convert_element_type.151), kind=kOutput, calls=%fused_computation.2 | convolution fusion | flops 6411973632 | bytes 48095232 | tf_op jit(solution)/shard_map/dot_general | solution.py:34
  342.0 15.3 %multiply_reduce_fusion.3 = (f32[768]{0:T(1024)S(1)}, f32[1344]{0:T(1024)S(1)}, f32[1344]{0:T(1024)S(1)}, f32[768]{0:T(1024)S(1)}, f32[1344,768]{1,0:T(8,128)S(1)}) fusion(f32[1344]{0:T(1024)S(1)} %copy-done.22, f32[1344]{0:T(1024)S(1)} %copy-done.20, f32[2,672,768]{2,1,0:T(8,128)} %get-tuple-element.100, f32[1344,768]{1,0:T(8,128)} %bitcast.112, ...), kind=kOutput, calls=%fused_computation.35 | convolution fusion | flops 6353136640 | bytes 25393152 | tf_op jit(solution)/shard_map/dot_general | solution.py:34
  369.1 13.0 %convolution_convert_fusion = bf16[3072,768]{1,0:T(8,128)(2,1)} fusion(bf16[1344,3072]{1,0:T(8,128)(2,1)} %get-tuple-element.132, bf16[1344,768]{1,0:T(8,128)(2,1)S(1)} %bitcast.117), kind=kOutput, calls=%fused_computation.20 | convolution fusion | flops 6344146944 | bytes 15040512 | tf_op jit(solution)/shard_map/dot_general | solution.py:38
  382.1 12.6 %convolution_convert_fusion.1 = bf16[768,3072]{1,0:T(8,128)(2,1)} fusion(bf16[1344,768]{1,0:T(8,128)(2,1)S(1)} %copy-done.8, bf16[1344,3072]{1,0:T(8,128)(2,1)} %get-tuple-element.195), kind=kOutput, calls=%fused_computation.21 | convolution fusion | flops 6344146944 | bytes 15040512 | tf_op jit(solution)/shard_map/dot_general | solution.py:38
  394.8 9.7 %reshape.339 = bf16[768,4,768]{2,1,0:T(4,128)(2,1)} reshape(bf16[768,3072]{1,0:T(8,128)(2,1)} %convolution_convert_fusion.1) | data formatting | bytes 9437184 | tf_op jit(solution)/shard_map/reshape | solution.py:781
  420.3 7.5 dynamic-slice_bitcast_fusion
  432.3 67.3 %attention_backward.3 = (bf16[8,336,384]{2,1,0:T(8,128)(2,1)}, f32[64,256]{1,0:T(8,128)}) custom-call(s32[50]{0:T(128)} %places.17, s32[1]{0:T(128)} %bitcast.me, s32[2,2]{1,0:T(2,128)} %extent.11, bf16[8,336,128]{2,1,0:T(8,128)(2,1)} %copy-done.14, bf16[3,4096,64]{2,1,0:T(8,128)(2,1)} %get-tuple-element.108.kept, f32[4096,128]{1,0:T(8,128)} %get-tuple-element.92.saved, ...), custom_call_target="tpu_custom_call" | custom-call | flops 42949672960 | bytes 12582912 | tf_op jit(solution)/shard_map/attention_backward/pallas_call | solution.py:542
  504.7 67.0 %attention_backward.4 = (bf16[8,336,384]{2,1,0:T(8,128)(2,1)}, f32[64,256]{1,0:T(8,128)}) custom-call(s32[50]{0:T(128)} %places.17, s32[1]{0:T(128)} %bitcast.me, s32[2,2]{1,0:T(2,128)} %extent.11, bf16[8,336,256]{2,1,0:T(8,128)(2,1)} %all-to-all-done.6.arrived, bf16[3,4096,64]{2,1,0:T(8,128)(2,1)} %get-tuple-element.116.kept, ...), custom_call_target="tpu_custom_call" | custom-call | flops 42949672960 | bytes 12582912 | tf_op jit(solution)/shard_map/attention_backward/pallas_call | solution.py:542
  588.0 8.1 collect.3
  600.7 67.4 %attention_backward.5 = (bf16[8,336,384]{2,1,0:T(8,128)(2,1)}, f32[64,256]{1,0:T(8,128)}) custom-call(s32[50]{0:T(128)} %places.17, s32[1]{0:T(128)} %bitcast.me, s32[2,2]{1,0:T(2,128)} %extent.11, bf16[8,336,256]{2,1,0:T(8,128)(2,1)} %all-to-all-done.6.arrived, bf16[3,4096,64]{2,1,0:T(8,128)(2,1)} %get-tuple-element.125.kept, ...), custom_call_target="tpu_custom_call" | custom-call | flops 42949672960 | bytes 12582912 | tf_op jit(solution)/shard_map/attention_backward/pallas_call | solution.py:542
  681.6 7.7 all-to-all-start.9
  689.3 9.7 %collect.4 = (f32[2,672,768]{2,1,0:T(8,128)}, bf16[768,768]{1,0:T(8,128)(2,1)}, f32[8,768]{1,0:T(8,128)}) custom-call(bf16[8,336,384]{2,1,0:T(8,128)(2,1)} %copy-done.10, bf16[2,672,768]{2,1,0:T(8,128)(2,1)} %get-tuple-element.133.normed, bf16[768,2304]{1,0:T(8,128)(2,1)} %wv.5, bf16[768,2304]{1,0:T(8,128)(2,1)} %wv.5, bf16[768,2304]{1,0:T(8,128)(2,1)} %wv.5, ...), custom_call_target="tpu_custom_call" | custom-call | flops 8000000000 | bytes 20971520 | tf_op jit(solution)/shard_map/collect/pallas_call | solution.py:667
  704.6 12.1 %add_add_fusion = f32[1344,768]{1,0:T(8,128)} fusion(f32[1344,768]{1,0:T(8,128)S(1)} %bitcast.113, bf16[1344,3072]{1,0:T(8,128)(2,1)} %get-tuple-element.132, bf16[3072,768]{1,0:T(8,128)(2,1)} %param.32, f32[768]{0:T(1024)} %convert_element_type.166), kind=kOutput, calls=%fused_computation.33 | convolution fusion | flops 6343852032 | bytes 21236736 | tf_op jit(solution)/shard_map/dot_general | solution.py:30
  730.3 7.4 all-to-all-done.9.arrived
  737.7 9.0 %collect.5 = (f32[2,672,768]{2,1,0:T(8,128)}, bf16[768,768]{1,0:T(8,128)(2,1)}, f32[8,768]{1,0:T(8,128)}) custom-call(bf16[8,336,384]{2,1,0:T(8,128)(2,1)} %all-to-all-done.9.arrived, bf16[2,672,768]{2,1,0:T(8,128)(2,1)} %get-tuple-element.133.normed, bf16[768,2304]{1,0:T(8,128)(2,1)} %wv.5, bf16[768,2304]{1,0:T(8,128)(2,1)} %wv.5, bf16[768,2304]{1,0:T(8,128)(2,1)} %wv.5, ...), custom_call_target="tpu_custom_call" | custom-call | flops 8000000000 | bytes 20971520 | tf_op jit(solution)/shard_map/collect/pallas_call | solution.py:667
  775.7 29.3 %all_gather.17 = f32[8,34,768]{2,1,0:T(8,128)S(1)} all-gather(f32[1,34,768]{2,1,0:T(8,128)S(1)} %all_gather_reshape.3), channel_id=1, replica_groups=mesh['dp'=4,'wide'=8] {'wide'}, dimensions={0}, use_global_device_ids=true | all-gather | bytes 940032 | tf_op jit(solution)/shard_map/all_gather | solution.py:861
  825.0 10.8 %all-gather.8.cloned.1.call-done = f32[4,106,768]{2,1,0:T(8,128)} async-done(((f32[1,106,768]{2,1,0:T(8,128)}), f32[4,106,768]{2,1,0:T(8,128)}) %all-gather.8.cloned.1.call-update) | async-done | bytes 1302544 | tf_op jit(solution)/shard_map/all_gather | solution.py:865
  (242 shorter events, 188.0 us)
Async XLA Ops:
  79.7 51.9 %all-to-all-start.1 = ((bf16[8,336,384]{2,1,0:T(8,128)(2,1)}), bf16[8,336,384]{2,1,0:T(8,128)(2,1)S(1)}, u32[]{:S(2)}, u32[]{:S(2)}) async-start(bf16[8,336,384]{2,1,0:T(8,128)(2,1)} %get-tuple-element.86), calls=%async_computation.1 | async-start | bytes 4128768 | tf_op jit(solution)/shard_map/all_to_all | solution.py:695
  131.6 52.9 %all-to-all-start.2 = ((bf16[8,336,384]{2,1,0:T(8,128)(2,1)}), bf16[8,336,384]{2,1,0:T(8,128)(2,1)}, u32[]{:S(2)}, u32[]{:S(2)}) async-start(bf16[8,336,384]{2,1,0:T(8,128)(2,1)} %get-tuple-element.93), calls=%async_computation.2 | async-start | bytes 4128768 | tf_op jit(solution)/shard_map/all_to_all | solution.py:695
  184.5 50.0 %all-to-all-start.3 = ((bf16[8,336,256]{2,1,0:T(8,128)(2,1)}), bf16[8,336,256]{2,1,0:T(8,128)(2,1)S(1)}, u32[]{:S(2)}, u32[]{:S(2)}) async-start(bf16[8,336,256]{2,1,0:T(8,128)(2,1)} %get-tuple-element.96), calls=%async_computation.3 | async-start | bytes 2752512 | tf_op jit(solution)/shard_map/all_to_all | solution.py:695
  234.6 24.3 %all-to-all-start.4 = ((bf16[8,336,128]{2,1,0:T(8,128)(2,1)}), bf16[8,336,128]{2,1,0:T(8,128)(2,1)}, u32[]{:S(2)}, u32[]{:S(2)}) async-start(bf16[8,336,128]{2,1,0:T(8,128)(2,1)} %get-tuple-element.98), calls=%async_computation.4 | async-start | bytes 1376256 | tf_op jit(solution)/shard_map/all_to_all | solution.py:695
  365.4 49.9 %all-to-all-start.5 = ((bf16[8,336,128]{2,1,0:T(8,128)(2,1)}), bf16[8,336,128]{2,1,0:T(8,128)(2,1)S(1)}, u32[]{:S(2)}, u32[]{:S(2)}) async-start(bf16[8,336,128]{2,1,0:T(8,128)(2,1)} %get-tuple-element.103), calls=%async_computation.5 | async-start | bytes 1376256 | tf_op jit(solution)/shard_map/all_to_all | solution.py:695
  415.3 84.3 %all-to-all-start.6 = ((bf16[8,336,256]{2,1,0:T(8,128)(2,1)}), bf16[8,336,256]{2,1,0:T(8,128)(2,1)}, u32[]{:S(2)}, u32[]{:S(2)}) async-start(bf16[8,336,256]{2,1,0:T(8,128)(2,1)} %get-tuple-element.111), calls=%async_computation.6 | async-start | bytes 2752512 | tf_op jit(solution)/shard_map/all_to_all | solution.py:695
  427.8 143.9 %collective-permute-start = (bf16[8,216,768]{2,1,0:T(8,128)(2,1)}, bf16[8,216,768]{2,1,0:T(8,128)(2,1)}, u32[]{:S(2)}, u32[]{:S(2)}) collective-permute-start(bf16[8,216,768]{2,1,0:T(8,128)(2,1)} %get-tuple-element.173), channel_id=1, source_target_pairs={{0,8},{8,16},{16,24},{24,0},{1,9},{9,17},{17,25},{25,1},{2,10},{10... | collective-permute-start | bytes 7962632 | tf_op jit(solution)/shard_map/ppermute | solution.py:710
  429.3 142.4 %collective-permute-start.1 = (bf16[8,216,768]{2,1,0:T(8,128)(2,1)}, bf16[8,216,768]{2,1,0:T(8,128)(2,1)}, u32[]{:S(2)}, u32[]{:S(2)}) collective-permute-start(bf16[8,216,768]{2,1,0:T(8,128)(2,1)} %get-tuple-element.172), channel_id=1, source_target_pairs={{0,16},{8,24},{16,0},{24,8},{1,17},{9,25},{17,1},{25,9},{2,18},{10... | collective-permute-start | bytes 7962632 | tf_op jit(solution)/shard_map/ppermute | solution.py:710
  430.9 140.9 %collective-permute-start.2 = (bf16[8,216,768]{2,1,0:T(8,128)(2,1)}, bf16[8,216,768]{2,1,0:T(8,128)(2,1)}, u32[]{:S(2)}, u32[]{:S(2)}) collective-permute-start(bf16[8,216,768]{2,1,0:T(8,128)(2,1)} %get-tuple-element.171), channel_id=1, source_target_pairs={{0,24},{8,0},{16,8},{24,16},{1,25},{9,1},{17,9},{25,17},{2,26},{10... | collective-permute-start | bytes 7962632 | tf_op jit(solution)/shard_map/ppermute | solution.py:710
  499.6 72.2 %all-to-all-start.7 = ((bf16[8,336,384]{2,1,0:T(8,128)(2,1)}), bf16[8,336,384]{2,1,0:T(8,128)(2,1)}, u32[]{:S(2)}, u32[]{:S(2)}) async-start(bf16[8,336,384]{2,1,0:T(8,128)(2,1)} %get-tuple-element.113), calls=%async_computation.7 | async-start | bytes 4128768 | tf_op jit(solution)/shard_map/all_to_all | solution.py:695
  504.7 172.9 %reduce-scatter.2.cloned.1.call-start = ((), (), s32[]{:S(2)}) async-start(), calls=%async_computation.12 | async-start | bytes 5971968 | tf_op jit(solution)/shard_map/reduce_scatter | solution.py:823
  582.9 87.5 %all-to-all-start.8 = ((bf16[8,336,384]{2,1,0:T(8,128)(2,1)}), bf16[8,336,384]{2,1,0:T(8,128)(2,1)S(1)}, u32[]{:S(2)}, u32[]{:S(2)}) async-start(bf16[8,336,384]{2,1,0:T(8,128)(2,1)} %get-tuple-element.119), calls=%async_computation.8 | async-start | bytes 4128768 | tf_op jit(solution)/shard_map/all_to_all | solution.py:695
  588.0 149.7 %all-gather.6.cloned.1.call-start = ((), (), s32[]{:S(2)}) async-start(), calls=%async_computation.13 | async-start | bytes 3317760 | tf_op jit(solution)/shard_map/all_gather | solution.py:826
  598.1 81.6 %collective-permute-start.5 = (bf16[8,24,768]{2,1,0:T(8,128)(2,1)S(1)}, bf16[8,24,768]{2,1,0:T(8,128)(2,1)S(1)}, u32[]{:S(2)}, u32[]{:S(2)}) collective-permute-start(bf16[8,24,768]{2,1,0:T(8,128)(2,1)S(1)} %get-tuple-element.178), channel_id=1, source_target_pairs={{0,24},{8,0},{16,8},{24,16},{1,25},{9,1},{17,9},{25,17},{2,26},{10... | collective-permute-start | bytes 884744 | tf_op jit(solution)/shard_map/ppermute | solution.py:710
  598.8 80.9 %collective-permute-start.4 = (bf16[8,24,768]{2,1,0:T(8,128)(2,1)S(1)}, bf16[8,24,768]{2,1,0:T(8,128)(2,1)S(1)}, u32[]{:S(2)}, u32[]{:S(2)}) collective-permute-start(bf16[8,24,768]{2,1,0:T(8,128)(2,1)S(1)} %get-tuple-element.179), channel_id=1, source_target_pairs={{0,16},{8,24},{16,0},{24,8},{1,17},{9,25},{17,1},{25,9},{2,18},{10... | collective-permute-start | bytes 884744 | tf_op jit(solution)/shard_map/ppermute | solution.py:710
  600.3 79.4 %collective-permute-start.3 = (bf16[8,24,768]{2,1,0:T(8,128)(2,1)S(1)}, bf16[8,24,768]{2,1,0:T(8,128)(2,1)}, u32[]{:S(2)}, u32[]{:S(2)}) collective-permute-start(bf16[8,24,768]{2,1,0:T(8,128)(2,1)S(1)} %get-tuple-element.177), channel_id=1, source_target_pairs={{0,8},{8,16},{16,24},{24,0},{1,9},{9,17},{17,25},{25,1},{2,10},{10... | collective-permute-start | bytes 884744 | tf_op jit(solution)/shard_map/ppermute | solution.py:710
  681.6 56.1 %all-to-all-start.9 = ((bf16[8,336,384]{2,1,0:T(8,128)(2,1)}), bf16[8,336,384]{2,1,0:T(8,128)(2,1)}, u32[]{:S(2)}, u32[]{:S(2)}) async-start(bf16[8,336,384]{2,1,0:T(8,128)(2,1)} %get-tuple-element.128), calls=%async_computation.9 | async-start | bytes 4128768 | tf_op jit(solution)/shard_map/all_to_all | solution.py:695
  701.1 27.9 %collective-permute-start.8 = (bf16[8,24,768]{2,1,0:T(8,128)(2,1)}, bf16[8,24,768]{2,1,0:T(8,128)(2,1)}, u32[]{:S(2)}, u32[]{:S(2)}) collective-permute-start(bf16[8,24,768]{2,1,0:T(8,128)(2,1)} %get-tuple-element.181), channel_id=1, source_target_pairs={{0,24},{8,0},{16,8},{24,16},{1,25},{9,1},{17,9},{25,17},{2,26},{10... | collective-permute-start | bytes 884744 | tf_op jit(solution)/shard_map/ppermute | solution.py:710
  703.5 25.5 %collective-permute-start.7 = (bf16[8,24,768]{2,1,0:T(8,128)(2,1)}, bf16[8,24,768]{2,1,0:T(8,128)(2,1)}, u32[]{:S(2)}, u32[]{:S(2)}) collective-permute-start(bf16[8,24,768]{2,1,0:T(8,128)(2,1)} %get-tuple-element.182), channel_id=1, source_target_pairs={{0,16},{8,24},{16,0},{24,8},{1,17},{9,25},{17,1},{25,9},{2,18},{10... | collective-permute-start | bytes 884744 | tf_op jit(solution)/shard_map/ppermute | solution.py:710
  704.0 24.9 %collective-permute-start.6 = (bf16[8,24,768]{2,1,0:T(8,128)(2,1)}, bf16[8,24,768]{2,1,0:T(8,128)(2,1)}, u32[]{:S(2)}, u32[]{:S(2)}) collective-permute-start(bf16[8,24,768]{2,1,0:T(8,128)(2,1)} %get-tuple-element.180), channel_id=1, source_target_pairs={{0,8},{8,16},{16,24},{24,0},{1,9},{9,17},{17,25},{25,1},{2,10},{10... | collective-permute-start | bytes 884744 | tf_op jit(solution)/shard_map/ppermute | solution.py:710
  750.6 14.7 %collective-permute-start.10 = (bf16[8,24,768]{2,1,0:T(8,128)(2,1)S(1)}, bf16[8,24,768]{2,1,0:T(8,128)(2,1)}, u32[]{:S(2)}, u32[]{:S(2)}) collective-permute-start(bf16[8,24,768]{2,1,0:T(8,128)(2,1)S(1)} %get-tuple-element.185), channel_id=1, source_target_pairs={{0,16},{8,24},{16,0},{24,8},{1,17},{9,25},{17,1},{25,9},{2,18},{10... | collective-permute-start | bytes 884744 | tf_op jit(solution)/shard_map/ppermute | solution.py:710
  751.1 14.1 %collective-permute-start.9 = (bf16[8,24,768]{2,1,0:T(8,128)(2,1)S(1)}, bf16[8,24,768]{2,1,0:T(8,128)(2,1)}, u32[]{:S(2)}, u32[]{:S(2)}) collective-permute-start(bf16[8,24,768]{2,1,0:T(8,128)(2,1)S(1)} %get-tuple-element.183), channel_id=1, source_target_pairs={{0,8},{8,16},{16,24},{24,0},{1,9},{9,17},{17,25},{25,1},{2,10},{10... | collective-permute-start | bytes 884744 | tf_op jit(solution)/shard_map/ppermute | solution.py:710
  767.6 37.5 %all-to-all-start.10 = ((bf16[8,24,2304]{2,1,0:T(8,128)(2,1)}), bf16[8,24,2304]{2,1,0:T(8,128)(2,1)}, u32[]{:S(2)}, u32[]{:S(2)}) async-start(bf16[8,24,2304]{2,1,0:T(8,128)(2,1)} %pad_maximum_fusion.1), calls=%async_computation.11 | async-start | bytes 1769472 | tf_op jit(solution)/shard_map/all_to_all | solution.py:695
  772.0 63.7 %all-gather.8.cloned.1.call-start = ((), (), s32[]{:S(2)}) async-start(), calls=%async_computation.14 | async-start | bytes 1720320 | tf_op jit(solution)/shard_map/all_gather | solution.py:865
  (45 other events, 1009.6 us)
Sparse Core Ops, SparseCore 0:
  578.8 98.6 reduce-scatter.1
  679.4 54.2 all-gather.5
  807.4 28.2 all-gather.7

commit v3 on v2

--- a/solution.py
+++ b/solution.py
@@ -24,6 +24,8 @@
 EPS = 1e-06
 NEG = -1e9
 VMEM = 60 << 20
+KEYS = 512
+TILE = 1024
 
 
 def dot(a, b):
@@ -103,130 +105,171 @@
     return ((cell // WIN < row_end) & (cell % WIN < col_end) & live).astype(F32)
 
 
+def send_lanes(plan, normed, weights, bias, send):
+    for part in range(3):
+        at = part * 256
+        made = dot(normed, weights[part][...]) + bias[part][...]
+        top, low = (made[: plan.rows].astype(BF), made[plan.rows :].astype(BF))
+        for g in range(GROUPS):
+            own = slice(g * HDIM, (g + 1) * HDIM)
+            both = jnp.concatenate([top[:, own], low[:, own]], axis=1)
+            send[g, :, part * 128 : (part + 1) * 128] = both
+
+
 def enter_kernel(plan, places, me, *refs):
     count = plan.slots
-    tokens, grads = (refs[:count], refs[count : 2 * count])
-    box, weight, bias, gain, shift = refs[2 * count : 2 * count + 5]
-    x_out, g_out, n_out = refs[2 * count + 5 : 2 * count + 8]
-    sends = refs[2 * count + 8 : 2 * count + 11]
-    xbuf, gbuf, turned = refs[2 * count + 11 :]
+    tokens = refs[:count]
+    weights, bias = (refs[count : count + 3], refs[count + 3 : count + 6])
+    gain, shift, x_out, n_out, send, xbuf = refs[count + 6 :]
+
+    @pl.when(pl.program_id(0) == 0)
+    def _():
+        xbuf[...] = jnp.zeros_like(xbuf)
+
+    for m in range(count):
+        place_rows(xbuf, tokens[m][0].astype(F32), plan, m)
+    x = xbuf[...].reshape(2 * plan.rows, D)
+    x_out[0] = x.astype(BF)
+    scaled, _ = norm_rows(x)
+    normed = (scaled * gain[...] + shift[...]).astype(BF)
+    n_out[0] = normed
+    send_lanes(plan, normed, weights, bias, send)
+
+
+def follow_kernel(plan, places, me, *refs):
+    count = plan.slots
+    grads = refs[:count]
+    box, normed = refs[count : count + 2]
+    weights, bias = (refs[count + 2 : count + 8], refs[count + 8 : count + 14])
+    g_out, *sends = refs[count + 14 : count + 17]
+    gbuf, turned = refs[count + 17 :]
     image = pl.program_id(0)
     slot_count = box.shape[0]
 
     @pl.when(image == 0)
     def _():
-        xbuf[...] = jnp.zeros_like(xbuf)
         gbuf[...] = jnp.zeros_like(gbuf)
         turned[...] = box[...].astype(F32).T
 
+    for h in range(2):
+        own = slice(h * 3, h * 3 + 3)
+        send_lanes(plan, normed[0], weights[own], bias[own], sends[h])
     residue = plan.residue(places, slot_count, me[0], image)
     for m in range(count):
-        place_rows(xbuf, tokens[m][0].astype(F32), plan, m)
         w = residue + plan.wide * m
         slot = plan.slot(places, slot_count, me[0], image, m)
         lane = lax.broadcasted_iota(jnp.int32, (WTOK, slot_count), 1)
         inside = jnp.sum(jnp.where(lane == slot, turned[...], 0.0), axis=1, keepdims=True)
         inside = inside * cell_mask(plan, w, w < WINS)
         place_rows(gbuf, grads[m][0].astype(F32) * inside, plan, m)
-    x = xbuf[...].reshape(2 * plan.rows, D)
-    x_out[0] = x.astype(BF)
     g_out[0] = gbuf[...].reshape(2 * plan.rows, D).astype(BF)
-    scaled, _ = norm_rows(x)
-    normed = (scaled * gain[...] + shift[...]).astype(BF)
-    n_out[0] = normed
-    for part in range(3):
-        made = dot(normed, weight[:, part * D : (part + 1) * D]) + bias[:, part * D : (part + 1) * D]
-        top, low = (made[: plan.rows].astype(BF), made[plan.rows :].astype(BF))
-        for h in range(CHUNKS):
-            for g in range(GROUPS):
-                at = (h * GROUPS + g) * HDIM
-                sends[h][g, :, part * 128 : (part + 1) * 128] = jnp.concatenate(
-                    [top[:, at : at + HDIM], low[:, at : at + HDIM]], axis=1
-                )
-
-
-def enter(plan, places, me, tokens, out_grad, box_mask, weight, bias, gain, shift):
-    slot_count = tokens.shape[0]
-
-    def window(m):
-        return pl.BlockSpec(
-            (1, WTOK, D), lambda i, p, a: (plan.slot(p, slot_count, a[0], i, m), 0, 0)
-        )
-
-    windows = [window(m) for m in range(plan.slots)]
-    fixed = [
-        pl.BlockSpec(x.shape, lambda i, p, a: (0, 0)) for x in (box_mask, weight, bias, gain, shift)
+
+
+def entry_specs(plan, slot_count):
+    windows = [
+        pl.BlockSpec((1, WTOK, D), lambda i, p, a, m=m: (plan.slot(p, slot_count, a[0], i, m), 0, 0))
+        for m in range(plan.slots)
+    ]
+    column = lambda rows, h: [
+        pl.BlockSpec((rows, 256), lambda i, p, a, b=part * CHUNKS + h: (0, b)) for part in range(3)
     ]
     rows = pl.BlockSpec((1, 2 * plan.rows, D), lambda i, p, a: (i, 0, 0))
     send = pl.BlockSpec((GROUPS, plan.rows, 384), lambda i, p, a: (i, 0, 0))
+    return (windows, column, rows, send)
+
+
+def enter(plan, places, me, tokens, weight, bias, gain, shift):
+    windows, column, rows, send = entry_specs(plan, tokens.shape[0])
+    fixed = pl.BlockSpec((1, D), lambda i, p, a: (0, 0))
     working = shape((plan.images, 2 * plan.rows, D), BF)
     return pl.pallas_call(
         partial(enter_kernel, plan),
-        out_shape=[working] * 3 + [shape((plan.wide, plan.rows, 384), BF)] * CHUNKS,
+        out_shape=[working, working, shape((plan.wide, plan.rows, 384), BF)],
         grid_spec=pltpu.PrefetchScalarGridSpec(
             num_scalar_prefetch=2,
             grid=(plan.images,),
-            in_specs=windows + windows + fixed,
-            out_specs=[rows] * 3 + [send] * CHUNKS,
+            in_specs=windows + column(D, 0) + column(1, 0) + [fixed, fixed],
+            out_specs=[rows, rows, send],
+            scratch_shapes=[pltpu.VMEM((2, plan.rows, D), F32)],
+        ),
+        compiler_params=params(),
+        cost_estimate=pl.CostEstimate(
+            flops=2 * 10**9, bytes_accessed=10 << 20, transcendentals=0
+        ),
+        name="enter",
+    )(places, me, *([tokens] * plan.slots), *([weight] * 3), *([bias] * 3), gain, shift)
+
+
+def follow(plan, places, me, out_grad, box_mask, normed, weight, bias):
+    slot_count = out_grad.shape[0]
+    windows, column, rows, send = entry_specs(plan, slot_count)
+    fixed = pl.BlockSpec(box_mask.shape, lambda i, p, a: (0, 0))
+    block = shape((plan.wide, plan.rows, 384), BF)
+    return pl.pallas_call(
+        partial(follow_kernel, plan),
+        out_shape=[shape((plan.images, 2 * plan.rows, D), BF), block, block],
+        grid_spec=pltpu.PrefetchScalarGridSpec(
+            num_scalar_prefetch=2,
+            grid=(plan.images,),
+            in_specs=windows
+            + [fixed, rows]
+            + column(D, 1)
+            + column(D, 2)
+            + column(1, 1)
+            + column(1, 2),
+            out_specs=[rows, send, send],
             scratch_shapes=[
-                pltpu.VMEM((2, plan.rows, D), F32),
                 pltpu.VMEM((2, plan.rows, D), F32),
                 pltpu.VMEM((WTOK, slot_count), F32),
             ],
         ),
         compiler_params=params(),
-        cost_estimate=pl.CostEstimate(flops=6 * 10**9, bytes_accessed=20 << 20, transcendentals=0),
-        name="enter",
-    )(
-        places,
-        me,
-        *([tokens] * plan.slots),
-        *([out_grad] * plan.slots),
-        box_mask,
-        weight,
-        bias,
-        gain,
-        shift,
-    )
-
-
-def leave_kernel(plan, places, me, values, out):
+        cost_estimate=pl.CostEstimate(
+            flops=4 * 10**9, bytes_accessed=16 << 20, transcendentals=0
+        ),
+        name="follow",
+    )(places, me, *([out_grad] * plan.slots), box_mask, normed, *([weight] * 6), *([bias] * 6))
+
+
+def leave_kernel(plan, places, me, values, out, held):
     slot = pl.program_id(0)
     slot_count = pl.num_programs(0)
-    out[...] = jnp.zeros_like(out)
+    held[...] = jnp.zeros_like(held)
     for image in range(plan.images):
         residue = plan.residue(places, slot_count, me[0], image)
         for m in range(plan.slots):
             w = residue + plan.wide * m
-            held = places[image * WINS + jnp.minimum(w, WINS - 1)]
-            hit = (w < WINS) & (held == me[0] * slot_count + slot)
+            place = places[image * WINS + jnp.minimum(w, WINS - 1)]
+            hit = (w < WINS) & (place == me[0] * slot_count + slot)
 
             @pl.when(hit)
             def _(image=image, m=m, w=w):
                 if m < plan.full:
-                    halves = []
+                    keep = cell_mask(plan, w, w < WINS)
                     for half in range(2):
                         at = half * plan.rows + m * HALF
-                        halves.append(values[image, at : at + HALF, :].astype(F32))
-                    keep = cell_mask(plan, w, w < WINS)
-                    out[0, :HALF, :] = (halves[0] * keep[:HALF]).astype(out.dtype)
-                    out[0, HALF:, :] = (halves[1] * keep[HALF:]).astype(out.dtype)
+                        part = slice(half * HALF, (half + 1) * HALF)
+                        held[part, :] = values[image, at : at + HALF, :] * keep[part]
                 else:
                     for row in range(8):
                         at = (row // 4) * plan.rows + plan.corner_at + (row % 4) * 8
-                        piece = values[image, at : at + 8, :]
-                        out[0, row * WIN : row * WIN + 8, :] = piece.astype(out.dtype)
-
-
-def leave(plan, places, me, values, slot_count):
+                        held[row * WIN : row * WIN + 8, :] = values[image, at : at + 8, :]
+
+    out[0] = held[...].astype(out.dtype)
+
+
+def leave(plan, places, me, values, slot_count, kind):
     return pl.pallas_call(
         partial(leave_kernel, plan),
-        out_shape=shape((slot_count, WTOK, D), values.dtype),
+        out_shape=shape((slot_count, WTOK, D), kind),
         grid_spec=pltpu.PrefetchScalarGridSpec(
             num_scalar_prefetch=2,
             grid=(slot_count,),
-            in_specs=[pl.BlockSpec(values.shape, lambda j, p, a: (0, 0, 0))],
+            in_specs=[
+                pl.BlockSpec(values.shape, lambda j, p, a: (0, 0, 0), pipeline_mode=pl.Buffered(1))
+            ],
             out_specs=pl.BlockSpec((1, WTOK, D), lambda j, p, a: (j, 0, 0)),
+            scratch_shapes=[pltpu.VMEM((WTOK, D), F32)],
         ),
         compiler_params=params(),
         cost_estimate=pl.CostEstimate(flops=1 << 20, bytes_accessed=12 << 20, transcendentals=0),
@@ -394,13 +437,18 @@
     count = tile // GRID
     rows, cols = rel_terms(q, table[...], extent[image, 0], extent[image, 1], step * count, count)
     marks = query_marks(q, rows, cols)
-    scores = [dot(marks[i], kt[:, i * (N // 2) : (i + 1) * (N // 2)]) for i in range(2)]
-    top = jnp.maximum(*[jnp.max(s, axis=1, keepdims=True) for s in scores])
-    total = None
-    for i in range(2):
-        weights = jnp.exp(scores[i] - top).astype(BF)
-        x = dot(weights, va[i * (N // 2) : (i + 1) * (N // 2), :])
-        total = x if total is None else total + x
+    side = N // 2
+    score = lambda c: dot(marks[c * KEYS // side], kt[:, c * KEYS : (c + 1) * KEYS])
+    total, top, now = (None, None, score(0))
+    for c in range(N // KEYS):
+        following = score(c + 1) if c + 1 < N // KEYS else None
+        higher = jnp.max(now, axis=1, keepdims=True)
+        if c:
+            higher = jnp.maximum(top, higher)
+        weights = jnp.exp(now - higher).astype(BF)
+        x = dot(weights, va[c * KEYS : (c + 1) * KEYS, :])
+        total = total * jnp.exp(top - higher) + x if c else x
+        top, now = (higher, following)
     mass = total[:, HDIM : HDIM + 1]
     out = total * (1.0 / mass)
     lane = lax.broadcasted_iota(jnp.int32, (tile, 128), 1)
@@ -415,7 +463,7 @@
             send[:, :, 128 * i : 128 * (i + 1)] = block[...]
 
 
-def attention_forward(plan, slot_count, places, me, extent, arrived, table, *earlier, tile=256):
+def attention_forward(plan, slot_count, places, me, extent, arrived, table, *earlier, tile=TILE):
     lanes = 128 * (1 + len(earlier))
     whole = lambda *dims: pl.BlockSpec(dims, lambda t, *_: (0,) * len(dims))
     return pl.pallas_call(
@@ -499,15 +547,21 @@
     do_less = jnp.concatenate([do, less.astype(BF)], 1)
     q_turned = (q.astype(F32) * 0.125).T.astype(BF)
     do_turned = do.astype(F32).T.astype(BF)
-    back = None
-    for i in range(2):
-        part = slice(i * side, (i + 1) * side)
-        weights = jnp.exp(dot(marks[i], kt[:, part]))
-        dscore = (weights * dot(do_less, vt[:, part])).astype(BF)
+    def products(c):
+        part = slice(c * KEYS, (c + 1) * KEYS)
+        return (dot(marks[c * KEYS // side], kt[:, part]), dot(do_less, vt[:, part]))
+
+    back, now = (None, products(0))
+    for c in range(N // KEYS):
+        part = slice(c * KEYS, (c + 1) * KEYS)
+        following = products(c + 1) if c + 1 < N // KEYS else None
+        weights = jnp.exp(now[0])
+        dscore = (weights * now[1]).astype(BF)
         dv[:, part] += dot(do_turned, weights.astype(BF))
         dk[:, part] += dot(q_turned, dscore)
         x = dot(dscore, ka[part, :])
         back = x if back is None else back + x
+        now = following
     blank = jnp.zeros((GRID, HDIM), F32)
     offsets = []
     for i in range(count):
@@ -536,7 +590,7 @@
 
 
 def attention_backward(
-    plan, slot_count, places, me, extent, arrived, lane, kept, saved, table, table_back, tile=512
+    plan, slot_count, places, me, extent, arrived, lane, kept, saved, table, table_back, tile=TILE
 ):
     whole = lambda *dims: pl.BlockSpec(dims, lambda t, *_: (0,) * len(dims))
     return pl.pallas_call(
@@ -571,67 +625,200 @@
     )(places, me, extent, arrived, kept, saved, table, table_back)
 
 
-def join_kernel(plan, first, last, x, weight, bias, attended, middle):
-    returned = (first.at[:, :, :128], first.at[:, :, 128:], last)
-    for half in range(2):
-        lanes = [
-            returned[h][g, :, half * HDIM : (half + 1) * HDIM]
-            for h in range(CHUNKS)
-            for g in range(GROUPS)
-        ]
-        attended[0, half * plan.rows : (half + 1) * plan.rows, :] = jnp.concatenate(lanes, axis=1)
-    middle[0] = x[0].astype(F32) + (dot(attended[0], weight[...]) + bias[...])
-
-
-def join(plan, first, last, x, weight, bias):
-    rows = pl.BlockSpec((1, 2 * plan.rows, D), lambda i: (i, 0, 0))
-    block = pl.BlockSpec((GROUPS, plan.rows, 128), lambda i: (i, 0, 0))
-    working = (plan.images, 2 * plan.rows, D)
+def middle_kernel(
+    plan, first, last, x, g, out_weight, fc1_weight, fc2_weight,
+    out_bias, fc1_bias, fc2_bias, gain, shift,
+    attended, normed, act, grad_before, result, grad_middle, grad_branch, send_first, send_last, sums,
+    grads,
+):
+    step = pl.program_id(0)
+    half = step % 2
+    blocks = [first.at[:, :, :128], first.at[:, :, 128:], last]
+    for side in range(2):
+
+        @pl.when(half == side)
+        def _(side=side):
+            lanes = [
+                blocks[h][k, :, side * HDIM : (side + 1) * HDIM]
+                for h in range(CHUNKS)
+                for k in range(GROUPS)
+            ]
+            attended[0] = jnp.concatenate(lanes, axis=1)
+
+    @pl.when(step == 0)
+    def _():
+        sums[...] = jnp.zeros_like(sums)
+
+    middle = x[0].astype(F32) + (dot(attended[0], out_weight[...]) + out_bias[...])
+    scaled, spread = norm_rows(middle)
+    n = (scaled * gain[...] + shift[...]).astype(BF)
+    normed[0] = n
+    grad = g[0]
+    total, grad_normed = (None, None)
+    add = lambda old, new: new if old is None else old + new
+    for c in range(4):
+        span = slice(c * D, (c + 1) * D)
+        before = dot(n, fc1_weight[:, span]) + fc1_bias[:, span]
+        share = 0.5 + 0.5 * lax.erf(before * (0.5**0.5))
+        low = (before * share).astype(BF)
+        act[0, :, span] = low
+        slope = share + before * (jnp.exp(before * before * -0.5) * 0.3989422804014327)
+        back = (dot_t(grad, fc2_weight[span, :]) * slope).astype(BF)
+        grad_before[0, :, span] = back
+        sums[:, (3 + c) * D : (4 + c) * D] += jnp.sum(back.astype(F32), axis=0, keepdims=True)
+        total = add(total, dot(low, fc2_weight[span, :]))
+        grad_normed = add(grad_normed, dot_t(back, fc1_weight[:, span]))
+    result[0] = middle + total + fc2_bias[...]
+    full = grad.astype(F32) + norm_back(grad_normed * gain[...], scaled, spread)
+    grad_middle[0] = full
+    branch = full.astype(BF)
+    grad_branch[0] = branch
+    for place, value in (
+        (0, branch.astype(F32)), (1, grad_normed * scaled), (2, grad_normed), (7, grad.astype(F32))
+    ):
+        sums[:, place * D : (place + 1) * D] += jnp.sum(value, axis=0, keepdims=True)
+    grads[...] = dot_t(branch, out_weight[...]).astype(BF)
+    targets = [send_first, send_last.at[:, :, :128], send_last.at[:, :, 128:]]
+    for side in range(2):
+
+        @pl.when(half == side)
+        def _(side=side):
+            for h in range(CHUNKS):
+                for k in range(GROUPS):
+                    at = (h * GROUPS + k) * HDIM
+                    made = grads[:, at : at + HDIM]
+                    targets[h][k, :, side * HDIM : (side + 1) * HDIM] = made
+
+
+def middle_part(plan, first, last, x, g, out_weight, fc1_weight, fc2_weight, *vectors):
+    rows, hidden = (plan.rows, fc1_weight.shape[1])
+    halves = 2 * plan.images
+    x, g = (v.reshape(halves, rows, D) for v in (x, g))
+    row = lambda width: pl.BlockSpec((1, rows, width), lambda i: (i, 0, 0))
+    whole = lambda v: pl.BlockSpec(v.shape, lambda i: (0, 0), pipeline_mode=pl.Buffered(1))
+    block = lambda lanes: pl.BlockSpec((GROUPS, rows, lanes), lambda i: (i // 2, 0, 0))
+    made = lambda width, kind: shape((halves, rows, width), kind)
+    fixed = (out_weight, fc1_weight, fc2_weight, *vectors)
     return pl.pallas_call(
-        partial(join_kernel, plan),
-        out_shape=(shape(working, BF), shape(working, F32)),
-        grid=(plan.images,),
-        in_specs=[
-            pl.BlockSpec((GROUPS, plan.rows, 256), lambda i: (i, 0, 0)), block, rows]
-        + [pl.BlockSpec((D, D), lambda i: (0, 0)), pl.BlockSpec((1, D), lambda i: (0, 0))],
-        out_specs=[rows, rows],
+        partial(middle_kernel, plan),
+        out_shape=(
+            made(D, BF), made(D, BF), made(hidden, BF), made(hidden, BF),
+            made(D, F32), made(D, F32), made(D, BF),
+            shape((plan.wide, rows, 128), BF), shape((plan.wide, rows, 256), BF),
+            shape((1, 8 * D), F32),
+        ),
+        grid=(halves,),
+        in_specs=[block(256), block(128), row(D), row(D)] + [whole(v) for v in fixed],
+        out_specs=(
+            row(D), row(D), row(hidden), row(hidden), row(D), row(D), row(D),
+            block(128), block(256), pl.BlockSpec((1, 8 * D), lambda i: (0, 0)),
+        ),
+        scratch_shapes=[pltpu.VMEM((rows, D), BF)],
         compiler_params=params(),
-        cost_estimate=pl.CostEstimate(flops=2 * 10**9, bytes_accessed=10 << 20, transcendentals=0),
-        name="join",
-    )(first, last, x, weight, bias)
-
-
-def part_kernel(plan, grad, weight, first, last):
-    sends = (first, last.at[:, :, :128], last.at[:, :, 128:])
-    made = dot_t(grad[0], weight[...])
-    top, low = (made[: plan.rows].astype(BF), made[plan.rows :].astype(BF))
-    for h in range(CHUNKS):
-        for g in range(GROUPS):
-            at = (h * GROUPS + g) * HDIM
-            made = jnp.concatenate([top[:, at : at + HDIM], low[:, at : at + HDIM]], axis=1)
-            sends[h][g, :, :] = made
-
-
-def part(plan, grad, weight):
+        cost_estimate=pl.CostEstimate(
+            flops=30 * 10**9, bytes_accessed=40 << 20, transcendentals=8 << 20
+        ),
+        name="middle",
+    )(first, last, x, g, *fixed)
+
+
+def shares_kernel(
+    plan, groups, own, normed, grad_before, g, act, attended, branch,
+    o0, o1, o2, o3, fc1, fc2, out, ready, turned_n, turned_g, sem,
+):
+    step, image = (pl.program_id(0), pl.program_id(1))
+    finished = image == pl.num_programs(1) - 1
+    outs = (o0, o1, o2, o3)
+    d = (own[0] + step) % groups
+    piece = D // plan.wide
+    part = piece // groups
+    width = D // groups
+
+    @pl.when(image == 0)
+    def _():
+        fc1[...] = jnp.zeros_like(fc1)
+        fc2[...] = jnp.zeros_like(fc2)
+
+    @pl.when((image == 0) & (step == 0))
+    def _():
+        out[...] = jnp.zeros_like(out)
+
+    @pl.when(step == 0)
+    def _():
+        turned_n[image] = normed[0].astype(F32).T.astype(BF)
+        turned_g[image] = g[0].astype(F32).T.astype(BF)
+        out[...] += t_dot(attended[0], branch[0])
+
+    fc1[...] += dot(turned_n[image], grad_before[0])
+    for k in range(groups):
+
+        @pl.when(d == k)
+        def _(k=k):
+            fc2[...] += dot(turned_g[image, k * width : (k + 1) * width, :], act[0])
+
+    for k in range(groups):
+
+        @pl.when(finished & (step == k))
+        def _(k=k):
+            if k:
+                pltpu.make_async_copy(ready, outs[k - 1], sem).wait()
+            for b in range(plan.wide):
+                ready[b, :piece, :] = fc1[b * piece : (b + 1) * piece, :].astype(BF)
+                cols = slice(b * 4 * piece, (b + 1) * 4 * piece)
+                for side in range(2):
+                    lanes = slice(side * 4 * piece, (side + 1) * 4 * piece)
+                    upper = fc2[side * piece : (side + 1) * piece, cols]
+                    ready[b, piece : 2 * piece, lanes] = upper.astype(BF)
+                at = pl.ds(pl.multiple_of(b * piece + d * part, 8), part)
+                ready[b, 2 * piece :, :] = out[at, :].astype(BF)
+            copy = pltpu.make_async_copy(ready, outs[k], sem)
+            copy.start()
+            if k == groups - 1:
+                copy.wait()
+
+
+def weight_shares(plan, groups, own, normed, grad_before, g, act, attended, branch):
+    rows = 2 * plan.rows
+    fold = lambda v: v.reshape(plan.images, rows, v.shape[-1])
+    values = [fold(v) for v in (normed, grad_before, g, act, attended, branch)]
+    once = pl.BlockSpec((1, rows, D), lambda s, i, o: (jnp.where(s == 0, i, plan.images - 1), 0, 0))
+    wide = pl.BlockSpec((1, rows, values[3].shape[-1]), lambda s, i, o: (i, 0, 0))
+    column = pl.BlockSpec((1, rows, D), lambda s, i, o: (i, 0, (o[0] + s) % groups))
+    block = (plan.wide, 2 * D // plan.wide + D // plan.wide // groups, D)
     return pl.pallas_call(
-        partial(part_kernel, plan),
-        out_shape=[shape((plan.wide, plan.rows, lanes), BF) for lanes in (128, 256)],
-        grid=(plan.images,),
-        in_specs=[
-            pl.BlockSpec((1, 2 * plan.rows, D), lambda i: (i, 0, 0)),
-            pl.BlockSpec((D, D), lambda i: (0, 0)),
-        ],
-        out_specs=[
-            pl.BlockSpec((GROUPS, plan.rows, lanes), lambda i: (i, 0, 0)) for lanes in (128, 256)
-        ],
-        compiler_params=params(),
-        cost_estimate=pl.CostEstimate(flops=2 * 10**9, bytes_accessed=6 << 20, transcendentals=0),
-        name="part",
-    )(grad, weight)
-
-
-def collect_kernel(plan, chunk, arrived, normed, wq, wk, wv, *refs):
-    before, (total, weight_grad, bias_grad, held) = (refs[:-4], refs[-4:])
+        partial(shares_kernel, plan, groups),
+        out_shape=[shape(block, BF)] * groups,
+        grid_spec=pltpu.PrefetchScalarGridSpec(
+            num_scalar_prefetch=1,
+            grid=(groups, plan.images),
+            in_specs=[once, column, once, wide, once, once],
+            out_specs=[pl.BlockSpec(memory_space=pl.ANY)] * groups,
+            scratch_shapes=[
+                pltpu.VMEM((D, D), F32),
+                pltpu.VMEM((D // groups, 4 * D), F32),
+                pltpu.VMEM((D, D), F32),
+                pltpu.VMEM(block, BF),
+                pltpu.VMEM((plan.images, D, rows), BF),
+                pltpu.VMEM((plan.images, D, rows), BF),
+                pltpu.SemaphoreType.DMA,
+            ],
+        ),
+        compiler_params=params("arbitrary", "arbitrary"),
+        cost_estimate=pl.CostEstimate(
+            flops=15 * 10**9, bytes_accessed=60 << 20, transcendentals=0
+        ),
+        name="weight_shares",
+    )(own, *values)
+
+
+def collect_kernel(plan, chunk, groups, kinds, own, arrived, normed, wq, wk, wv, *refs):
+    before, middle_grad, x, gain = (None,) * 4
+    if chunk > 0:
+        before, refs = (refs[0], refs[1:])
+    if chunk == CHUNKS - 1:
+        (middle_grad, x, gain), refs = (refs[:3], refs[3:])
+    total, bias_grad = refs[:2]
+    outs, (held,) = (refs[2:-1], refs[-1:])
     image = pl.program_id(0)
 
     @pl.when(image == 0)
@@ -640,7 +827,7 @@
         bias_grad[...] = jnp.zeros_like(bias_grad)
 
     n = normed[0]
-    whole = None
+    whole = before[0] if chunk > 0 else None
     for p, weight in enumerate((wq, wk, wv)):
         halves = []
         for half in range(2):
@@ -648,43 +835,64 @@
             lanes = [arrived[g, :, at : at + HDIM] for g in range(GROUPS)]
             halves.append(jnp.concatenate(lanes, axis=1))
         y = jnp.concatenate(halves, axis=0)
-        x = dot_t(y, weight[...])
-        whole = x if whole is None else whole + x
+        made = dot_t(y, weight[...])
+        whole = made if whole is None else whole + made
         span = slice(p * 256, (p + 1) * 256)
         held[:, span] += t_dot(n, y)
         bias_grad[0:1, span] += jnp.sum(y.astype(F32), axis=0, keepdims=True)
-    total[0] = whole + before[0][0] if before else whole
+    if chunk == CHUNKS - 1:
+        scaled, spread = norm_rows(x[0].astype(F32))
+        total[0] = middle_grad[0] + norm_back(whole * gain[...], scaled, spread)
+        bias_grad[0:1, D : 2 * D] += jnp.sum(whole * scaled, axis=0, keepdims=True)
+        bias_grad[0:1, 2 * D :] += jnp.sum(whole, axis=0, keepdims=True)
+    else:
+        total[0] = whole
 
     @pl.when(image == pl.num_programs(0) - 1)
     def _():
-        weight_grad[...] = held[...].astype(weight_grad.dtype)
-
-
-def collect(plan, chunk, arrived, normed, weight, before):
-    rows = pl.BlockSpec((1, 2 * plan.rows, D), lambda i: (i, 0, 0))
-    columns = [pl.BlockSpec((D, 256), lambda i, p=p: (0, p * 3 + chunk)) for p in range(3)]
-    extra = () if before is None else (before,)
-    return pl.pallas_call(
-        partial(collect_kernel, plan, chunk),
-        out_shape=(
-            shape((plan.images, 2 * plan.rows, D), F32),
-            shape((D, D), BF),
-            shape((8, D), F32),
-        ),
-        grid=(plan.images,),
-        in_specs=[pl.BlockSpec((GROUPS, plan.rows, 384), lambda i: (i, 0, 0)), rows]
-        + columns
-        + [rows] * len(extra),
-        out_specs=[
-            rows,
-            pl.BlockSpec((D, D), lambda i: (0, 0)),
-            pl.BlockSpec((8, D), lambda i: (0, 0)),
-        ],
-        scratch_shapes=[pltpu.VMEM((D, D), F32)],
+        if len(outs) == 1:
+            outs[0][...] = held[...].astype(BF)
+            return
+        piece = D // plan.wide
+        part = piece // groups
+        for k in range(groups):
+            first = (own[0] + k) % groups * part
+            for b in range(plan.wide):
+                at = pl.ds(pl.multiple_of(first + b * piece, 8), part)
+                outs[k][b] = held[at, :].astype(BF)
+
+
+def collect(plan, chunk, groups, own, aligned, arrived, normed, weight, *extra):
+    rows = pl.BlockSpec((1, 2 * plan.rows, D), lambda i, o: (i, 0, 0))
+    columns = [pl.BlockSpec((D, 256), lambda i, o, p=p: (0, p * 3 + chunk)) for p in range(3)]
+    last = chunk == CHUNKS - 1
+    width = 3 * D if last else D
+    fixed = lambda *dims: pl.BlockSpec(dims, lambda i, o: (0,) * len(dims))
+    if aligned:
+        blocks = [(plan.wide, D // plan.wide // groups, D)] * groups
+    else:
+        blocks = [(D, D)]
+    more = [rows] * (chunk > 0) + ([rows, rows, fixed(1, D)] if last else [])
+    total, sums, *outs = pl.pallas_call(
+        partial(collect_kernel, plan, chunk, groups, None),
+        out_shape=[shape((plan.images, 2 * plan.rows, D), F32), shape((8, width), F32)]
+        + [shape(b, BF) for b in blocks],
+        grid_spec=pltpu.PrefetchScalarGridSpec(
+            num_scalar_prefetch=1,
+            grid=(plan.images,),
+            in_specs=[pl.BlockSpec((GROUPS, plan.rows, 384), lambda i, o: (i, 0, 0)), rows]
+            + columns
+            + more,
+            out_specs=[rows, fixed(8, width)] + [fixed(*b) for b in blocks],
+            scratch_shapes=[pltpu.VMEM((D, D), F32)],
+        ),
         compiler_params=params(),
-        cost_estimate=pl.CostEstimate(flops=8 * 10**9, bytes_accessed=20 << 20, transcendentals=0),
+        cost_estimate=pl.CostEstimate(
+            flops=8 * 10**9, bytes_accessed=20 << 20, transcendentals=0
+        ),
         name="collect",
-    )(arrived, normed, weight, weight, weight, *extra)
+    )(own, arrived, normed, weight, weight, weight, *extra)
+    return (total, sums[0], outs)
 
 
 def tie(value, *others):
@@ -700,15 +908,20 @@
     return grad.astype(BF).reshape(wide, groups, piece, D).transpose(1, 0, 2, 3)
 
 
-def over_groups(low):
+def over_groups(blocks):
+    groups = len(blocks)
+    got = [blocks[0]]
+    for d in range(1, groups):
+        pairs = [(i, (i + d) % groups) for i in range(groups)]
+        got.append(lax.ppermute(blocks[d], "dp", pairs))
+    return got
+
+
+def turn_groups(low):
     groups = low.shape[0]
     own = lax.axis_index("dp")
     take = lambda i: lax.dynamic_index_in_dim(low, i, 0, keepdims=False)
-    got = [take(own)]
-    for d in range(1, groups):
-        pairs = [(i, (i + d) % groups) for i in range(groups)]
-        got.append(lax.ppermute(take((own + d) % groups), "dp", pairs))
-    return got
+    return [take((own + d) % groups) for d in range(groups)]
 
 
 def add_groups(got):
@@ -731,17 +944,22 @@
     me = lax.axis_index("wide").astype(jnp.int32).reshape(1)
     plan = Plan(wide, image_extent.shape[0])
     slots = tokens.shape[0]
+    aligned = D // wide // groups % 8 == 0 and D // wide * 4 % 128 == 0
     wide_f = lambda v: v.astype(F32).reshape(1, -1)
     bias = jnp.concatenate([qv_bias[0], jnp.zeros((D,), BF), qv_bias[1]])
     blank = jnp.zeros((1, HDIM), BF)
     table = jnp.concatenate([rel_rows[::-1], blank, rel_cols[::-1], blank], 0)
     table_back = jnp.concatenate([rel_rows[::-1], blank, rel_cols, blank], 0)
-    x, grad_out, normed1, *sends = enter(
-        plan, window_place, me, tokens, out_grad, box_mask,
+    x, normed1, send = enter(
+        plan, window_place, me, tokens,
         qkv_weight, wide_f(bias), wide_f(norm1_gain), wide_f(norm1_shift),
     )
     forward = []
-    arrived = exchange(sends[0])
+    arrived = exchange(send)
+    grad_out, *sends = follow(
+        plan, window_place, me, out_grad, box_mask, normed1, qkv_weight, wide_f(bias)
+    )
+    sends = [send, *sends]
     for h in range(CHUNKS):
         if h + 1 < CHUNKS:
             following, arrived = lax.optimization_barrier((sends[h + 1], arrived))
@@ -757,49 +975,43 @@
         )
         arrived = following
     last, first = lax.optimization_barrier((forward[2][0], first))
-    attended, middle = join(plan, first, exchange(last), x, out_weight, wide_f(out_bias))
+    last = exchange(last)
     rows = plan.images * 2 * plan.rows
-    attended = attended.reshape(rows, D)
-    middle = middle.reshape(rows, D)
-    grad_low = grad_out.reshape(rows, D)
-    grad_result = grad_low.astype(F32)
-    scaled2, spread2 = norm_rows(middle)
-    normed2 = (scaled2 * wide_f(norm2_gain) + wide_f(norm2_shift)).astype(BF)
-    before = dot(normed2, fc1_weight) + wide_f(fc1_bias)
-    activated, gelu_pull = jax.vjp(partial(jax.nn.gelu, approximate=False), before)
-    act_low = activated.astype(BF)
-    grad_before = gelu_pull(dot_t(grad_low, fc2_weight))[0].astype(BF)
-    grad_normed2 = dot_t(grad_before, fc1_weight)
-    grad_middle = grad_result + norm_back(grad_normed2 * wide_f(norm2_gain), scaled2, spread2)
-    grad_branch = grad_middle.astype(BF)
-    grad_sends = part(plan, grad_branch.reshape(plan.images, 2 * plan.rows, D), out_weight)
-
-    grad_arrived = exchange(grad_sends[0])
-    normed2, act_low, attended, _ = lax.optimization_barrier(
-        (normed2, act_low, attended, grad_sends[0])
+    (
+        attended, normed2, act_low, grad_before, result, grad_middle, grad_branch,
+        send_first, send_last, early,
+    ) = middle_part(
+        plan, first, last, x, grad_out, out_weight, fc1_weight, fc2_weight,
+        wide_f(out_bias), wide_f(fc1_bias), wide_f(fc2_bias), wide_f(norm2_gain), wide_f(norm2_shift),
     )
-    fc1_low = t_dot(normed2, grad_before).astype(BF).reshape(D, groups, D).transpose(1, 0, 2)
-    shares = jnp.concatenate(
-        [
-            fc1_low.reshape(groups, wide, D // wide, D),
-            share_rows(t_dot(act_low, grad_low), wide, groups),
-            share_rows(t_dot(attended, grad_branch), wide, groups),
-        ],
-        axis=2,
-    )
-    total = lambda v: jnp.sum(v.astype(F32), axis=0)
-    early = jnp.concatenate(
-        [
-            total(grad_branch),
-            total(grad_normed2 * scaled2),
-            total(grad_normed2),
-            total(grad_before),
-            total(grad_result),
-        ]
-    )
-    shares, grad_arrived, early = lax.optimization_barrier((shares, grad_arrived, early))
+    grad_middle = grad_middle.reshape(rows, D)
+    early = early.reshape(-1)
+    grad_arrived = exchange(send_first)
+    own = lax.axis_index("dp").astype(jnp.int32).reshape(1)
+    if aligned:
+        shares = weight_shares(
+            plan, groups, own, normed2, grad_before, grad_out, act_low, attended, grad_branch
+        )
+    else:
+        normed2, act_low, attended, _ = lax.optimization_barrier(
+            (normed2, act_low, attended, send_first)
+        )
+        flat = lambda v: v.reshape(rows, v.shape[-1])
+        fc1_low = t_dot(flat(normed2), flat(grad_before)).astype(BF)
+        fc1_low = fc1_low.reshape(D, groups, D).transpose(1, 0, 2)
+        shares = turn_groups(
+            jnp.concatenate(
+                [
+                    fc1_low.reshape(groups, wide, D // wide, D),
+                    share_rows(t_dot(flat(act_low), flat(grad_out)), wide, groups),
+                    share_rows(t_dot(flat(attended), flat(grad_branch)), wide, groups),
+                ],
+                axis=2,
+            )
+        )
+    *shares, grad_arrived = lax.optimization_barrier((*shares, grad_arrived))
     shares = over_groups(shares)
-    following = exchange(tie(grad_sends[1], grad_arrived))
+    following = exchange(tie(send_last, grad_arrived))
 
     rel_total = None
     grad_qkv = []
@@ -820,58 +1032,55 @@
         grad_qkv.append(exchange(send))
         if h + 1 < CHUNKS and h > 0:
             grad_arrived = tie(grad_arrived, grad_qkv[-2])
-    shares = lax.psum_scatter(shares, "wide", scatter_dimension=0, tiled=True)[0]
-    result, act_low, _ = lax.optimization_barrier((middle, act_low, send))
+    shares = lax.psum_scatter(shares.astype(BF), "wide", scatter_dimension=0, tiled=True)[0]
     shares = tie(shares, send)
-    shares = lax.all_gather(shares, "dp", axis=0, tiled=False)
-    result = result + dot(act_low, fc2_weight) + wide_f(fc2_bias)
-    tokens_out = leave(plan, window_place, me, result.reshape(plan.images, 2 * plan.rows, D), slots)
-    tokens_out = tokens_out.astype(BF)
-    grad_normed1 = None
-    weight_grads, bias_grads = ([], [])
-    for h in range(CHUNKS):
-        arrived = grad_qkv[h]
-        if h == 2:
-            arrived, shares, tokens_out, _ = lax.optimization_barrier(
-                (arrived, shares, tokens_out, grad_normed1)
-            )
-        grad_normed1, weight_grad, bias_grad = collect(
-            plan, h, arrived, normed1, qkv_weight, grad_normed1
-        )
-        weight_grads.append(
-            add_groups(over_groups(share_rows(weight_grad, wide, groups))).astype(BF)
-        )
-        bias_grads.append(bias_grad[0].reshape(3, 256))
-    weight_grads = exchange(jnp.concatenate(weight_grads, axis=2))
-    bias_grad = jnp.stack(bias_grads, axis=1).reshape(3, D)
-    grad_normed1 = grad_normed1.reshape(rows, D)
-    scaled1, spread1 = norm_rows(x.reshape(rows, D).astype(F32))
-    grad_inputs = grad_middle + norm_back(grad_normed1 * wide_f(norm1_gain), scaled1, spread1)
-    sums = jnp.concatenate(
-        [
-            early,
-            total(grad_normed1 * scaled1),
-            total(grad_normed1),
-            bias_grad[0],
-            bias_grad[2],
-            rel_total.reshape(-1),
-            jnp.zeros((512,), F32),
-        ]
-    ).reshape(-1, D)
-    sums = jnp.sum(lax.all_gather(sums, "wide", axis=0, tiled=False), axis=0)
+    shares = lax.all_gather(shares, "dp", axis=0, tiled=False).astype(F32)
+    result = tie(result, send)
+    tokens_out = leave(
+        plan, window_place, me, result.reshape(plan.images, 2 * plan.rows, D), slots, BF
+    )
+    mid = jnp.concatenate([early, rel_total.reshape(-1), jnp.zeros((512,), F32)]).reshape(-1, D)
+    mid = jnp.sum(lax.all_gather(tie(mid, send), "dp", axis=0, tiled=False), axis=0)
+    fold = lambda v: v.reshape(plan.images, 2 * plan.rows, D)
+    around = lambda b: over_groups(b if aligned else turn_groups(share_rows(b[0], wide, groups)))
+    gather = partial(collect, plan)
+    fixed = (groups, own, aligned)
+    totals, sums0, blocks = gather(0, *fixed, grad_qkv[0], normed1, qkv_weight)
+    got0 = around(blocks)
+    totals, sums1, blocks = gather(1, *fixed, grad_qkv[1], normed1, qkv_weight, totals)
+    got1 = around(blocks)
+    *got, _ = lax.optimization_barrier((*got0, *got1, tokens_out))
+    ready = [add_groups(got[:groups]).astype(BF), add_groups(got[groups:]).astype(BF)]
+    arrived, shares, mid, *ready = lax.optimization_barrier((grad_qkv[2], shares, mid, *ready))
+    early_sums = exchange(jnp.concatenate(ready, axis=2))
+    totals, sums2, blocks = gather(
+        2, *fixed, arrived, normed1, qkv_weight, totals, fold(grad_middle), x, wide_f(norm1_gain)
+    )
+    weight_grad = add_groups(around(blocks)).astype(BF)
+    third = [c[:D].reshape(3, 256) for c in (sums0, sums1, sums2)]
+    late = jnp.concatenate([sums2[D:]] + [t[0] for t in third] + [t[2] for t in third])
+    small = jnp.concatenate([late.reshape(-1, D), mid], axis=0)
+    small = jnp.sum(lax.all_gather(small, "wide", axis=0, tiled=False), axis=0)
+    weight_grad, early_sums, small, totals, shares = lax.optimization_barrier(
+        (weight_grad, early_sums, small, totals, shares)
+    )
+    last = exchange(weight_grad)
     share = D // wide
     piece = share // groups
-    last = jnp.concatenate([add_wide(weight_grads).reshape(-1, D), sums], axis=0)
+    weight_sums = jnp.concatenate([add_wide(early_sums), add_wide(last)], axis=1)
+    last = jnp.concatenate([weight_sums.reshape(-1, D), small[:4]], axis=0)
     last = lax.all_gather(last, "dp", axis=0, tiled=False)
     qkv_weight_grad = last[:, : 3 * piece].reshape(share, CHUNKS, 3, 256)
     qkv_weight_grad = qkv_weight_grad.transpose(0, 2, 1, 3).reshape(share, 3 * D)
-    sums = jnp.sum(last[:, 3 * piece :], axis=0).reshape(-1)
-    tokens_grad = leave(
-        plan, window_place, me, grad_inputs.reshape(plan.images, 2 * plan.rows, D), slots
-    )
-    late = sums[8 * D : 12 * D]
-    rel_total = sums[12 * D : 12 * D + HDIM * 256].reshape(HDIM, 256).T
+    late = jnp.sum(last[:, 3 * piece :], axis=0).reshape(-1)
+    sums = small[4:].reshape(-1)
+    tokens_grad = leave(plan, window_place, me, totals, slots, F32)
+    rel_total = sums[8 * D : 8 * D + HDIM * 256].reshape(HDIM, 256).T
     small = sums[: 8 * D]
+    fc2_share = shares[:, share : 2 * share]
+    if aligned:
+        fc2_share = fc2_share.reshape(groups, share, 2, 4 * share).transpose(3, 0, 2, 1)
+    fc2_share = fc2_share.reshape(4 * share, D)
     return (
         tokens_out,
         tokens_grad,
@@ -887,7 +1096,7 @@
         small[2 * D : 3 * D],
         shares[:, :share].transpose(1, 0, 2).reshape(share, 4 * D),
         small[3 * D : 7 * D],
-        shares[:, share : 2 * share].reshape(4 * share, D),
+        fc2_share,
         small[7 * D :],
     )
 

time: 861 us -> 693 us (0.80)
  matrix products: 123 us -> 0 us
  waiting for transfers between devices: 51.5 us -> 94.8 us
  other arithmetic: 50.7 us -> 15.3 us
  local copies, waits for them, and re-layouts: 57.4 us -> 24.8 us
  blocking collectives: 84.1 us -> 60.8 us
  starting transfers between devices: 62.4 us -> 72.4 us
    dot_general x7 -> x0, matrix products: 123 us -> none  [the longest x2 59.2 us: dot(): return jnp.dot(a, b, preferred_element_type=F32)]
    pallas_call x6 -> x7, Pallas kernels: 50.6 us -> 123 us  [the longest x1 46.5 us: middle_part(): pl.pallas_call(partial(middle_kernel, plan), out_shape=(made(D, BF), made...]
    all_to_all x10 -> x12, waiting for transfers between devices: 27.9 us -> 94.7 us  [exchange(): return lax.all_to_all(blocks, axis, split_axis=0, concat_axis=0, tiled=True)]
    all_to_all x1 -> x0, blocking collectives: 54.8 us -> none  [exchange(): return lax.all_to_all(blocks, axis, split_axis=0, concat_axis=0, tiled=True)]
    pallas_call x3, Pallas kernels: 140 us -> 93.3 us  [attention_forward(): pl.pallas_call(partial(forward_kernel, plan, tile, slot_count), out_shape...]
    all_gather x1 -> x3, blocking collectives: 29.3 us -> 60.8 us  [the longest x1 24 us: shards(): small = jnp.sum(lax.all_gather(small, 'wide', axis=0, tiled=False), axis=0)]
    pallas_call x3, Pallas kernels: 202 us -> 174 us  [attention_backward(): pl.pallas_call(partial(backward_kernel, plan, tile, slot_count), out_shap...]
    squeeze x6 -> x0, local copies, waits for them, and re-layouts: 14.7 us -> none  [the longest x4 12.1 us: over_groups(): take = lambda i: lax.dynamic_index_in_dim(low, i, 0, keepdims=False)]
  transfers between devices with their start and end apart: 25 -> 26, of which waited for: 8 -> 6; matrix products, arithmetic and copies ran while one was open for 13% -> 4% of each run, Pallas kernels for 44% -> 49%
where the time goes in v3:
time: 693 us; the launch traced here: 687 us
  Pallas kernels  404 us (58%)
  waiting for transfers between devices  94.8 us (14%)
  starting transfers between devices  72.4 us (10%)
  blocking collectives  60.8 us (9%)
  local copies, waits for them, and re-layouts  24.8 us (4%)
  other arithmetic  15.3 us (2%)
  between operations  15 us (2%)
    pallas_call x3, Pallas kernels, attention_backward(): pl.pallas_call(partial(backward_kernel, plan, tile, slot_count), out_shap...  174 us
    all_to_all x12, waiting for transfers between devices, exchange(): return lax.all_to_all(blocks, axis, split_axis=0, concat_axis=0, tiled=True)  94.7 us
    pallas_call x3, Pallas kernels, attention_forward(): pl.pallas_call(partial(forward_kernel, plan, tile, slot_count), out_shape...  93.3 us
    all_to_all x12, starting transfers between devices, exchange(): return lax.all_to_all(blocks, axis, split_axis=0, concat_axis=0, tiled=True)  56.6 us
    pallas_call x1, Pallas kernels, middle_part(): pl.pallas_call(partial(middle_kernel, plan), out_shape=(made(D, BF), made...  46.5 us
    pallas_call x1, Pallas kernels, weight_shares(): pl.pallas_call(partial(shares_kernel, plan, groups), out_shape=[shape(blo...  30.9 us
    pallas_call x3, Pallas kernels, collect(): pl.pallas_call(partial(collect_kernel, plan, chunk, groups, None), out_sh...  28.9 us
    all_gather x1, blocking collectives, shards(): small = jnp.sum(lax.all_gather(small, 'wide', axis=0, tiled=False), axis=0)  24 us
  transfers between devices with their start and end apart: 26, of which 6 were waited for; matrix products, arithmetic and copies ran while one was open for 4% of the time, Pallas kernels for 49%

profile of v3, /device:TPU:0, one launch (start us, length us, event | category | flops | bytes accessed | tf_op | source)
XLA Modules:
  0.0 687.5 jit_solution(8963926850447239739)
XLA Ops:
  11.1 7.1 %enter.1 = (bf16[2,672,768]{2,1,0:T(8,128)(2,1)}, bf16[2,672,768]{2,1,0:T(8,128)(2,1)}, bf16[8,336,384]{2,1,0:T(8,128)(2,1)}) custom-call(s32[50]{0:T(128)} %places.19, s32[1]{0:T(128)} %bitcast.me, bf16[7,196,768]{2,1,0:T(8,128)(2,1)} %refs_3_.2, bf16[7,196,768]{2,1,0:T(8,128)(2,1)} %refs_3_.2, bf16[7,196,768]{2,1,0:T(8,128)(2,1)} %refs_3_.2, ...), custom_call_target="tpu_custom_call" | custom-call | flops 2000000000 | bytes 10485760 | tf_op jit(solution)/shard_map/enter/pallas_call | solution.py:185
  18.2 6.3 all-to-all-start
  24.5 9.4 %follow.1 = (bf16[2,672,768]{2,1,0:T(8,128)(2,1)}, bf16[8,336,384]{2,1,0:T(8,128)(2,1)}, bf16[8,336,384]{2,1,0:T(8,128)(2,1)}) custom-call(s32[50]{0:T(128)} %places.19, s32[1]{0:T(128)} %bitcast.me, bf16[7,196,768]{2,1,0:T(8,128)(2,1)} %refs_3_.3, bf16[7,196,768]{2,1,0:T(8,128)(2,1)} %refs_3_.3, bf16[7,196,768]{2,1,0:T(8,128)(2,1)} %refs_3_.3, ...), custom_call_target="tpu_custom_call" | custom-call | flops 4000000000 | bytes 16777216 | tf_op jit(solution)/shard_map/follow/pallas_call | solution.py:208
  33.9 39.0 %all-to-all-done.arrived = bf16[8,336,384]{2,1,0:T(8,128)(2,1)S(1)} async-done(((bf16[8,336,384]{2,1,0:T(8,128)(2,1)}), bf16[8,336,384]{2,1,0:T(8,128)(2,1)S(1)}, u32[]{:S(2)}, u32[]{:S(2)}) %all-to-all-start) | async-done | bytes 2064416 | tf_op jit(solution)/shard_map/all_to_all | solution.py:903
  79.0 30.9 %attention_forward.3 = (bf16[8,336,128]{2,1,0:T(8,128)(2,1)}, bf16[3,4096,64]{2,1,0:T(8,128)(2,1)}, f32[4096,128]{1,0:T(8,128)}) custom-call(s32[50]{0:T(128)} %places.19, s32[1]{0:T(128)} %bitcast.me, s32[2,2]{1,0:T(2,128)} %extent.11, bf16[8,336,384]{2,1,0:T(8,128)(2,1)} %copy-done.4, bf16[256,64]{1,0:T(8,128)(2,1)} %get-tuple-element.279.table), custom_call_target="tpu_custom_call" | custom-call | flops 17179869184 | bytes 12582912 | tf_op jit(solution)/shard_map/attention_forward/pallas_call | solution.py:469
  109.8 16.4 %all-to-all-done.1.arrived = bf16[8,336,384]{2,1,0:T(8,128)(2,1)} async-done(((bf16[8,336,384]{2,1,0:T(8,128)(2,1)}), bf16[8,336,384]{2,1,0:T(8,128)(2,1)}, u32[]{:S(2)}, u32[]{:S(2)}) %all-to-all-start.1) | async-done | bytes 2064416 | tf_op jit(solution)/shard_map/all_to_all | solution.py:903
  130.0 31.5 %attention_forward.4 = (bf16[8,336,256]{2,1,0:T(8,128)(2,1)}, bf16[3,4096,64]{2,1,0:T(8,128)(2,1)}, f32[4096,128]{1,0:T(8,128)}) custom-call(s32[50]{0:T(128)} %places.19, s32[1]{0:T(128)} %bitcast.me, s32[2,2]{1,0:T(2,128)} %extent.11, bf16[8,336,384]{2,1,0:T(8,128)(2,1)} %all-to-all-done.1.arrived, bf16[256,64]{1,0:T(8,128)(2,1)} %get-tuple-element.279.table, ...), custom_call_target="tpu_custom_call" | custom-call | flops 17179869184 | bytes 12582912 | tf_op jit(solution)/shard_map/attention_forward/pallas_call | solution.py:469
  161.5 16.8 %all-to-all-done.2.arrived = bf16[8,336,384]{2,1,0:T(8,128)(2,1)S(1)} async-done(((bf16[8,336,384]{2,1,0:T(8,128)(2,1)}), bf16[8,336,384]{2,1,0:T(8,128)(2,1)S(1)}, u32[]{:S(2)}, u32[]{:S(2)}) %all-to-all-start.2) | async-done | bytes 2064416 | tf_op jit(solution)/shard_map/all_to_all | solution.py:903
  182.4 31.0 %attention_forward.5 = (bf16[8,336,128]{2,1,0:T(8,128)(2,1)}, bf16[3,4096,64]{2,1,0:T(8,128)(2,1)}, f32[4096,128]{1,0:T(8,128)}) custom-call(s32[50]{0:T(128)} %places.19, s32[1]{0:T(128)} %bitcast.me, s32[2,2]{1,0:T(2,128)} %extent.11, bf16[8,336,384]{2,1,0:T(8,128)(2,1)} %copy-done.5, bf16[256,64]{1,0:T(8,128)(2,1)} %get-tuple-element.279.table), custom_call_target="tpu_custom_call" | custom-call | flops 17179869184 | bytes 12582912 | tf_op jit(solution)/shard_map/attention_forward/pallas_call | solution.py:469
  222.5 15.8 %all-to-all-done.4.last = bf16[8,336,128]{2,1,0:T(8,128)(2,1)S(1)} async-done(((bf16[8,336,128]{2,1,0:T(8,128)(2,1)}), bf16[8,336,128]{2,1,0:T(8,128)(2,1)S(1)}, u32[]{:S(2)}, u32[]{:S(2)}) %all-to-all-start.4) | async-done | bytes 688160 | tf_op jit(solution)/shard_map/all_to_all | solution.py:903
  239.2 46.5 %middle.1 = (bf16[4,336,768]{2,1,0:T(8,128)(2,1)}, bf16[4,336,768]{2,1,0:T(8,128)(2,1)}, bf16[4,336,3072]{2,1,0:T(8,128)(2,1)}, bf16[4,336,3072]{2,1,0:T(8,128)(...) custom-call(bf16[8,336,256]{2,1,0:T(8,128)(2,1)} %copy-done.7, ...), custom_call_target="tpu_custom_call" | custom-call | flops 30000001024 | bytes 41943040 | tf_op jit(solution)/shard_map/middle/pallas_call | solution.py:702
  289.2 30.9 %weight_shares.1 = (bf16[8,216,768]{2,1,0:T(8,128)(2,1)}, bf16[8,216,768]{2,1,0:T(8,128)(2,1)}, bf16[8,216,768]{2,1,0:T(8,128)(2,1)}, bf16[8,216,768]{2,1,0:T(8,128)(2,1)}) custom-call(s32[1]{0:T(128)} %bitcast.4.own, bf16[2,672,768]{2,1,0:T(8,128)(2,1)} %bitcast.64, bf16[2,672,3072]{2,1,0:T(8,128)(2,1)} %bitcast.61, ...), custom_call_target="tpu_custom_call" | custom-call | flops 15000000512 | bytes 62914560 | tf_op jit(solution)/shard_map/weight_shares/pallas_call | solution.py:788
  329.7 58.0 %attention_backward.3 = (bf16[8,336,384]{2,1,0:T(8,128)(2,1)}, f32[64,256]{1,0:T(8,128)}) custom-call(s32[50]{0:T(128)} %places.19, s32[1]{0:T(128)} %bitcast.me, s32[2,2]{1,0:T(2,128)} %extent.11, bf16[8,336,128]{2,1,0:T(8,128)(2,1)} %copy-done.8, bf16[3,4096,64]{2,1,0:T(8,128)(2,1)} %get-tuple-element.147.kept, f32[4096,128]{1,0:T(8,128)} %get-tuple-element.126.saved, ...), custom_call_target="tpu_custom_call" | custom-call | flops 42949672960 | bytes 12582912 | tf_op jit(solution)/shard_map/attention_backward/pallas_call | solution.py:596
  392.8 57.7 %attention_backward.4 = (bf16[8,336,384]{2,1,0:T(8,128)(2,1)}, f32[64,256]{1,0:T(8,128)}) custom-call(s32[50]{0:T(128)} %places.19, s32[1]{0:T(128)} %bitcast.me, s32[2,2]{1,0:T(2,128)} %extent.11, bf16[8,336,256]{2,1,0:T(8,128)(2,1)} %copy-done.6, bf16[3,4096,64]{2,1,0:T(8,128)(2,1)} %get-tuple-element.158.kept, f32[4096,128]{1,0:T(8,128)} %get-tuple-element.159.saved, ...), custom_call_target="tpu_custom_call" | custom-call | flops 42949672960 | bytes 12582912 | tf_op jit(solution)/shard_map/attention_backward/pallas_call | solution.py:596
  456.0 6.2 convert_add_fusion
  462.2 58.1 %attention_backward.5 = (bf16[8,336,384]{2,1,0:T(8,128)(2,1)}, f32[64,256]{1,0:T(8,128)}) custom-call(s32[50]{0:T(128)} %places.19, s32[1]{0:T(128)} %bitcast.me, s32[2,2]{1,0:T(2,128)} %extent.11, bf16[8,336,256]{2,1,0:T(8,128)(2,1)} %copy-done.6, bf16[3,4096,64]{2,1,0:T(8,128)(2,1)} %get-tuple-element.167.kept, f32[4096,128]{1,0:T(8,128)} %get-tuple-element.168.saved, ...), custom_call_target="tpu_custom_call" | custom-call | flops 42949672960 | bytes 12582912 | tf_op jit(solution)/shard_map/attention_backward/pallas_call | solution.py:596
  529.0 8.1 %collect.3 = (f32[2,672,768]{2,1,0:T(8,128)}, f32[8,768]{1,0:T(8,128)}, bf16[8,24,768]{2,1,0:T(8,128)(2,1)}, bf16[8,24,768]{2,1,0:T(8,128)(2,1)}, bf16[8,24,768]...) custom-call(s32[1]{0:T(128)} %bitcast.4.own, bf16[8,336,384]{2,1,0:T(8,128)(2,1)} %all-to-all-done.7.arrived, ...), custom_call_target="tpu_custom_call" | custom-call | flops 8000000000 | bytes 20971520 | tf_op jit(solution)/shard_map/collect/pallas_call | solution.py:876
  541.1 8.7 %collect.4 = (f32[2,672,768]{2,1,0:T(8,128)}, f32[8,768]{1,0:T(8,128)}, bf16[8,24,768]{2,1,0:T(8,128)(2,1)}, bf16[8,24,768]{2,1,0:T(8,128)(2,1)}, bf16[8,24,768]...) custom-call(s32[1]{0:T(128)} %bitcast.4.own, bf16[8,336,384]{2,1,0:T(8,128)(2,1)} %all-to-all-done.8.arrived, ...), custom_call_target="tpu_custom_call" | custom-call | flops 8000000000 | bytes 20971520 | tf_op jit(solution)/shard_map/collect/pallas_call | solution.py:876
  554.7 22.6 %all-gather.4 = f32[4,30,768]{2,1,0:T(8,128)S(1)} all-gather(f32[1,30,768]{2,1,0:T(8,128)S(1)} %bitcast.46), channel_id=3, replica_groups=mesh['dp'=4,'wide'=8] {'dp'}, dimensions={0}, use_global_device_ids=true | all-gather | bytes 460800 | tf_op jit(solution)/shard_map/all_gather | solution.py:1043
  577.4 7.0 %leave.2 = bf16[7,196,768]{2,1,0:T(8,128)(2,1)} custom-call(s32[50]{0:T(128)} %places.19, s32[1]{0:T(128)} %bitcast.me, f32[2,672,768]{2,1,0:T(8,128)} %bitcast.43), custom_call_target="tpu_custom_call" | custom-call | flops 1048576 | bytes 12582912 | tf_op jit(solution)/shard_map/leave/pallas_call | solution.py:262
  587.1 12.0 %collect.5 = (f32[2,672,768]{2,1,0:T(8,128)}, f32[8,2304]{1,0:T(8,128)}, bf16[8,24,768]{2,1,0:T(8,128)(2,1)}, bf16[8,24,768]{2,1,0:T(8,128)(2,1)}, bf16[8,24,768...) custom-call(s32[1]{0:T(128)} %bitcast.4.own, bf16[8,336,384]{2,1,0:T(8,128)(2,1)} %all-to-all-done.9.arrived, ...), custom_call_target="tpu_custom_call" | custom-call | flops 8000000000 | bytes 20971520 | tf_op jit(solution)/shard_map/collect/pallas_call | solution.py:876
  609.6 24.0 %all-gather.5 = f32[8,34,768]{2,1,0:T(8,128)} all-gather(f32[1,34,768]{2,1,0:T(8,128)S(1)} %maximum_bitcast_fusion.1), channel_id=4, replica_groups=mesh['dp'=4,'wide'=8] {'wide'}, dimensions={0}, use_global_device_ids=true | all-gather | bytes 940032 | tf_op jit(solution)/shard_map/all_gather | solution.py:1063
  652.5 7.5 %leave.3 = f32[7,196,768]{2,1,0:T(8,128)} custom-call(s32[50]{0:T(128)} %places.19, s32[1]{0:T(128)} %bitcast.me, f32[2,672,768]{2,1,0:T(8,128)} %get-tuple-element.211.values), custom_call_target="tpu_custom_call" | custom-call | flops 1048576 | bytes 12582912 | tf_op jit(solution)/shard_map/leave/pallas_call | solution.py:262
  662.7 14.1 %all-gather.6 = f32[4,76,768]{2,1,0:T(8,128)S(1)} all-gather(f32[1,76,768]{2,1,0:T(8,128)S(1)} %maximum_bitcast_fusion), channel_id=5, replica_groups=mesh['dp'=4,'wide'=8] {'dp'}, dimensions={0}, use_global_device_ids=true | all-gather | bytes 1167360 | tf_op jit(solution)/shard_map/all_gather | solution.py:1072
  (167 shorter events, 106.8 us)
Async XLA Ops:
  18.2 54.7 %all-to-all-start = ((bf16[8,336,384]{2,1,0:T(8,128)(2,1)}), bf16[8,336,384]{2,1,0:T(8,128)(2,1)S(1)}, u32[]{:S(2)}, u32[]{:S(2)}) async-start(bf16[8,336,384]{2,1,0:T(8,128)(2,1)} %get-tuple-element.119), calls=%async_computation | async-start | bytes 4128768 | tf_op jit(solution)/shard_map/all_to_all | solution.py:903
  72.9 53.4 %all-to-all-start.1 = ((bf16[8,336,384]{2,1,0:T(8,128)(2,1)}), bf16[8,336,384]{2,1,0:T(8,128)(2,1)}, u32[]{:S(2)}, u32[]{:S(2)}) async-start(bf16[8,336,384]{2,1,0:T(8,128)(2,1)} %get-tuple-element.120), calls=%async_computation.1 | async-start | bytes 4128768 | tf_op jit(solution)/shard_map/all_to_all | solution.py:903
  126.2 52.1 %all-to-all-start.2 = ((bf16[8,336,384]{2,1,0:T(8,128)(2,1)}), bf16[8,336,384]{2,1,0:T(8,128)(2,1)S(1)}, u32[]{:S(2)}, u32[]{:S(2)}) async-start(bf16[8,336,384]{2,1,0:T(8,128)(2,1)} %get-tuple-element.127), calls=%async_computation.2 | async-start | bytes 4128768 | tf_op jit(solution)/shard_map/all_to_all | solution.py:903
  178.3 37.5 %all-to-all-start.3 = ((bf16[8,336,256]{2,1,0:T(8,128)(2,1)}), bf16[8,336,256]{2,1,0:T(8,128)(2,1)S(1)}, u32[]{:S(2)}, u32[]{:S(2)}) async-start(bf16[8,336,256]{2,1,0:T(8,128)(2,1)} %get-tuple-element.130), calls=%async_computation.3 | async-start | bytes 2752512 | tf_op jit(solution)/shard_map/all_to_all | solution.py:903
  285.7 34.5 %all-to-all-start.5 = ((bf16[8,336,128]{2,1,0:T(8,128)(2,1)}), bf16[8,336,128]{2,1,0:T(8,128)(2,1)S(1)}, u32[]{:S(2)}, u32[]{:S(2)}) async-start(bf16[8,336,128]{2,1,0:T(8,128)(2,1)} %get-tuple-element.145), calls=%async_computation.5 | async-start | bytes 1376256 | tf_op jit(solution)/shard_map/all_to_all | solution.py:903
  320.2 67.4 %all-to-all-start.6 = ((bf16[8,336,256]{2,1,0:T(8,128)(2,1)}), bf16[8,336,256]{2,1,0:T(8,128)(2,1)S(1)}, u32[]{:S(2)}, u32[]{:S(2)}) async-start(bf16[8,336,256]{2,1,0:T(8,128)(2,1)} %get-tuple-element.150), calls=%async_computation.6 | async-start | bytes 2752512 | tf_op jit(solution)/shard_map/all_to_all | solution.py:903
  325.2 130.7 %collective-permute-start = (bf16[8,216,768]{2,1,0:T(8,128)(2,1)}, bf16[8,216,768]{2,1,0:T(8,128)(2,1)}, u32[]{:S(2)}, u32[]{:S(2)}) collective-permute-start(bf16[8,216,768]{2,1,0:T(8,128)(2,1)} %get-tuple-element.155), channel_id=1, source_target_pairs={{0,8},{8,16},{16,24},{24,0},{1,9},{9,17},{17,25},{25,1},{2,10},{10... | collective-permute-start | bytes 7962632 | tf_op jit(solution)/shard_map/ppermute | solution.py:916
  326.8 129.1 %collective-permute-start.1 = (bf16[8,216,768]{2,1,0:T(8,128)(2,1)}, bf16[8,216,768]{2,1,0:T(8,128)(2,1)}, u32[]{:S(2)}, u32[]{:S(2)}) collective-permute-start(bf16[8,216,768]{2,1,0:T(8,128)(2,1)} %get-tuple-element.156), channel_id=1, source_target_pairs={{0,16},{8,24},{16,0},{24,8},{1,17},{9,25},{17,1},{25,9},{2,18},{10... | collective-permute-start | bytes 7962632 | tf_op jit(solution)/shard_map/ppermute | solution.py:916
  328.2 127.7 %collective-permute-start.2 = (bf16[8,216,768]{2,1,0:T(8,128)(2,1)}, bf16[8,216,768]{2,1,0:T(8,128)(2,1)}, u32[]{:S(2)}, u32[]{:S(2)}) collective-permute-start(bf16[8,216,768]{2,1,0:T(8,128)(2,1)} %get-tuple-element.157), channel_id=1, source_target_pairs={{0,24},{8,0},{16,8},{24,16},{1,25},{9,1},{17,9},{25,17},{2,26},{10... | collective-permute-start | bytes 7962632 | tf_op jit(solution)/shard_map/ppermute | solution.py:916
  387.7 62.8 %all-to-all-start.7 = ((bf16[8,336,384]{2,1,0:T(8,128)(2,1)}), bf16[8,336,384]{2,1,0:T(8,128)(2,1)}, u32[]{:S(2)}, u32[]{:S(2)}) async-start(bf16[8,336,384]{2,1,0:T(8,128)(2,1)} %get-tuple-element.152), calls=%async_computation.7 | async-start | bytes 4128768 | tf_op jit(solution)/shard_map/all_to_all | solution.py:903
  450.5 74.1 %all-to-all-start.8 = ((bf16[8,336,384]{2,1,0:T(8,128)(2,1)}), bf16[8,336,384]{2,1,0:T(8,128)(2,1)}, u32[]{:S(2)}, u32[]{:S(2)}) async-start(bf16[8,336,384]{2,1,0:T(8,128)(2,1)} %get-tuple-element.161), calls=%async_computation.8 | async-start | bytes 4128768 | tf_op jit(solution)/shard_map/all_to_all | solution.py:903
  455.9 85.1 %reduce-scatter.2.cloned.1.call-start = ((), (), s32[]{:S(2)}) async-start(), calls=%async_computation.13 | async-start | bytes 2985984 | tf_op jit(solution)/shard_map/reduce_scatter | solution.py:1035
  524.6 62.5 %all-to-all-start.9 = ((bf16[8,336,384]{2,1,0:T(8,128)(2,1)}), bf16[8,336,384]{2,1,0:T(8,128)(2,1)}, u32[]{:S(2)}, u32[]{:S(2)}) async-start(bf16[8,336,384]{2,1,0:T(8,128)(2,1)} %get-tuple-element.170), calls=%async_computation.9 | async-start | bytes 4128768 | tf_op jit(solution)/shard_map/all_to_all | solution.py:903
  528.9 56.6 %all-gather.9.cloned.1.call-start = ((), (), s32[]{:S(2)}) async-start(), calls=%async_computation.14 | async-start | bytes 1658880 | tf_op jit(solution)/shard_map/all_gather | solution.py:1037
  538.1 47.1 %collective-permute-start.4 = (bf16[8,24,768]{2,1,0:T(8,128)(2,1)}, bf16[8,24,768]{2,1,0:T(8,128)(2,1)S(1)}, u32[]{:S(2)}, u32[]{:S(2)}) collective-permute-start(bf16[8,24,768]{2,1,0:T(8,128)(2,1)} %get-tuple-element.181), channel_id=1, source_target_pairs={{0,16},{8,24},{16,0},{24,8},{1,17},{9,25},{17,1},{25,9},{2,18},{10... | collective-permute-start | bytes 884744 | tf_op jit(solution)/shard_map/ppermute | solution.py:916
  538.6 46.6 %collective-permute-start.5 = (bf16[8,24,768]{2,1,0:T(8,128)(2,1)}, bf16[8,24,768]{2,1,0:T(8,128)(2,1)S(1)}, u32[]{:S(2)}, u32[]{:S(2)}) collective-permute-start(bf16[8,24,768]{2,1,0:T(8,128)(2,1)} %get-tuple-element.182), channel_id=1, source_target_pairs={{0,24},{8,0},{16,8},{24,16},{1,25},{9,1},{17,9},{25,17},{2,26},{10... | collective-permute-start | bytes 884744 | tf_op jit(solution)/shard_map/ppermute | solution.py:916
  549.8 35.3 %collective-permute-start.6 = (bf16[8,24,768]{2,1,0:T(8,128)(2,1)}, bf16[8,24,768]{2,1,0:T(8,128)(2,1)S(1)}, u32[]{:S(2)}, u32[]{:S(2)}) collective-permute-start(bf16[8,24,768]{2,1,0:T(8,128)(2,1)} %get-tuple-element.185), channel_id=1, source_target_pairs={{0,8},{8,16},{16,24},{24,0},{1,9},{9,17},{17,25},{25,1},{2,10},{10... | collective-permute-start | bytes 884744 | tf_op jit(solution)/shard_map/ppermute | solution.py:916
  549.9 35.3 %collective-permute-start.7 = (bf16[8,24,768]{2,1,0:T(8,128)(2,1)}, bf16[8,24,768]{2,1,0:T(8,128)(2,1)S(1)}, u32[]{:S(2)}, u32[]{:S(2)}) collective-permute-start(bf16[8,24,768]{2,1,0:T(8,128)(2,1)} %get-tuple-element.186), channel_id=1, source_target_pairs={{0,16},{8,24},{16,0},{24,8},{1,17},{9,25},{17,1},{25,9},{2,18},{10... | collective-permute-start | bytes 884744 | tf_op jit(solution)/shard_map/ppermute | solution.py:916
  551.2 34.0 %collective-permute-start.8 = (bf16[8,24,768]{2,1,0:T(8,128)(2,1)}, bf16[8,24,768]{2,1,0:T(8,128)(2,1)S(1)}, u32[]{:S(2)}, u32[]{:S(2)}) collective-permute-start(bf16[8,24,768]{2,1,0:T(8,128)(2,1)} %get-tuple-element.187), channel_id=1, source_target_pairs={{0,24},{8,0},{16,8},{24,16},{1,25},{9,1},{17,9},{25,17},{2,26},{10... | collective-permute-start | bytes 884744 | tf_op jit(solution)/shard_map/ppermute | solution.py:916
  601.5 35.6 %all-to-all-start.10 = ((bf16[8,24,1536]{2,1,0:T(8,128)(2,1)}), bf16[8,24,1536]{2,1,0:T(8,128)(2,1)S(1)}, u32[]{:S(2)}, u32[]{:S(2)}) async-start(bf16[8,24,1536]{2,1,0:T(8,128)(2,1)} %pad_maximum_fusion), calls=%async_computation.11 | async-start | bytes 1179648 | tf_op jit(solution)/shard_map/all_to_all | solution.py:903
  606.2 28.7 %collective-permute-start.10 = (bf16[8,24,768]{2,1,0:T(8,128)(2,1)}, bf16[8,24,768]{2,1,0:T(8,128)(2,1)}, u32[]{:S(2)}, u32[]{:S(2)}) collective-permute-start(bf16[8,24,768]{2,1,0:T(8,128)(2,1)} %get-tuple-element.201), channel_id=1, source_target_pairs={{0,16},{8,24},{16,0},{24,8},{1,17},{9,25},{17,1},{25,9},{2,18},{10... | collective-permute-start | bytes 884744 | tf_op jit(solution)/shard_map/ppermute | solution.py:916
  607.6 27.4 %collective-permute-start.11 = (bf16[8,24,768]{2,1,0:T(8,128)(2,1)}, bf16[8,24,768]{2,1,0:T(8,128)(2,1)}, u32[]{:S(2)}, u32[]{:S(2)}) collective-permute-start(bf16[8,24,768]{2,1,0:T(8,128)(2,1)} %get-tuple-element.202), channel_id=1, source_target_pairs={{0,24},{8,0},{16,8},{24,16},{1,25},{9,1},{17,9},{25,17},{2,26},{10... | collective-permute-start | bytes 884744 | tf_op jit(solution)/shard_map/ppermute | solution.py:916
  609.1 25.8 %collective-permute-start.9 = (bf16[8,24,768]{2,1,0:T(8,128)(2,1)}, bf16[8,24,768]{2,1,0:T(8,128)(2,1)}, u32[]{:S(2)}, u32[]{:S(2)}) collective-permute-start(bf16[8,24,768]{2,1,0:T(8,128)(2,1)} %get-tuple-element.200), channel_id=1, source_target_pairs={{0,8},{8,16},{16,24},{24,0},{1,9},{9,17},{17,25},{25,1},{2,10},{10... | collective-permute-start | bytes 884744 | tf_op jit(solution)/shard_map/ppermute | solution.py:916
  637.1 24.5 %all-to-all-start.11 = ((bf16[8,24,768]{2,1,0:T(8,128)(2,1)}), bf16[8,24,768]{2,1,0:T(8,128)(2,1)}, u32[]{:S(2)}, u32[]{:S(2)}) async-start(bf16[8,24,768]{2,1,0:T(8,128)(2,1)} %add_convert_fusion), calls=%async_computation.12 | async-start | bytes 589824 | tf_op jit(solution)/shard_map/all_to_all | solution.py:903
  (27 other events, 423.8 us)
Sparse Core Ops, SparseCore 0:
  462.3 64.8 reduce-scatter.1
  541.1 40.2 all-gather.8

commit v4 on v3

--- a/solution.py
+++ b/solution.py
@@ -57,7 +57,8 @@
         self.full = WINS // wide if self.corner else -(-WINS // wide)
         self.slots = self.full + int(self.corner)
         used = self.full * HALF + 32 * int(self.corner)
-        self.rows = max(-(-used // 16) * 16, self.start(self.full - 1) + 112)
+        self.rows = max(-(-used // 8) * 8, self.start(self.full - 1) + 112)
+        self.tail = self.rows - self.start(self.full)
         self.corner_at = self.full * HALF
 
     def start(self, m):
@@ -294,7 +295,7 @@
 
 
 def corner_matrix(plan, flip):
-    dims = (48, 256) if flip else (256, 48)
+    dims = (plan.tail, 256) if flip else (256, plan.tail)
     cell = lax.broadcasted_iota(jnp.int32, dims, 1 if flip else 0)
     item = lax.broadcasted_iota(jnp.int32, dims, 0 if flip else 1)
     row, col = (cell // GRID, cell % GRID)
@@ -325,7 +326,7 @@
         if last and plan.corner:
             source = ((WINS - 1) % plan.wide + turn) % plan.wide
             at = plan.start(plan.full)
-            extra = dot(corner_matrix(plan, False), arrived[source, at : at + 48, :])
+            extra = dot(corner_matrix(plan, False), arrived[source, at : at + plan.tail, :])
         for part in range(parts):
             top = found[:, part * 128 : part * 128 + HDIM]
             low = found[:, part * 128 + HDIM : (part + 1) * 128]
@@ -374,7 +375,7 @@
             made = dot(corner_matrix(plan, True), jnp.concatenate(lanes, axis=1)).astype(BF)
             dest = ((WINS - 1) % plan.wide + turn) % plan.wide
             at = plan.start(plan.full)
-            out[dest, at : at + 48, span] += made
+            out[dest, at : at + plan.tail, span] += made
 
 
 def split(x):
@@ -412,8 +413,10 @@
     ]
 
 
-def forward_kernel(plan, tile, slot_count, places, me, extent, arrived, table, *refs):
-    earlier, (send, kept, saved, kt, va, held) = (refs[:-6], refs[-6:])
+def forward_kernel(plan, tile, slot_count, keep, places, me, extent, arrived, table, *refs):
+    refs, (kt, va, held) = (refs[:-3], refs[-3:])
+    refs, probs = (refs[:-1], refs[-1]) if keep else (refs, None)
+    earlier, (send, kept, saved) = (refs[:-3], refs[-3:])
     step = pl.program_id(0)
     image = me[0] // GROUPS
     turn = plan.turn(places, slot_count, image)
@@ -439,20 +442,29 @@
     marks = query_marks(q, rows, cols)
     side = N // 2
     score = lambda c: dot(marks[c * KEYS // side], kt[:, c * KEYS : (c + 1) * KEYS])
-    total, top, now = (None, None, score(0))
+    total, top, now, tops = (None, None, score(0), [])
     for c in range(N // KEYS):
         following = score(c + 1) if c + 1 < N // KEYS else None
         higher = jnp.max(now, axis=1, keepdims=True)
         if c:
             higher = jnp.maximum(top, higher)
         weights = jnp.exp(now - higher).astype(BF)
+        tops.append(higher)
+        if keep:
+            probs[:, c * KEYS : (c + 1) * KEYS] = weights
         x = dot(weights, va[c * KEYS : (c + 1) * KEYS, :])
         total = total * jnp.exp(top - higher) + x if c else x
         top, now = (higher, following)
     mass = total[:, HDIM : HDIM + 1]
     out = total * (1.0 / mass)
     lane = lax.broadcasted_iota(jnp.int32, (tile, 128), 1)
-    saved[...] = jnp.where(lane < HDIM, out, top + jnp.log(mass))
+    level = top + jnp.log(mass)
+    if keep:
+        for c, higher in enumerate(tops):
+            out = jnp.where(lane == HDIM + c, jnp.exp(higher - level), out)
+        saved[...] = out
+    else:
+        saved[...] = jnp.where(lane < HDIM, out, level)
     held[here, :] = out[:, :HDIM].astype(BF)
 
     @pl.when(step == pl.num_programs(0) - 1)
@@ -463,16 +475,19 @@
             send[:, :, 128 * i : 128 * (i + 1)] = block[...]
 
 
-def attention_forward(plan, slot_count, places, me, extent, arrived, table, *earlier, tile=TILE):
+def attention_forward(
+    plan, slot_count, places, me, extent, arrived, table, *earlier, keep=False, tile=TILE
+):
     lanes = 128 * (1 + len(earlier))
     whole = lambda *dims: pl.BlockSpec(dims, lambda t, *_: (0,) * len(dims))
     return pl.pallas_call(
-        partial(forward_kernel, plan, tile, slot_count),
+        partial(forward_kernel, plan, tile, slot_count, keep),
         out_shape=(
             shape((plan.wide, plan.rows, lanes), BF),
             shape((3, N, HDIM), BF),
             shape((N, 128), F32),
-        ),
+        )
+        + (shape((N, N), BF),) * keep,
         grid_spec=pltpu.PrefetchScalarGridSpec(
             num_scalar_prefetch=3,
             grid=(N // tile,),
@@ -481,7 +496,8 @@
                 whole(plan.wide, plan.rows, lanes),
                 whole(3, N, HDIM),
                 pl.BlockSpec((tile, 128), lambda t, *_: (t, 0)),
-            ],
+            ]
+            + [pl.BlockSpec((tile, N), lambda t, *_: (t, 0))] * keep,
             scratch_shapes=[
                 pltpu.VMEM((256, N), BF),
                 pltpu.VMEM((N, 128), BF),
@@ -625,6 +641,129 @@
     )(places, me, extent, arrived, kept, saved, table, table_back)
 
 
+def replay_kernel(
+    plan, tile, slot_count, places, me,
+    arrived, kept, saved, probs, table_back,
+    send, rel_grad,
+    vt, ka, dout, dq, dk, dv,
+):
+    step = pl.program_id(0)
+    image = me[0] // GROUPS
+    turn = plan.turn(places, slot_count, image)
+
+    @pl.when(step == 0)
+    def _():
+        minus = lax.broadcasted_iota(jnp.int32, (HDIM, N), 0) < 2
+        vt[HDIM:, :] = jnp.where(minus, -1.0, 0.0).astype(BF)
+        key = lax.broadcasted_iota(jnp.int32, (N, 128), 0)
+        mark = lax.broadcasted_iota(jnp.int32, (N, 128), 1)
+        col = (GRID - 1 - mark) == key % GRID
+        row = (mark - GRID) == key // GRID
+        ka[:, HDIM:192] = jnp.where(mark < GRID, col.astype(F32), row.astype(F32)).astype(BF)
+        ka[:, 192:] = jnp.zeros((N, HDIM), BF)
+        rel_grad[...] = jnp.zeros_like(rel_grad)
+        dk[...] = jnp.zeros_like(dk)
+        dv[...] = jnp.zeros_like(dv)
+        ka[:, :HDIM] = (kept[1].astype(F32) * 0.125).astype(BF)
+        vt[:HDIM, :] = kept[2].astype(F32).T.astype(BF)
+
+        def store(part, first, values):
+            dout[first : first + values.shape[0], :] = values.astype(BF)
+
+        grid_rows(plan, turn, arrived, 1, store)
+
+    here = pl.ds(pl.multiple_of(step * tile, tile), tile)
+    q = kept[0, here, :]
+    do = dout[here, :].astype(F32)
+    old = saved[...]
+    count = tile // GRID
+    inner = jnp.sum(do * old[:, :HDIM], axis=1, keepdims=True)
+    lane = lax.broadcasted_iota(jnp.int32, (tile, HDIM), 1)
+    q_turned = (q.astype(F32) * 0.125).T.astype(BF)
+    do_turned = do.T
+    factors = old[:, HDIM:].T
+
+    def products(c):
+        part = slice(c * KEYS, (c + 1) * KEYS)
+        factor = old[:, HDIM + c : HDIM + c + 1]
+        high, low = split(inner * factor)
+        less = jnp.where(lane == 0, high.astype(F32), jnp.where(lane == 1, low.astype(F32), 0.0))
+        do_less = jnp.concatenate([(do * factor).astype(BF), less.astype(BF)], 1)
+        return dot(do_less, vt[:, part])
+
+    back, now = (None, products(0))
+    for c in range(N // KEYS):
+        part = slice(c * KEYS, (c + 1) * KEYS)
+        following = products(c + 1) if c + 1 < N // KEYS else None
+        weights = probs[:, part]
+        dscore = (weights.astype(F32) * now).astype(BF)
+        dv[:, part] += dot((do_turned * factors[c : c + 1, :]).astype(BF), weights)
+        dk[:, part] += dot(q_turned, dscore)
+        x = dot(dscore, ka[part, :])
+        back = x if back is None else back + x
+        now = following
+    blank = jnp.zeros((GRID, HDIM), F32)
+    offsets = []
+    for i in range(count):
+        own = slice(i * GRID, (i + 1) * GRID)
+        row_part = jnp.concatenate([back[own, 128:192], blank], 1)
+        col_part = jnp.concatenate([back[own, HDIM:128], blank], 1)
+        row_part = pltpu.roll(row_part, (2 * GRID - 1 + GRID - step * count - i) % 128, 1)
+        col_part = pltpu.roll(col_part, 0, 1, stride=1, stride_axis=0)
+        offsets.append(jnp.concatenate([row_part, col_part], 1))
+    high, low = split(jnp.concatenate(offsets, 0))
+    rel = table_back[...]
+    both = dot(jnp.concatenate([high, low], 1), jnp.concatenate([rel, rel], 0))
+    dq[here, :] = (back[:, :HDIM] + both).astype(BF)
+    q_whole = q.astype(F32).T.astype(BF)
+    rel_grad[...] += dot(q_whole, high) + dot(q_whole, low)
+
+    @pl.when(step == pl.num_programs(0) - 1)
+    def _():
+        def load(part, first, size):
+            if part == 0:
+                return dq[first : first + size, :]
+            return turned[part - 1][first : first + size, :]
+
+        turned = (dk[...].T.astype(BF), dv[...].T.astype(BF))
+        scatter_grid(plan, turn, send, 3, load)
+
+
+def attention_replay(
+    plan, slot_count, places, me, arrived, lane, kept, saved, probs, table_back, tile=TILE
+):
+    whole = lambda *dims: pl.BlockSpec(dims, lambda t, *_: (0,) * len(dims))
+    return pl.pallas_call(
+        partial(replay_kernel, plan, tile, slot_count),
+        out_shape=(shape((plan.wide, plan.rows, 384), BF), shape((HDIM, 256), F32)),
+        grid_spec=pltpu.PrefetchScalarGridSpec(
+            num_scalar_prefetch=2,
+            grid=(N // tile,),
+            in_specs=[
+                pl.BlockSpec((plan.wide, plan.rows, 128), lambda t, *_: (0, 0, lane)),
+                whole(3, N, HDIM),
+                pl.BlockSpec((tile, 128), lambda t, *_: (t, 0)),
+                pl.BlockSpec((tile, N), lambda t, *_: (t, 0)),
+                whole(*table_back.shape),
+            ],
+            out_specs=[whole(plan.wide, plan.rows, 384), whole(HDIM, 256)],
+            scratch_shapes=[
+                pltpu.VMEM((128, N), BF),
+                pltpu.VMEM((N, 256), BF),
+                pltpu.VMEM((N, HDIM), BF),
+                pltpu.VMEM((N, HDIM), BF),
+                pltpu.VMEM((HDIM, N), F32),
+                pltpu.VMEM((HDIM, N), F32),
+            ],
+        ),
+        compiler_params=params(),
+        cost_estimate=pl.CostEstimate(
+            flops=10 * N * N * 256, bytes_accessed=44 << 20, transcendentals=0
+        ),
+        name="attention_replay",
+    )(places, me, arrived, kept, saved, probs, table_back)
+
+
 def middle_kernel(
     plan, first, last, x, g, out_weight, fc1_weight, fc2_weight,
     out_bias, fc1_bias, fc2_bias, gain, shift,
@@ -656,18 +795,26 @@
     grad = g[0]
     total, grad_normed = (None, None)
     add = lambda old, new: new if old is None else old + new
+
+    def products(c):
+        span = slice(c * D, (c + 1) * D)
+        return (dot(n, fc1_weight[:, span]), dot_t(grad, fc2_weight[span, :]))
+
+    now = products(0)
     for c in range(4):
         span = slice(c * D, (c + 1) * D)
-        before = dot(n, fc1_weight[:, span]) + fc1_bias[:, span]
+        following = products(c + 1) if c < 3 else None
+        before = now[0] + fc1_bias[:, span]
         share = 0.5 + 0.5 * lax.erf(before * (0.5**0.5))
         low = (before * share).astype(BF)
         act[0, :, span] = low
         slope = share + before * (jnp.exp(before * before * -0.5) * 0.3989422804014327)
-        back = (dot_t(grad, fc2_weight[span, :]) * slope).astype(BF)
+        back = (now[1] * slope).astype(BF)
         grad_before[0, :, span] = back
         sums[:, (3 + c) * D : (4 + c) * D] += jnp.sum(back.astype(F32), axis=0, keepdims=True)
         total = add(total, dot(low, fc2_weight[span, :]))
         grad_normed = add(grad_normed, dot_t(back, fc1_weight[:, span]))
+        now = following
     result[0] = middle + total + fc2_bias[...]
     full = grad.astype(F32) + norm_back(grad_normed * gain[...], scaled, spread)
     grad_middle[0] = full
@@ -826,20 +973,20 @@
         held[...] = jnp.zeros_like(held)
         bias_grad[...] = jnp.zeros_like(bias_grad)
 
-    n = normed[0]
-    whole = before[0] if chunk > 0 else None
-    for p, weight in enumerate((wq, wk, wv)):
-        halves = []
-        for half in range(2):
-            at = p * 128 + half * HDIM
-            lanes = [arrived[g, :, at : at + HDIM] for g in range(GROUPS)]
-            halves.append(jnp.concatenate(lanes, axis=1))
-        y = jnp.concatenate(halves, axis=0)
-        made = dot_t(y, weight[...])
-        whole = made if whole is None else whole + made
-        span = slice(p * 256, (p + 1) * 256)
-        held[:, span] += t_dot(n, y)
-        bias_grad[0:1, span] += jnp.sum(y.astype(F32), axis=0, keepdims=True)
+    halves = []
+    for half in range(2):
+        lanes = [
+            arrived[g, :, p * 128 + half * HDIM : p * 128 + (half + 1) * HDIM]
+            for p in range(3)
+            for g in range(GROUPS)
+        ]
+        halves.append(jnp.concatenate(lanes, axis=1))
+    y = jnp.concatenate(halves, axis=0)
+    held[...] += t_dot(normed[0], y)
+    bias_grad[0:1, :D] += jnp.sum(y.astype(F32), axis=0, keepdims=True)
+    whole = dot_t(y, jnp.concatenate([wq[...], wk[...], wv[...]], axis=1))
+    if chunk > 0:
+        whole = whole + before[0]
     if chunk == CHUNKS - 1:
         scaled, spread = norm_rows(x[0].astype(F32))
         total[0] = middle_grad[0] + norm_back(whole * gain[...], scaled, spread)
@@ -970,7 +1117,8 @@
         earlier = (forward[0][0],) if h == 1 else ()
         forward.append(
             attention_forward(
-                plan, slots, window_place, me, image_extent, arrived, table, *earlier
+                plan, slots, window_place, me, image_extent, arrived, table, *earlier,
+                keep=h < CHUNKS - 1,
             )
         )
         arrived = following
@@ -1020,10 +1168,16 @@
             *shares, _ = lax.optimization_barrier((*shares, send))
             shares = add_groups(shares)
             grad_arrived, shares = lax.optimization_barrier((grad_arrived, shares))
-        send, rel_grad = attention_backward(
-            plan, slots, window_place, me, image_extent, grad_arrived, max(h - 1, 0),
-            forward[h][1], forward[h][2], table, table_back,
-        )
+        lane = max(h - 1, 0)
+        if h < CHUNKS - 1:
+            send, rel_grad = attention_replay(
+                plan, slots, window_place, me, grad_arrived, lane, *forward[h][1:], table_back
+            )
+        else:
+            send, rel_grad = attention_backward(
+                plan, slots, window_place, me, image_extent, grad_arrived, lane,
+                forward[h][1], forward[h][2], table, table_back,
+            )
         if h == 0:
             send, grad_arrived = lax.optimization_barrier((send, following))
         rel_total = rel_grad if h == 0 else rel_total + rel_grad
@@ -1040,7 +1194,6 @@
         plan, window_place, me, result.reshape(plan.images, 2 * plan.rows, D), slots, BF
     )
     mid = jnp.concatenate([early, rel_total.reshape(-1), jnp.zeros((512,), F32)]).reshape(-1, D)
-    mid = jnp.sum(lax.all_gather(tie(mid, send), "dp", axis=0, tiled=False), axis=0)
     fold = lambda v: v.reshape(plan.images, 2 * plan.rows, D)
     around = lambda b: over_groups(b if aligned else turn_groups(share_rows(b[0], wide, groups)))
     gather = partial(collect, plan)
@@ -1051,7 +1204,7 @@
     got1 = around(blocks)
     *got, _ = lax.optimization_barrier((*got0, *got1, tokens_out))
     ready = [add_groups(got[:groups]).astype(BF), add_groups(got[groups:]).astype(BF)]
-    arrived, shares, mid, *ready = lax.optimization_barrier((grad_qkv[2], shares, mid, *ready))
+    arrived, shares, *ready = lax.optimization_barrier((grad_qkv[2], shares, *ready))
     early_sums = exchange(jnp.concatenate(ready, axis=2))
     totals, sums2, blocks = gather(
         2, *fixed, arrived, normed1, qkv_weight, totals, fold(grad_middle), x, wide_f(norm1_gain)
@@ -1059,21 +1212,22 @@
     weight_grad = add_groups(around(blocks)).astype(BF)
     third = [c[:D].reshape(3, 256) for c in (sums0, sums1, sums2)]
     late = jnp.concatenate([sums2[D:]] + [t[0] for t in third] + [t[2] for t in third])
+    weight_grad, early_sums, late, totals, shares = lax.optimization_barrier(
+        (weight_grad, early_sums, late, totals, shares)
+    )
+    last = exchange(weight_grad)
     small = jnp.concatenate([late.reshape(-1, D), mid], axis=0)
     small = jnp.sum(lax.all_gather(small, "wide", axis=0, tiled=False), axis=0)
-    weight_grad, early_sums, small, totals, shares = lax.optimization_barrier(
-        (weight_grad, early_sums, small, totals, shares)
-    )
-    last = exchange(weight_grad)
     share = D // wide
     piece = share // groups
     weight_sums = jnp.concatenate([add_wide(early_sums), add_wide(last)], axis=1)
-    last = jnp.concatenate([weight_sums.reshape(-1, D), small[:4]], axis=0)
+    last = jnp.concatenate([weight_sums.reshape(-1, D), small], axis=0)
+    totals, shares, last = lax.optimization_barrier((totals, shares, last))
     last = lax.all_gather(last, "dp", axis=0, tiled=False)
     qkv_weight_grad = last[:, : 3 * piece].reshape(share, CHUNKS, 3, 256)
     qkv_weight_grad = qkv_weight_grad.transpose(0, 2, 1, 3).reshape(share, 3 * D)
-    late = jnp.sum(last[:, 3 * piece :], axis=0).reshape(-1)
-    sums = small[4:].reshape(-1)
+    sums = jnp.sum(last[:, 3 * piece :], axis=0).reshape(-1)
+    late, sums = (sums[: 4 * D], sums[4 * D :])
     tokens_grad = leave(plan, window_place, me, totals, slots, F32)
     rel_total = sums[8 * D : 8 * D + HDIM * 256].reshape(HDIM, 256).T
     small = sums[: 8 * D]

time: 693 us -> 679 us (0.980)
  blocking collectives: 60.8 us -> 20.3 us
  waiting for transfers between devices: 94.8 us -> 107 us
  local copies, waits for them, and re-layouts: 24.8 us -> 35.3 us
    pallas_call x3 -> x5, Pallas kernels: 93.3 us -> 212 us  [the longest x3 109 us: attention_forward(): pl.pallas_call(partial(forward_kernel, plan, tile, slot_count, keep), out...]
    pallas_call x3 -> x1, Pallas kernels: 174 us -> 58 us  [attention_backward(): pl.pallas_call(partial(backward_kernel, plan, tile, slot_count), out_shap...]
    all_gather x2 -> x0, blocking collectives: 36.8 us -> none  [the longest x1 22.6 us: shards(): lax.all_gather(tie(mid, send), 'dp', axis=0, tiled=False)]
    all_to_all x12, waiting for transfers between devices: 94.7 us -> 74.1 us  [exchange(): return lax.all_to_all(blocks, axis, split_axis=0, concat_axis=0, tiled=True)]
    all_gather x0 -> x1, waiting for transfers between devices: none -> 13.9 us  [shards(): last = lax.all_gather(last, 'dp', axis=0, tiled=False)]
    all_gather x1, waiting for transfers between devices: 0.02 us -> 9.54 us  [shards(): shares = lax.all_gather(shares, 'dp', axis=0, tiled=False).astype(F32)]
    unnamed x60 -> x54, local copies, waits for them, and re-layouts: 2.67 us -> 11.7 us
    ppermute x12, waiting for transfers between devices: 0.03 us -> 9.01 us  [over_groups(): got.append(lax.ppermute(blocks[d], 'dp', pairs))]
  transfers between devices with their start and end apart: 26 -> 27, of which waited for: 6 -> 11; matrix products, arithmetic and copies ran while one was open for 4% -> 5% of each run, Pallas kernels for 49% -> 51%
where the time goes in v4:
time: 679 us; the launch traced here: 673 us
  Pallas kernels  406 us (60%)
  waiting for transfers between devices  107 us (16%)
  starting transfers between devices  71.6 us (11%)
  local copies, waits for them, and re-layouts  35.3 us (5%)
  blocking collectives  20.3 us (3%)
  other arithmetic  18.9 us (3%)
  between operations  14.7 us (2%)
    pallas_call x3, Pallas kernels, attention_forward(): pl.pallas_call(partial(forward_kernel, plan, tile, slot_count, keep), out...  109 us
    pallas_call x2, Pallas kernels, attention_replay(): pl.pallas_call(partial(replay_kernel, plan, tile, slot_count), out_shape=...  103 us
    all_to_all x12, waiting for transfers between devices, exchange(): return lax.all_to_all(blocks, axis, split_axis=0, concat_axis=0, tiled=True)  74.1 us
    pallas_call x1, Pallas kernels, attention_backward(): pl.pallas_call(partial(backward_kernel, plan, tile, slot_count), out_shap...  58 us
    all_to_all x12, starting transfers between devices, exchange(): return lax.all_to_all(blocks, axis, split_axis=0, concat_axis=0, tiled=True)  55.6 us
    pallas_call x1, Pallas kernels, middle_part(): pl.pallas_call(partial(middle_kernel, plan), out_shape=(made(D, BF), made...  45.6 us
    pallas_call x1, Pallas kernels, weight_shares(): pl.pallas_call(partial(shares_kernel, plan, groups), out_shape=[shape(blo...  30.8 us
    pallas_call x3, Pallas kernels, collect(): pl.pallas_call(partial(collect_kernel, plan, chunk, groups, None), out_sh...  28.9 us
  transfers between devices with their start and end apart: 27, of which 11 were waited for; matrix products, arithmetic and copies ran while one was open for 5% of the time, Pallas kernels for 51%

profile of v4, /device:TPU:0, one launch (start us, length us, event | category | flops | bytes accessed | tf_op | source)
XLA Modules:
  0.0 672.8 jit_solution(17095600791981250705)
XLA Ops:
  11.1 7.0 %enter.1 = (bf16[2,656,768]{2,1,0:T(8,128)(2,1)}, bf16[2,656,768]{2,1,0:T(8,128)(2,1)}, bf16[8,328,384]{2,1,0:T(8,128)(2,1)}) custom-call(s32[50]{0:T(128)} %places.19, s32[1]{0:T(128)} %bitcast.me, bf16[7,196,768]{2,1,0:T(8,128)(2,1)} %refs_3_.2, bf16[7,196,768]{2,1,0:T(8,128)(2,1)} %refs_3_.2, bf16[7,196,768]{2,1,0:T(8,128)(2,1)} %refs_3_.2, ...), custom_call_target="tpu_custom_call" | custom-call | flops 2000000000 | bytes 10485760 | tf_op jit(solution)/shard_map/enter/pallas_call | solution.py:186
  18.1 6.3 all-to-all-start
  24.4 9.1 %follow.1 = (bf16[2,656,768]{2,1,0:T(8,128)(2,1)}, bf16[8,328,384]{2,1,0:T(8,128)(2,1)}, bf16[8,328,384]{2,1,0:T(8,128)(2,1)}) custom-call(s32[50]{0:T(128)} %places.19, s32[1]{0:T(128)} %bitcast.me, bf16[7,196,768]{2,1,0:T(8,128)(2,1)} %refs_3_.3, bf16[7,196,768]{2,1,0:T(8,128)(2,1)} %refs_3_.3, bf16[7,196,768]{2,1,0:T(8,128)(2,1)} %refs_3_.3, ...), custom_call_target="tpu_custom_call" | custom-call | flops 4000000000 | bytes 16777216 | tf_op jit(solution)/shard_map/follow/pallas_call | solution.py:209
  33.6 38.2 %all-to-all-done.arrived = bf16[8,328,384]{2,1,0:T(8,128)(2,1)S(1)} async-done(((bf16[8,328,384]{2,1,0:T(8,128)(2,1)}), bf16[8,328,384]{2,1,0:T(8,128)(2,1)S(1)}, u32[]{:S(2)}, u32[]{:S(2)}) %all-to-all-start) | async-done | bytes 2015264 | tf_op jit(solution)/shard_map/all_to_all | solution.py:1050
  77.9 38.7 %attention_forward.3 = (bf16[8,328,128]{2,1,0:T(8,128)(2,1)}, bf16[3,4096,64]{2,1,0:T(8,128)(2,1)}, f32[4096,128]{1,0:T(8,128)}, bf16[4096,4096]{1,0:T(8,128)(2,1)}) custom-call(s32[50]{0:T(128)} %places.19, s32[1]{0:T(128)} %bitcast.me, s32[2,2]{1,0:T(2,128)} %extent.7, bf16[8,328,384]{2,1,0:T(8,128)(2,1)} %copy-done.3, ...), custom_call_target="tpu_custom_call" | custom-call | flops 17179869184 | bytes 12582912 | tf_op jit(solution)/shard_map/attention_forward/pallas_call | solution.py:483
  116.7 7.4 %all-to-all-done.1.arrived = bf16[8,328,384]{2,1,0:T(8,128)(2,1)S(1)} async-done(((bf16[8,328,384]{2,1,0:T(8,128)(2,1)}), bf16[8,328,384]{2,1,0:T(8,128)(2,1)S(1)}, u32[]{:S(2)}, u32[]{:S(2)}) %all-to-all-start.1) | async-done | bytes 2015264 | tf_op jit(solution)/shard_map/all_to_all | solution.py:1050
  128.8 39.2 %attention_forward.4 = (bf16[8,328,256]{2,1,0:T(8,128)(2,1)}, bf16[3,4096,64]{2,1,0:T(8,128)(2,1)}, f32[4096,128]{1,0:T(8,128)}, bf16[4096,4096]{1,0:T(8,128)(2,1)}) custom-call(s32[50]{0:T(128)} %places.19, s32[1]{0:T(128)} %bitcast.me, s32[2,2]{1,0:T(2,128)} %extent.7, bf16[8,328,384]{2,1,0:T(8,128)(2,1)} %copy-done.2, ...), custom_call_target="tpu_custom_call" | custom-call | flops 17179869184 | bytes 12582912 | tf_op jit(solution)/shard_map/attention_forward/pallas_call | solution.py:483
  168.1 8.1 %all-to-all-done.2.arrived = bf16[8,328,384]{2,1,0:T(8,128)(2,1)} async-done(((bf16[8,328,384]{2,1,0:T(8,128)(2,1)}), bf16[8,328,384]{2,1,0:T(8,128)(2,1)}, u32[]{:S(2)}, u32[]{:S(2)}) %all-to-all-start.2) | async-done | bytes 2015264 | tf_op jit(solution)/shard_map/all_to_all | solution.py:1050
  180.0 31.0 %attention_forward.5 = (bf16[8,328,128]{2,1,0:T(8,128)(2,1)}, bf16[3,4096,64]{2,1,0:T(8,128)(2,1)}, f32[4096,128]{1,0:T(8,128)}) custom-call(s32[50]{0:T(128)} %places.19, s32[1]{0:T(128)} %bitcast.me, s32[2,2]{1,0:T(2,128)} %extent.7, bf16[8,328,384]{2,1,0:T(8,128)(2,1)} %all-to-all-done.2.arrived, bf16[256,64]{1,0:T(8,128)(2,1)} %get-tuple-element.283.table), custom_call_target="tpu_custom_call" | custom-call | flops 17179869184 | bytes 12582912 | tf_op jit(solution)/shard_map/attention_forward/pallas_call | solution.py:483
  219.4 15.5 %all-to-all-done.4.last = bf16[8,328,128]{2,1,0:T(8,128)(2,1)S(1)} async-done(((bf16[8,328,128]{2,1,0:T(8,128)(2,1)}), bf16[8,328,128]{2,1,0:T(8,128)(2,1)S(1)}, u32[]{:S(2)}, u32[]{:S(2)}) %all-to-all-start.4) | async-done | bytes 671776 | tf_op jit(solution)/shard_map/all_to_all | solution.py:1050
  235.8 45.6 %middle.1 = (bf16[4,328,768]{2,1,0:T(8,128)(2,1)}, bf16[4,328,768]{2,1,0:T(8,128)(2,1)}, bf16[4,328,3072]{2,1,0:T(8,128)(2,1)}, bf16[4,328,3072]{2,1,0:T(8,128)(...) custom-call(bf16[8,328,256]{2,1,0:T(8,128)(2,1)} %copy-done.5, ...), custom_call_target="tpu_custom_call" | custom-call | flops 30000001024 | bytes 41943040 | tf_op jit(solution)/shard_map/middle/pallas_call | solution.py:849
  285.3 30.8 %weight_shares.1 = (bf16[8,216,768]{2,1,0:T(8,128)(2,1)}, bf16[8,216,768]{2,1,0:T(8,128)(2,1)}, bf16[8,216,768]{2,1,0:T(8,128)(2,1)}, bf16[8,216,768]{2,1,0:T(8,128)(2,1)}) custom-call(s32[1]{0:T(128)} %bitcast.4.own, bf16[2,656,768]{2,1,0:T(8,128)(2,1)} %bitcast.62, bf16[2,656,3072]{2,1,0:T(8,128)(2,1)} %bitcast.59, ...), custom_call_target="tpu_custom_call" | custom-call | flops 15000000512 | bytes 62914560 | tf_op jit(solution)/shard_map/weight_shares/pallas_call | solution.py:935
  325.6 51.4 %attention_replay.2 = (bf16[8,328,384]{2,1,0:T(8,128)(2,1)}, f32[64,256]{1,0:T(8,128)}) custom-call(s32[50]{0:T(128)} %places.19, s32[1]{0:T(128)} %bitcast.me, bf16[8,328,128]{2,1,0:T(8,128)(2,1)} %copy-done.6, bf16[3,4096,64]{2,1,0:T(8,128)(2,1)} %get-tuple-element.150.kept, f32[4096,128]{1,0:T(8,128)} %get-tuple-element.129.saved, ...), custom_call_target="tpu_custom_call" | custom-call | flops 42949672960 | bytes 46137344 | tf_op jit(solution)/shard_map/attention_replay/pallas_call | solution.py:736
  382.2 51.7 %attention_replay.3 = (bf16[8,328,384]{2,1,0:T(8,128)(2,1)}, f32[64,256]{1,0:T(8,128)}) custom-call(s32[50]{0:T(128)} %places.19, s32[1]{0:T(128)} %bitcast.me, bf16[8,328,256]{2,1,0:T(8,128)(2,1)} %copy-done.4, bf16[3,4096,64]{2,1,0:T(8,128)(2,1)} %get-tuple-element.162.kept, f32[4096,128]{1,0:T(8,128)} %get-tuple-element.163.saved, ...), custom_call_target="tpu_custom_call" | custom-call | flops 42949672960 | bytes 46137344 | tf_op jit(solution)/shard_map/attention_replay/pallas_call | solution.py:736
  439.4 6.1 convert_add_fusion
  445.5 58.0 %attention_backward.1 = (bf16[8,328,384]{2,1,0:T(8,128)(2,1)}, f32[64,256]{1,0:T(8,128)}) custom-call(s32[50]{0:T(128)} %places.19, s32[1]{0:T(128)} %bitcast.me, s32[2,2]{1,0:T(2,128)} %extent.7, bf16[8,328,256]{2,1,0:T(8,128)(2,1)} %copy-done.4, bf16[3,4096,64]{2,1,0:T(8,128)(2,1)} %get-tuple-element.172.kept, f32[4096,128]{1,0:T(8,128)} %get-tuple-element.173.saved, ...), custom_call_target="tpu_custom_call" | custom-call | flops 42949672960 | bytes 12582912 | tf_op jit(solution)/shard_map/attention_backward/pallas_call | solution.py:612
  511.0 8.0 %collect.3 = (f32[2,656,768]{2,1,0:T(8,128)}, f32[8,768]{1,0:T(8,128)}, bf16[8,24,768]{2,1,0:T(8,128)(2,1)}, bf16[8,24,768]{2,1,0:T(8,128)(2,1)}, bf16[8,24,768]...) custom-call(s32[1]{0:T(128)} %bitcast.4.own, bf16[8,328,384]{2,1,0:T(8,128)(2,1)} %all-to-all-done.7.arrived, ...), custom_call_target="tpu_custom_call" | custom-call | flops 8000000000 | bytes 20971520 | tf_op jit(solution)/shard_map/collect/pallas_call | solution.py:1023
  522.4 8.9 %collect.4 = (f32[2,656,768]{2,1,0:T(8,128)}, f32[8,768]{1,0:T(8,128)}, bf16[8,24,768]{2,1,0:T(8,128)(2,1)}, bf16[8,24,768]{2,1,0:T(8,128)(2,1)}, bf16[8,24,768]...) custom-call(s32[1]{0:T(128)} %bitcast.4.own, bf16[8,328,384]{2,1,0:T(8,128)(2,1)} %all-to-all-done.8.arrived, ...), custom_call_target="tpu_custom_call" | custom-call | flops 8000000000 | bytes 20971520 | tf_op jit(solution)/shard_map/collect/pallas_call | solution.py:1023
  537.9 6.9 %leave.2 = bf16[7,196,768]{2,1,0:T(8,128)(2,1)} custom-call(s32[50]{0:T(128)} %places.19, s32[1]{0:T(128)} %bitcast.me, f32[2,656,768]{2,1,0:T(8,128)} %bitcast.41), custom_call_target="tpu_custom_call" | custom-call | flops 1048576 | bytes 12582912 | tf_op jit(solution)/shard_map/leave/pallas_call | solution.py:263
  551.5 9.5 %all-gather.8.cloned.1.call-done = bf16[864,768]{1,0:T(8,128)(2,1)} async-done(((bf16[216,768]{1,0:T(8,128)(2,1)}), bf16[864,768]{1,0:T(8,128)(2,1)}) %all-gather.8.cloned.1.call-update) | async-done | bytes 1327120 | tf_op jit(solution)/shard_map/all_gather | solution.py:1191
  562.6 12.1 %collect.5 = (f32[2,656,768]{2,1,0:T(8,128)}, f32[8,2304]{1,0:T(8,128)}, bf16[8,24,768]{2,1,0:T(8,128)(2,1)}, bf16[8,24,768]{2,1,0:T(8,128)(2,1)}, bf16[8,24,768...) custom-call(s32[1]{0:T(128)} %bitcast.4.own, bf16[8,328,384]{2,1,0:T(8,128)(2,1)} %all-to-all-done.9.arrived, ...), custom_call_target="tpu_custom_call" | custom-call | flops 8000000000 | bytes 20971520 | tf_op jit(solution)/shard_map/collect/pallas_call | solution.py:1023
  605.4 20.3 %all-gather.3 = f32[8,34,768]{2,1,0:T(8,128)} all-gather(f32[1,34,768]{2,1,0:T(8,128)S(1)} %maximum_bitcast_fusion), channel_id=3, replica_groups=mesh['dp'=4,'wide'=8] {'wide'}, dimensions={0}, use_global_device_ids=true | all-gather | bytes 940032 | tf_op jit(solution)/shard_map/all_gather | solution.py:1220
  638.0 7.3 %leave.3 = f32[7,196,768]{2,1,0:T(8,128)} custom-call(s32[50]{0:T(128)} %places.19, s32[1]{0:T(128)} %bitcast.me, f32[2,656,768]{2,1,0:T(8,128)} %get-tuple-element.219.values), custom_call_target="tpu_custom_call" | custom-call | flops 1048576 | bytes 12582912 | tf_op jit(solution)/shard_map/leave/pallas_call | solution.py:263
  645.3 13.9 %all-gather.10.cloned.1.call-done = f32[4,106,768]{2,1,0:T(8,128)} async-done(((f32[1,106,768]{2,1,0:T(8,128)}), f32[4,106,768]{2,1,0:T(8,128)}) %all-gather.10.cloned.1.call-update) | async-done | bytes 1302544 | tf_op jit(solution)/shard_map/all_gather | solution.py:1226
  (161 shorter events, 127.3 us)
Async XLA Ops:
  18.1 53.6 %all-to-all-start = ((bf16[8,328,384]{2,1,0:T(8,128)(2,1)}), bf16[8,328,384]{2,1,0:T(8,128)(2,1)S(1)}, u32[]{:S(2)}, u32[]{:S(2)}) async-start(bf16[8,328,384]{2,1,0:T(8,128)(2,1)} %get-tuple-element.122), calls=%async_computation | async-start | bytes 4030464 | tf_op jit(solution)/shard_map/all_to_all | solution.py:1050
  73.0 51.0 %all-to-all-start.1 = ((bf16[8,328,384]{2,1,0:T(8,128)(2,1)}), bf16[8,328,384]{2,1,0:T(8,128)(2,1)S(1)}, u32[]{:S(2)}, u32[]{:S(2)}) async-start(bf16[8,328,384]{2,1,0:T(8,128)(2,1)} %get-tuple-element.123), calls=%async_computation.1 | async-start | bytes 4030464 | tf_op jit(solution)/shard_map/all_to_all | solution.py:1050
  124.1 52.1 %all-to-all-start.2 = ((bf16[8,328,384]{2,1,0:T(8,128)(2,1)}), bf16[8,328,384]{2,1,0:T(8,128)(2,1)}, u32[]{:S(2)}, u32[]{:S(2)}) async-start(bf16[8,328,384]{2,1,0:T(8,128)(2,1)} %get-tuple-element.130), calls=%async_computation.2 | async-start | bytes 4030464 | tf_op jit(solution)/shard_map/all_to_all | solution.py:1050
  176.1 36.6 %all-to-all-start.3 = ((bf16[8,328,256]{2,1,0:T(8,128)(2,1)}), bf16[8,328,256]{2,1,0:T(8,128)(2,1)S(1)}, u32[]{:S(2)}, u32[]{:S(2)}) async-start(bf16[8,328,256]{2,1,0:T(8,128)(2,1)} %get-tuple-element.133), calls=%async_computation.3 | async-start | bytes 2686976 | tf_op jit(solution)/shard_map/all_to_all | solution.py:1050
  212.7 22.2 %all-to-all-start.4 = ((bf16[8,328,128]{2,1,0:T(8,128)(2,1)}), bf16[8,328,128]{2,1,0:T(8,128)(2,1)S(1)}, u32[]{:S(2)}, u32[]{:S(2)}) async-start(bf16[8,328,128]{2,1,0:T(8,128)(2,1)} %get-tuple-element.135), calls=%async_computation.4 | async-start | bytes 1343488 | tf_op jit(solution)/shard_map/all_to_all | solution.py:1050
  281.3 34.8 %all-to-all-start.5 = ((bf16[8,328,128]{2,1,0:T(8,128)(2,1)}), bf16[8,328,128]{2,1,0:T(8,128)(2,1)S(1)}, u32[]{:S(2)}, u32[]{:S(2)}) async-start(bf16[8,328,128]{2,1,0:T(8,128)(2,1)} %get-tuple-element.148), calls=%async_computation.5 | async-start | bytes 1343488 | tf_op jit(solution)/shard_map/all_to_all | solution.py:1050
  316.1 60.9 %all-to-all-start.6 = ((bf16[8,328,256]{2,1,0:T(8,128)(2,1)}), bf16[8,328,256]{2,1,0:T(8,128)(2,1)S(1)}, u32[]{:S(2)}, u32[]{:S(2)}) async-start(bf16[8,328,256]{2,1,0:T(8,128)(2,1)} %get-tuple-element.154), calls=%async_computation.6 | async-start | bytes 2686976 | tf_op jit(solution)/shard_map/all_to_all | solution.py:1050
  321.2 118.1 %collective-permute-start = (bf16[8,216,768]{2,1,0:T(8,128)(2,1)}, bf16[8,216,768]{2,1,0:T(8,128)(2,1)}, u32[]{:S(2)}, u32[]{:S(2)}) collective-permute-start(bf16[8,216,768]{2,1,0:T(8,128)(2,1)} %get-tuple-element.159), channel_id=1, source_target_pairs={{0,8},{8,16},{16,24},{24,0},{1,9},{9,17},{17,25},{25,1},{2,10},{10... | collective-permute-start | bytes 7962632 | tf_op jit(solution)/shard_map/ppermute | solution.py:1063
  322.7 116.7 %collective-permute-start.1 = (bf16[8,216,768]{2,1,0:T(8,128)(2,1)}, bf16[8,216,768]{2,1,0:T(8,128)(2,1)}, u32[]{:S(2)}, u32[]{:S(2)}) collective-permute-start(bf16[8,216,768]{2,1,0:T(8,128)(2,1)} %get-tuple-element.160), channel_id=1, source_target_pairs={{0,16},{8,24},{16,0},{24,8},{1,17},{9,25},{17,1},{25,9},{2,18},{10... | collective-permute-start | bytes 7962632 | tf_op jit(solution)/shard_map/ppermute | solution.py:1063
  324.2 115.2 %collective-permute-start.2 = (bf16[8,216,768]{2,1,0:T(8,128)(2,1)}, bf16[8,216,768]{2,1,0:T(8,128)(2,1)}, u32[]{:S(2)}, u32[]{:S(2)}) collective-permute-start(bf16[8,216,768]{2,1,0:T(8,128)(2,1)} %get-tuple-element.161), channel_id=1, source_target_pairs={{0,24},{8,0},{16,8},{24,16},{1,25},{9,1},{17,9},{25,17},{2,26},{10... | collective-permute-start | bytes 7962632 | tf_op jit(solution)/shard_map/ppermute | solution.py:1063
  377.0 56.8 %all-to-all-start.7 = ((bf16[8,328,384]{2,1,0:T(8,128)(2,1)}), bf16[8,328,384]{2,1,0:T(8,128)(2,1)}, u32[]{:S(2)}, u32[]{:S(2)}) async-start(bf16[8,328,384]{2,1,0:T(8,128)(2,1)} %get-tuple-element.156), calls=%async_computation.7 | async-start | bytes 4030464 | tf_op jit(solution)/shard_map/all_to_all | solution.py:1050
  433.9 72.7 %all-to-all-start.8 = ((bf16[8,328,384]{2,1,0:T(8,128)(2,1)}), bf16[8,328,384]{2,1,0:T(8,128)(2,1)}, u32[]{:S(2)}, u32[]{:S(2)}) async-start(bf16[8,328,384]{2,1,0:T(8,128)(2,1)} %get-tuple-element.166), calls=%async_computation.8 | async-start | bytes 4030464 | tf_op jit(solution)/shard_map/all_to_all | solution.py:1050
  439.3 83.0 %reduce-scatter.2.cloned.1.call-start = ((), (), s32[]{:S(2)}) async-start(), calls=%async_computation.13 | async-start | bytes 2985984 | tf_op jit(solution)/shard_map/reduce_scatter | solution.py:1189
  506.6 56.0 %all-to-all-start.9 = ((bf16[8,328,384]{2,1,0:T(8,128)(2,1)}), bf16[8,328,384]{2,1,0:T(8,128)(2,1)}, u32[]{:S(2)}, u32[]{:S(2)}) async-start(bf16[8,328,384]{2,1,0:T(8,128)(2,1)} %get-tuple-element.175), calls=%async_computation.9 | async-start | bytes 4030464 | tf_op jit(solution)/shard_map/all_to_all | solution.py:1050
  510.9 50.1 %all-gather.8.cloned.1.call-start = ((), (), s32[]{:S(2)}) async-start(), calls=%async_computation.14 | async-start | bytes 1658880 | tf_op jit(solution)/shard_map/all_gather | solution.py:1191
  519.5 26.6 %collective-permute-start.4 = (bf16[8,24,768]{2,1,0:T(8,128)(2,1)}, bf16[8,24,768]{2,1,0:T(8,128)(2,1)S(1)}, u32[]{:S(2)}, u32[]{:S(2)}) collective-permute-start(bf16[8,24,768]{2,1,0:T(8,128)(2,1)} %get-tuple-element.181), channel_id=1, source_target_pairs={{0,16},{8,24},{16,0},{24,8},{1,17},{9,25},{17,1},{25,9},{2,18},{10... | collective-permute-start | bytes 884744 | tf_op jit(solution)/shard_map/ppermute | solution.py:1063
  519.5 26.6 %collective-permute-start.5 = (bf16[8,24,768]{2,1,0:T(8,128)(2,1)}, bf16[8,24,768]{2,1,0:T(8,128)(2,1)S(1)}, u32[]{:S(2)}, u32[]{:S(2)}) collective-permute-start(bf16[8,24,768]{2,1,0:T(8,128)(2,1)} %get-tuple-element.182), channel_id=1, source_target_pairs={{0,24},{8,0},{16,8},{24,16},{1,25},{9,1},{17,9},{25,17},{2,26},{10... | collective-permute-start | bytes 884744 | tf_op jit(solution)/shard_map/ppermute | solution.py:1063
  531.3 14.9 %collective-permute-start.6 = (bf16[8,24,768]{2,1,0:T(8,128)(2,1)}, bf16[8,24,768]{2,1,0:T(8,128)(2,1)S(1)}, u32[]{:S(2)}, u32[]{:S(2)}) collective-permute-start(bf16[8,24,768]{2,1,0:T(8,128)(2,1)} %get-tuple-element.185), channel_id=1, source_target_pairs={{0,8},{8,16},{16,24},{24,0},{1,9},{9,17},{17,25},{25,1},{2,10},{10... | collective-permute-start | bytes 884744 | tf_op jit(solution)/shard_map/ppermute | solution.py:1063
  531.6 19.6 %collective-permute-start.7 = (bf16[8,24,768]{2,1,0:T(8,128)(2,1)}, bf16[8,24,768]{2,1,0:T(8,128)(2,1)S(1)}, u32[]{:S(2)}, u32[]{:S(2)}) collective-permute-start(bf16[8,24,768]{2,1,0:T(8,128)(2,1)} %get-tuple-element.186), channel_id=1, source_target_pairs={{0,16},{8,24},{16,0},{24,8},{1,17},{9,25},{17,1},{25,9},{2,18},{10... | collective-permute-start | bytes 884744 | tf_op jit(solution)/shard_map/ppermute | solution.py:1063
  533.1 18.1 %collective-permute-start.8 = (bf16[8,24,768]{2,1,0:T(8,128)(2,1)}, bf16[8,24,768]{2,1,0:T(8,128)(2,1)S(1)}, u32[]{:S(2)}, u32[]{:S(2)}) collective-permute-start(bf16[8,24,768]{2,1,0:T(8,128)(2,1)} %get-tuple-element.187), channel_id=1, source_target_pairs={{0,24},{8,0},{16,8},{24,16},{1,25},{9,1},{17,9},{25,17},{2,26},{10... | collective-permute-start | bytes 884744 | tf_op jit(solution)/shard_map/ppermute | solution.py:1063
  576.4 22.6 %all-to-all-start.10 = ((bf16[8,24,1536]{2,1,0:T(8,128)(2,1)}), bf16[8,24,1536]{2,1,0:T(8,128)(2,1)S(1)}, u32[]{:S(2)}, u32[]{:S(2)}) async-start(bf16[8,24,1536]{2,1,0:T(8,128)(2,1)} %pad_maximum_fusion), calls=%async_computation.11 | async-start | bytes 1179648 | tf_op jit(solution)/shard_map/all_to_all | solution.py:1050
  583.9 14.2 %collective-permute-start.9 = (bf16[8,24,768]{2,1,0:T(8,128)(2,1)}, bf16[8,24,768]{2,1,0:T(8,128)(2,1)S(1)}, u32[]{:S(2)}, u32[]{:S(2)}) collective-permute-start(bf16[8,24,768]{2,1,0:T(8,128)(2,1)} %get-tuple-element.200), channel_id=1, source_target_pairs={{0,8},{8,16},{16,24},{24,0},{1,9},{9,17},{17,25},{25,1},{2,10},{10... | collective-permute-start | bytes 884744 | tf_op jit(solution)/shard_map/ppermute | solution.py:1063
  599.0 29.4 %all-to-all-start.11 = ((bf16[8,24,768]{2,1,0:T(8,128)(2,1)}), bf16[8,24,768]{2,1,0:T(8,128)(2,1)S(1)}, u32[]{:S(2)}, u32[]{:S(2)}) async-start(bf16[8,24,768]{2,1,0:T(8,128)(2,1)} %add_convert_fusion), calls=%async_computation.12 | async-start | bytes 589824 | tf_op jit(solution)/shard_map/all_to_all | solution.py:1050
  603.8 55.4 %all-gather.10.cloned.1.call-start = ((), (), s32[]{:S(2)}) async-start(), calls=%async_computation.15 | async-start | bytes 1720320 | tf_op jit(solution)/shard_map/all_gather | solution.py:1226
  (26 other events, 463.3 us)
Sparse Core Ops, SparseCore 0:
  445.6 64.3 reduce-scatter.1
  522.4 38.6 all-gather.7
  631.2 27.9 all-gather.9

commit v5 on v4

--- a/solution.py
+++ b/solution.py
@@ -1209,32 +1209,34 @@
     totals, sums2, blocks = gather(
         2, *fixed, arrived, normed1, qkv_weight, totals, fold(grad_middle), x, wide_f(norm1_gain)
     )
-    weight_grad = add_groups(around(blocks)).astype(BF)
-    third = [c[:D].reshape(3, 256) for c in (sums0, sums1, sums2)]
-    late = jnp.concatenate([sums2[D:]] + [t[0] for t in third] + [t[2] for t in third])
-    weight_grad, early_sums, late, totals, shares = lax.optimization_barrier(
-        (weight_grad, early_sums, late, totals, shares)
-    )
-    last = exchange(weight_grad)
-    small = jnp.concatenate([late.reshape(-1, D), mid], axis=0)
-    small = jnp.sum(lax.all_gather(small, "wide", axis=0, tiled=False), axis=0)
+    got2 = around(blocks)
     share = D // wide
     piece = share // groups
-    weight_sums = jnp.concatenate([add_wide(early_sums), add_wide(last)], axis=1)
-    last = jnp.concatenate([weight_sums.reshape(-1, D), small], axis=0)
-    totals, shares, last = lax.optimization_barrier((totals, shares, last))
-    last = lax.all_gather(last, "dp", axis=0, tiled=False)
-    qkv_weight_grad = last[:, : 3 * piece].reshape(share, CHUNKS, 3, 256)
-    qkv_weight_grad = qkv_weight_grad.transpose(0, 2, 1, 3).reshape(share, 3 * D)
-    sums = jnp.sum(last[:, 3 * piece :], axis=0).reshape(-1)
-    late, sums = (sums[: 4 * D], sums[4 * D :])
     tokens_grad = leave(plan, window_place, me, totals, slots, F32)
-    rel_total = sums[8 * D : 8 * D + HDIM * 256].reshape(HDIM, 256).T
-    small = sums[: 8 * D]
+    fc1_share = shares[:, :share].transpose(1, 0, 2).reshape(share, 4 * D)
     fc2_share = shares[:, share : 2 * share]
     if aligned:
         fc2_share = fc2_share.reshape(groups, share, 2, 4 * share).transpose(3, 0, 2, 1)
     fc2_share = fc2_share.reshape(4 * share, D)
+    out_share = shares[:, 2 * share :].reshape(share, D)
+    third = [c[:D].reshape(3, 256) for c in (sums0, sums1, sums2)]
+    late = jnp.concatenate([sums2[D:]] + [t[0] for t in third] + [t[2] for t in third])
+    small = jnp.concatenate([late.reshape(-1, D), mid], axis=0)
+    *got2, tokens_grad, fc1_share, fc2_share, out_share, small = lax.optimization_barrier(
+        (*got2, tokens_grad, fc1_share, fc2_share, out_share, small)
+    )
+    weight_grad = add_groups(got2).astype(BF)
+    weight_grad, early_sums, small = lax.optimization_barrier((weight_grad, early_sums, small))
+    last = exchange(weight_grad)
+    small = jnp.sum(lax.all_gather(small, "wide", axis=0, tiled=False), axis=0)
+    small = jnp.sum(lax.all_gather(small, "dp", axis=0, tiled=False), axis=0).reshape(-1)
+    weight_sums = jnp.concatenate([add_wide(early_sums), add_wide(last)], axis=1)
+    last = lax.all_gather(weight_sums, "dp", axis=0, tiled=True)
+    qkv_weight_grad = last.reshape(share, CHUNKS, 3, 256)
+    qkv_weight_grad = qkv_weight_grad.transpose(0, 2, 1, 3).reshape(share, 3 * D)
+    late, sums = (small[: 4 * D], small[4 * D :])
+    rel_total = sums[8 * D : 8 * D + HDIM * 256].reshape(HDIM, 256).T
+    small = sums[: 8 * D]
     return (
         tokens_out,
         tokens_grad,
@@ -1244,11 +1246,11 @@
         late[2 * D :].reshape(2, D),
         rel_total[:127][::-1],
         rel_total[128:255],
-        shares[:, 2 * share :].reshape(share, D),
+        out_share,
         small[:D],
         small[D : 2 * D],
         small[2 * D : 3 * D],
-        shares[:, :share].transpose(1, 0, 2).reshape(share, 4 * D),
+        fc1_share,
         small[3 * D : 7 * D],
         fc2_share,
         small[7 * D :],

time: 679 us -> 670 us (0.987)
  blocking collectives: 20.3 us -> 43.3 us
  waiting for transfers between devices: 107 us -> 90.4 us
  local copies, waits for them, and re-layouts: 35.3 us -> 24.7 us
    all_gather x0 -> x2, blocking collectives: none -> 22 us  [the longest x1 11.9 us: shards(): last = lax.all_gather(weight_sums, 'dp', axis=0, tiled=True)]
    all_gather x1 -> x0, waiting for transfers between devices: 13.9 us -> none  [shards(): last = lax.all_gather(last, 'dp', axis=0, tiled=False)]
    unnamed x54 -> x56, local copies, waits for them, and re-layouts: 11.7 us -> 3.93 us
  transfers between devices with their start and end apart: 27 -> 26, of which waited for: 11 -> 10; matrix products, arithmetic and copies ran while one was open for 5% -> 4% of each run, Pallas kernels for 51% -> 51%
where the time goes in v5:
time: 670 us; the launch traced here: 665 us
  Pallas kernels  406 us (61%)
  waiting for transfers between devices  90.4 us (13%)
  starting transfers between devices  71.7 us (11%)
  blocking collectives  43.3 us (6%)
  local copies, waits for them, and re-layouts  24.7 us (4%)
  between operations  15.1 us (2%)
  other arithmetic  14 us (2%)
    pallas_call x3, Pallas kernels, attention_forward(): pl.pallas_call(partial(forward_kernel, plan, tile, slot_count, keep), out...  109 us
    pallas_call x2, Pallas kernels, attention_replay(): pl.pallas_call(partial(replay_kernel, plan, tile, slot_count), out_shape=...  103 us
    all_to_all x12, waiting for transfers between devices, exchange(): return lax.all_to_all(blocks, axis, split_axis=0, concat_axis=0, tiled=True)  74 us
    pallas_call x1, Pallas kernels, attention_backward(): pl.pallas_call(partial(backward_kernel, plan, tile, slot_count), out_shap...  57.9 us
    all_to_all x12, starting transfers between devices, exchange(): return lax.all_to_all(blocks, axis, split_axis=0, concat_axis=0, tiled=True)  55.6 us
    pallas_call x1, Pallas kernels, middle_part(): pl.pallas_call(partial(middle_kernel, plan), out_shape=(made(D, BF), made...  45.5 us
    pallas_call x1, Pallas kernels, weight_shares(): pl.pallas_call(partial(shares_kernel, plan, groups), out_shape=[shape(blo...  30.8 us
    pallas_call x3, Pallas kernels, collect(): pl.pallas_call(partial(collect_kernel, plan, chunk, groups, None), out_sh...  28.9 us
  transfers between devices with their start and end apart: 26, of which 10 were waited for; matrix products, arithmetic and copies ran while one was open for 4% of the time, Pallas kernels for 51%

profile of v5, /device:TPU:0, one launch (start us, length us, event | category | flops | bytes accessed | tf_op | source)
XLA Modules:
  0.0 664.7 jit_solution(14131886135830607875)
XLA Ops:
  11.1 7.0 %enter.1 = (bf16[2,656,768]{2,1,0:T(8,128)(2,1)}, bf16[2,656,768]{2,1,0:T(8,128)(2,1)}, bf16[8,328,384]{2,1,0:T(8,128)(2,1)}) custom-call(s32[50]{0:T(128)} %places.19, s32[1]{0:T(128)} %bitcast.me, bf16[7,196,768]{2,1,0:T(8,128)(2,1)} %refs_3_.2, bf16[7,196,768]{2,1,0:T(8,128)(2,1)} %refs_3_.2, bf16[7,196,768]{2,1,0:T(8,128)(2,1)} %refs_3_.2, ...), custom_call_target="tpu_custom_call" | custom-call | flops 2000000000 | bytes 10485760 | tf_op jit(solution)/shard_map/enter/pallas_call | solution.py:186
  18.1 6.3 all-to-all-start
  24.4 9.1 %follow.1 = (bf16[2,656,768]{2,1,0:T(8,128)(2,1)}, bf16[8,328,384]{2,1,0:T(8,128)(2,1)}, bf16[8,328,384]{2,1,0:T(8,128)(2,1)}) custom-call(s32[50]{0:T(128)} %places.19, s32[1]{0:T(128)} %bitcast.me, bf16[7,196,768]{2,1,0:T(8,128)(2,1)} %refs_3_.3, bf16[7,196,768]{2,1,0:T(8,128)(2,1)} %refs_3_.3, bf16[7,196,768]{2,1,0:T(8,128)(2,1)} %refs_3_.3, ...), custom_call_target="tpu_custom_call" | custom-call | flops 4000000000 | bytes 16777216 | tf_op jit(solution)/shard_map/follow/pallas_call | solution.py:209
  33.6 38.2 %all-to-all-done.arrived = bf16[8,328,384]{2,1,0:T(8,128)(2,1)S(1)} async-done(((bf16[8,328,384]{2,1,0:T(8,128)(2,1)}), bf16[8,328,384]{2,1,0:T(8,128)(2,1)S(1)}, u32[]{:S(2)}, u32[]{:S(2)}) %all-to-all-start) | async-done | bytes 2015264 | tf_op jit(solution)/shard_map/all_to_all | solution.py:1050
  77.9 38.7 %attention_forward.3 = (bf16[8,328,128]{2,1,0:T(8,128)(2,1)}, bf16[3,4096,64]{2,1,0:T(8,128)(2,1)}, f32[4096,128]{1,0:T(8,128)}, bf16[4096,4096]{1,0:T(8,128)(2,1)}) custom-call(s32[50]{0:T(128)} %places.19, s32[1]{0:T(128)} %bitcast.me, s32[2,2]{1,0:T(2,128)} %extent.7, bf16[8,328,384]{2,1,0:T(8,128)(2,1)} %copy-done.3, ...), custom_call_target="tpu_custom_call" | custom-call | flops 17179869184 | bytes 12582912 | tf_op jit(solution)/shard_map/attention_forward/pallas_call | solution.py:483
  116.7 7.4 %all-to-all-done.1.arrived = bf16[8,328,384]{2,1,0:T(8,128)(2,1)S(1)} async-done(((bf16[8,328,384]{2,1,0:T(8,128)(2,1)}), bf16[8,328,384]{2,1,0:T(8,128)(2,1)S(1)}, u32[]{:S(2)}, u32[]{:S(2)}) %all-to-all-start.1) | async-done | bytes 2015264 | tf_op jit(solution)/shard_map/all_to_all | solution.py:1050
  128.8 39.3 %attention_forward.4 = (bf16[8,328,256]{2,1,0:T(8,128)(2,1)}, bf16[3,4096,64]{2,1,0:T(8,128)(2,1)}, f32[4096,128]{1,0:T(8,128)}, bf16[4096,4096]{1,0:T(8,128)(2,1)}) custom-call(s32[50]{0:T(128)} %places.19, s32[1]{0:T(128)} %bitcast.me, s32[2,2]{1,0:T(2,128)} %extent.7, bf16[8,328,384]{2,1,0:T(8,128)(2,1)} %copy-done.2, ...), custom_call_target="tpu_custom_call" | custom-call | flops 17179869184 | bytes 12582912 | tf_op jit(solution)/shard_map/attention_forward/pallas_call | solution.py:483
  168.1 8.0 %all-to-all-done.2.arrived = bf16[8,328,384]{2,1,0:T(8,128)(2,1)} async-done(((bf16[8,328,384]{2,1,0:T(8,128)(2,1)}), bf16[8,328,384]{2,1,0:T(8,128)(2,1)}, u32[]{:S(2)}, u32[]{:S(2)}) %all-to-all-start.2) | async-done | bytes 2015264 | tf_op jit(solution)/shard_map/all_to_all | solution.py:1050
  180.0 31.0 %attention_forward.5 = (bf16[8,328,128]{2,1,0:T(8,128)(2,1)}, bf16[3,4096,64]{2,1,0:T(8,128)(2,1)}, f32[4096,128]{1,0:T(8,128)}) custom-call(s32[50]{0:T(128)} %places.19, s32[1]{0:T(128)} %bitcast.me, s32[2,2]{1,0:T(2,128)} %extent.7, bf16[8,328,384]{2,1,0:T(8,128)(2,1)} %all-to-all-done.2.arrived, bf16[256,64]{1,0:T(8,128)(2,1)} %get-tuple-element.291.table), custom_call_target="tpu_custom_call" | custom-call | flops 17179869184 | bytes 12582912 | tf_op jit(solution)/shard_map/attention_forward/pallas_call | solution.py:483
  219.4 15.5 %all-to-all-done.4.last = bf16[8,328,128]{2,1,0:T(8,128)(2,1)S(1)} async-done(((bf16[8,328,128]{2,1,0:T(8,128)(2,1)}), bf16[8,328,128]{2,1,0:T(8,128)(2,1)S(1)}, u32[]{:S(2)}, u32[]{:S(2)}) %all-to-all-start.4) | async-done | bytes 671776 | tf_op jit(solution)/shard_map/all_to_all | solution.py:1050
  235.8 45.5 %middle.1 = (bf16[4,328,768]{2,1,0:T(8,128)(2,1)}, bf16[4,328,768]{2,1,0:T(8,128)(2,1)}, bf16[4,328,3072]{2,1,0:T(8,128)(2,1)}, bf16[4,328,3072]{2,1,0:T(8,128)(...) custom-call(bf16[8,328,256]{2,1,0:T(8,128)(2,1)} %copy-done.5, ...), custom_call_target="tpu_custom_call" | custom-call | flops 30000001024 | bytes 41943040 | tf_op jit(solution)/shard_map/middle/pallas_call | solution.py:849
  285.3 30.8 %weight_shares.1 = (bf16[8,216,768]{2,1,0:T(8,128)(2,1)}, bf16[8,216,768]{2,1,0:T(8,128)(2,1)}, bf16[8,216,768]{2,1,0:T(8,128)(2,1)}, bf16[8,216,768]{2,1,0:T(8,128)(2,1)}) custom-call(s32[1]{0:T(128)} %bitcast.4.own, bf16[2,656,768]{2,1,0:T(8,128)(2,1)} %bitcast.62, bf16[2,656,3072]{2,1,0:T(8,128)(2,1)} %bitcast.59, ...), custom_call_target="tpu_custom_call" | custom-call | flops 15000000512 | bytes 62914560 | tf_op jit(solution)/shard_map/weight_shares/pallas_call | solution.py:935
  325.6 51.4 %attention_replay.2 = (bf16[8,328,384]{2,1,0:T(8,128)(2,1)}, f32[64,256]{1,0:T(8,128)}) custom-call(s32[50]{0:T(128)} %places.19, s32[1]{0:T(128)} %bitcast.me, bf16[8,328,128]{2,1,0:T(8,128)(2,1)} %copy-done.6, bf16[3,4096,64]{2,1,0:T(8,128)(2,1)} %get-tuple-element.154.kept, f32[4096,128]{1,0:T(8,128)} %get-tuple-element.133.saved, ...), custom_call_target="tpu_custom_call" | custom-call | flops 42949672960 | bytes 46137344 | tf_op jit(solution)/shard_map/attention_replay/pallas_call | solution.py:736
  382.2 51.7 %attention_replay.3 = (bf16[8,328,384]{2,1,0:T(8,128)(2,1)}, f32[64,256]{1,0:T(8,128)}) custom-call(s32[50]{0:T(128)} %places.19, s32[1]{0:T(128)} %bitcast.me, bf16[8,328,256]{2,1,0:T(8,128)(2,1)} %copy-done.4, bf16[3,4096,64]{2,1,0:T(8,128)(2,1)} %get-tuple-element.166.kept, f32[4096,128]{1,0:T(8,128)} %get-tuple-element.167.saved, ...), custom_call_target="tpu_custom_call" | custom-call | flops 42949672960 | bytes 46137344 | tf_op jit(solution)/shard_map/attention_replay/pallas_call | solution.py:736
  445.5 57.9 %attention_backward.1 = (bf16[8,328,384]{2,1,0:T(8,128)(2,1)}, f32[64,256]{1,0:T(8,128)}) custom-call(s32[50]{0:T(128)} %places.19, s32[1]{0:T(128)} %bitcast.me, s32[2,2]{1,0:T(2,128)} %extent.7, bf16[8,328,256]{2,1,0:T(8,128)(2,1)} %copy-done.4, bf16[3,4096,64]{2,1,0:T(8,128)(2,1)} %get-tuple-element.176.kept, f32[4096,128]{1,0:T(8,128)} %get-tuple-element.177.saved, ...), custom_call_target="tpu_custom_call" | custom-call | flops 42949672960 | bytes 12582912 | tf_op jit(solution)/shard_map/attention_backward/pallas_call | solution.py:612
  511.0 8.0 %collect.3 = (f32[2,656,768]{2,1,0:T(8,128)}, f32[8,768]{1,0:T(8,128)}, bf16[8,24,768]{2,1,0:T(8,128)(2,1)}, bf16[8,24,768]{2,1,0:T(8,128)(2,1)}, bf16[8,24,768]...) custom-call(s32[1]{0:T(128)} %bitcast.4.own, bf16[8,328,384]{2,1,0:T(8,128)(2,1)} %all-to-all-done.7.arrived, ...), custom_call_target="tpu_custom_call" | custom-call | flops 8000000000 | bytes 20971520 | tf_op jit(solution)/shard_map/collect/pallas_call | solution.py:1023
  522.4 8.8 %collect.4 = (f32[2,656,768]{2,1,0:T(8,128)}, f32[8,768]{1,0:T(8,128)}, bf16[8,24,768]{2,1,0:T(8,128)(2,1)}, bf16[8,24,768]{2,1,0:T(8,128)(2,1)}, bf16[8,24,768]...) custom-call(s32[1]{0:T(128)} %bitcast.4.own, bf16[8,328,384]{2,1,0:T(8,128)(2,1)} %all-to-all-done.8.arrived, ...), custom_call_target="tpu_custom_call" | custom-call | flops 8000000000 | bytes 20971520 | tf_op jit(solution)/shard_map/collect/pallas_call | solution.py:1023
  537.3 6.9 %leave.2 = bf16[7,196,768]{2,1,0:T(8,128)(2,1)} custom-call(s32[50]{0:T(128)} %places.19, s32[1]{0:T(128)} %bitcast.me, f32[2,656,768]{2,1,0:T(8,128)} %bitcast.40), custom_call_target="tpu_custom_call" | custom-call | flops 1048576 | bytes 12582912 | tf_op jit(solution)/shard_map/leave/pallas_call | solution.py:263
  551.6 9.5 %all-gather.7.cloned.1.call-done = bf16[864,768]{1,0:T(8,128)(2,1)} async-done(((bf16[216,768]{1,0:T(8,128)(2,1)}), bf16[864,768]{1,0:T(8,128)(2,1)}) %all-gather.7.cloned.1.call-update) | async-done | bytes 1327120 | tf_op jit(solution)/shard_map/all_gather | solution.py:1191
  562.6 12.1 %collect.5 = (f32[2,656,768]{2,1,0:T(8,128)}, f32[8,2304]{1,0:T(8,128)}, bf16[8,24,768]{2,1,0:T(8,128)(2,1)}, bf16[8,24,768]{2,1,0:T(8,128)(2,1)}, bf16[8,24,768...) custom-call(s32[1]{0:T(128)} %bitcast.4.own, bf16[8,328,384]{2,1,0:T(8,128)(2,1)} %all-to-all-done.9.arrived, ...), custom_call_target="tpu_custom_call" | custom-call | flops 8000000000 | bytes 20971520 | tf_op jit(solution)/shard_map/collect/pallas_call | solution.py:1023
  591.2 7.3 %leave.3 = f32[7,196,768]{2,1,0:T(8,128)} custom-call(s32[50]{0:T(128)} %places.19, s32[1]{0:T(128)} %bitcast.me, f32[2,656,768]{2,1,0:T(8,128)} %get-tuple-element.207.values), custom_call_target="tpu_custom_call" | custom-call | flops 1048576 | bytes 12582912 | tf_op jit(solution)/shard_map/leave/pallas_call | solution.py:263
  607.2 21.3 %all-gather.3 = f32[8,34,768]{2,1,0:T(8,128)S(1)} all-gather(f32[1,34,768]{2,1,0:T(8,128)S(1)} %bitcast.43), channel_id=3, replica_groups=mesh['dp'=4,'wide'=8] {'wide'}, dimensions={0}, use_global_device_ids=true | all-gather | bytes 940032 | tf_op jit(solution)/shard_map/all_gather | solution.py:1231
  628.6 10.1 %all-gather.4 = f32[4,34,768]{2,1,0:T(8,128)S(1)} all-gather(f32[1,34,768]{2,1,0:T(8,128)S(1)} %bitcast.44), channel_id=4, replica_groups=mesh['dp'=4,'wide'=8] {'dp'}, dimensions={0}, use_global_device_ids=true | all-gather | bytes 522240 | tf_op jit(solution)/shard_map/all_gather | solution.py:1232
  643.2 11.9 %all_gather.27 = f32[96,2304]{1,0:T(8,128)S(1)} all-gather(f32[24,2304]{1,0:T(8,128)S(1)} %pad_maximum_fusion.1), channel_id=1, replica_groups=mesh['dp'=4,'wide'=8] {'dp'}, dimensions={0}, use_global_device_ids=true | all-gather | bytes 1105920 | tf_op jit(solution)/shard_map/all_gather | solution.py:1234
  (158 shorter events, 115.9 us)
Async XLA Ops:
  18.1 53.6 %all-to-all-start = ((bf16[8,328,384]{2,1,0:T(8,128)(2,1)}), bf16[8,328,384]{2,1,0:T(8,128)(2,1)S(1)}, u32[]{:S(2)}, u32[]{:S(2)}) async-start(bf16[8,328,384]{2,1,0:T(8,128)(2,1)} %get-tuple-element.126), calls=%async_computation | async-start | bytes 4030464 | tf_op jit(solution)/shard_map/all_to_all | solution.py:1050
  73.1 51.0 %all-to-all-start.1 = ((bf16[8,328,384]{2,1,0:T(8,128)(2,1)}), bf16[8,328,384]{2,1,0:T(8,128)(2,1)S(1)}, u32[]{:S(2)}, u32[]{:S(2)}) async-start(bf16[8,328,384]{2,1,0:T(8,128)(2,1)} %get-tuple-element.127), calls=%async_computation.1 | async-start | bytes 4030464 | tf_op jit(solution)/shard_map/all_to_all | solution.py:1050
  124.1 52.0 %all-to-all-start.2 = ((bf16[8,328,384]{2,1,0:T(8,128)(2,1)}), bf16[8,328,384]{2,1,0:T(8,128)(2,1)}, u32[]{:S(2)}, u32[]{:S(2)}) async-start(bf16[8,328,384]{2,1,0:T(8,128)(2,1)} %get-tuple-element.134), calls=%async_computation.2 | async-start | bytes 4030464 | tf_op jit(solution)/shard_map/all_to_all | solution.py:1050
  176.1 36.6 %all-to-all-start.3 = ((bf16[8,328,256]{2,1,0:T(8,128)(2,1)}), bf16[8,328,256]{2,1,0:T(8,128)(2,1)S(1)}, u32[]{:S(2)}, u32[]{:S(2)}) async-start(bf16[8,328,256]{2,1,0:T(8,128)(2,1)} %get-tuple-element.137), calls=%async_computation.3 | async-start | bytes 2686976 | tf_op jit(solution)/shard_map/all_to_all | solution.py:1050
  212.7 22.2 %all-to-all-start.4 = ((bf16[8,328,128]{2,1,0:T(8,128)(2,1)}), bf16[8,328,128]{2,1,0:T(8,128)(2,1)S(1)}, u32[]{:S(2)}, u32[]{:S(2)}) async-start(bf16[8,328,128]{2,1,0:T(8,128)(2,1)} %get-tuple-element.139), calls=%async_computation.4 | async-start | bytes 1343488 | tf_op jit(solution)/shard_map/all_to_all | solution.py:1050
  281.3 34.8 %all-to-all-start.5 = ((bf16[8,328,128]{2,1,0:T(8,128)(2,1)}), bf16[8,328,128]{2,1,0:T(8,128)(2,1)S(1)}, u32[]{:S(2)}, u32[]{:S(2)}) async-start(bf16[8,328,128]{2,1,0:T(8,128)(2,1)} %get-tuple-element.152), calls=%async_computation.5 | async-start | bytes 1343488 | tf_op jit(solution)/shard_map/all_to_all | solution.py:1050
  316.1 60.9 %all-to-all-start.6 = ((bf16[8,328,256]{2,1,0:T(8,128)(2,1)}), bf16[8,328,256]{2,1,0:T(8,128)(2,1)S(1)}, u32[]{:S(2)}, u32[]{:S(2)}) async-start(bf16[8,328,256]{2,1,0:T(8,128)(2,1)} %get-tuple-element.158), calls=%async_computation.6 | async-start | bytes 2686976 | tf_op jit(solution)/shard_map/all_to_all | solution.py:1050
  321.2 118.1 %collective-permute-start = (bf16[8,216,768]{2,1,0:T(8,128)(2,1)}, bf16[8,216,768]{2,1,0:T(8,128)(2,1)}, u32[]{:S(2)}, u32[]{:S(2)}) collective-permute-start(bf16[8,216,768]{2,1,0:T(8,128)(2,1)} %get-tuple-element.163), channel_id=1, source_target_pairs={{0,8},{8,16},{16,24},{24,0},{1,9},{9,17},{17,25},{25,1},{2,10},{10... | collective-permute-start | bytes 7962632 | tf_op jit(solution)/shard_map/ppermute | solution.py:1063
  322.7 116.6 %collective-permute-start.1 = (bf16[8,216,768]{2,1,0:T(8,128)(2,1)}, bf16[8,216,768]{2,1,0:T(8,128)(2,1)}, u32[]{:S(2)}, u32[]{:S(2)}) collective-permute-start(bf16[8,216,768]{2,1,0:T(8,128)(2,1)} %get-tuple-element.164), channel_id=1, source_target_pairs={{0,16},{8,24},{16,0},{24,8},{1,17},{9,25},{17,1},{25,9},{2,18},{10... | collective-permute-start | bytes 7962632 | tf_op jit(solution)/shard_map/ppermute | solution.py:1063
  324.2 115.1 %collective-permute-start.2 = (bf16[8,216,768]{2,1,0:T(8,128)(2,1)}, bf16[8,216,768]{2,1,0:T(8,128)(2,1)}, u32[]{:S(2)}, u32[]{:S(2)}) collective-permute-start(bf16[8,216,768]{2,1,0:T(8,128)(2,1)} %get-tuple-element.165), channel_id=1, source_target_pairs={{0,24},{8,0},{16,8},{24,16},{1,25},{9,1},{17,9},{25,17},{2,26},{10... | collective-permute-start | bytes 7962632 | tf_op jit(solution)/shard_map/ppermute | solution.py:1063
  377.0 56.8 %all-to-all-start.7 = ((bf16[8,328,384]{2,1,0:T(8,128)(2,1)}), bf16[8,328,384]{2,1,0:T(8,128)(2,1)}, u32[]{:S(2)}, u32[]{:S(2)}) async-start(bf16[8,328,384]{2,1,0:T(8,128)(2,1)} %get-tuple-element.160), calls=%async_computation.7 | async-start | bytes 4030464 | tf_op jit(solution)/shard_map/all_to_all | solution.py:1050
  433.9 72.7 %all-to-all-start.8 = ((bf16[8,328,384]{2,1,0:T(8,128)(2,1)}), bf16[8,328,384]{2,1,0:T(8,128)(2,1)}, u32[]{:S(2)}, u32[]{:S(2)}) async-start(bf16[8,328,384]{2,1,0:T(8,128)(2,1)} %get-tuple-element.170), calls=%async_computation.8 | async-start | bytes 4030464 | tf_op jit(solution)/shard_map/all_to_all | solution.py:1050
  439.3 83.0 %reduce-scatter.2.cloned.1.call-start = ((), (), s32[]{:S(2)}) async-start(), calls=%async_computation.13 | async-start | bytes 2985984 | tf_op jit(solution)/shard_map/reduce_scatter | solution.py:1189
  506.6 56.0 %all-to-all-start.9 = ((bf16[8,328,384]{2,1,0:T(8,128)(2,1)}), bf16[8,328,384]{2,1,0:T(8,128)(2,1)}, u32[]{:S(2)}, u32[]{:S(2)}) async-start(bf16[8,328,384]{2,1,0:T(8,128)(2,1)} %get-tuple-element.179), calls=%async_computation.9 | async-start | bytes 4030464 | tf_op jit(solution)/shard_map/all_to_all | solution.py:1050
  510.9 50.1 %all-gather.7.cloned.1.call-start = ((), (), s32[]{:S(2)}) async-start(), calls=%async_computation.14 | async-start | bytes 1658880 | tf_op jit(solution)/shard_map/all_gather | solution.py:1191
  519.5 25.4 %collective-permute-start.4 = (bf16[8,24,768]{2,1,0:T(8,128)(2,1)}, bf16[8,24,768]{2,1,0:T(8,128)(2,1)S(1)}, u32[]{:S(2)}, u32[]{:S(2)}) collective-permute-start(bf16[8,24,768]{2,1,0:T(8,128)(2,1)} %get-tuple-element.185), channel_id=1, source_target_pairs={{0,16},{8,24},{16,0},{24,8},{1,17},{9,25},{17,1},{25,9},{2,18},{10... | collective-permute-start | bytes 884744 | tf_op jit(solution)/shard_map/ppermute | solution.py:1063
  519.5 25.4 %collective-permute-start.5 = (bf16[8,24,768]{2,1,0:T(8,128)(2,1)}, bf16[8,24,768]{2,1,0:T(8,128)(2,1)S(1)}, u32[]{:S(2)}, u32[]{:S(2)}) collective-permute-start(bf16[8,24,768]{2,1,0:T(8,128)(2,1)} %get-tuple-element.186), channel_id=1, source_target_pairs={{0,24},{8,0},{16,8},{24,16},{1,25},{9,1},{17,9},{25,17},{2,26},{10... | collective-permute-start | bytes 884744 | tf_op jit(solution)/shard_map/ppermute | solution.py:1063
  531.3 14.9 %collective-permute-start.6 = (bf16[8,24,768]{2,1,0:T(8,128)(2,1)}, bf16[8,24,768]{2,1,0:T(8,128)(2,1)S(1)}, u32[]{:S(2)}, u32[]{:S(2)}) collective-permute-start(bf16[8,24,768]{2,1,0:T(8,128)(2,1)} %get-tuple-element.189), channel_id=1, source_target_pairs={{0,8},{8,16},{16,24},{24,0},{1,9},{9,17},{17,25},{25,1},{2,10},{10... | collective-permute-start | bytes 884744 | tf_op jit(solution)/shard_map/ppermute | solution.py:1063
  531.6 19.7 %collective-permute-start.7 = (bf16[8,24,768]{2,1,0:T(8,128)(2,1)}, bf16[8,24,768]{2,1,0:T(8,128)(2,1)S(1)}, u32[]{:S(2)}, u32[]{:S(2)}) collective-permute-start(bf16[8,24,768]{2,1,0:T(8,128)(2,1)} %get-tuple-element.190), channel_id=1, source_target_pairs={{0,16},{8,24},{16,0},{24,8},{1,17},{9,25},{17,1},{25,9},{2,18},{10... | collective-permute-start | bytes 884744 | tf_op jit(solution)/shard_map/ppermute | solution.py:1063
  533.1 18.2 %collective-permute-start.8 = (bf16[8,24,768]{2,1,0:T(8,128)(2,1)}, bf16[8,24,768]{2,1,0:T(8,128)(2,1)S(1)}, u32[]{:S(2)}, u32[]{:S(2)}) collective-permute-start(bf16[8,24,768]{2,1,0:T(8,128)(2,1)} %get-tuple-element.191), channel_id=1, source_target_pairs={{0,24},{8,0},{16,8},{24,16},{1,25},{9,1},{17,9},{25,17},{2,26},{10... | collective-permute-start | bytes 884744 | tf_op jit(solution)/shard_map/ppermute | solution.py:1063
  577.1 25.4 %all-to-all-start.10 = ((bf16[8,24,1536]{2,1,0:T(8,128)(2,1)}), bf16[8,24,1536]{2,1,0:T(8,128)(2,1)}, u32[]{:S(2)}, u32[]{:S(2)}) async-start(bf16[8,24,1536]{2,1,0:T(8,128)(2,1)} %pad_maximum_fusion), calls=%async_computation.11 | async-start | bytes 1179648 | tf_op jit(solution)/shard_map/all_to_all | solution.py:1050
  581.8 16.8 %collective-permute-start.10 = (bf16[8,24,768]{2,1,0:T(8,128)(2,1)}, bf16[8,24,768]{2,1,0:T(8,128)(2,1)}, u32[]{:S(2)}, u32[]{:S(2)}) collective-permute-start(bf16[8,24,768]{2,1,0:T(8,128)(2,1)} %get-tuple-element.205), channel_id=1, source_target_pairs={{0,16},{8,24},{16,0},{24,8},{1,17},{9,25},{17,1},{25,9},{2,18},{10... | collective-permute-start | bytes 884744 | tf_op jit(solution)/shard_map/ppermute | solution.py:1063
  583.3 15.3 %collective-permute-start.11 = (bf16[8,24,768]{2,1,0:T(8,128)(2,1)}, bf16[8,24,768]{2,1,0:T(8,128)(2,1)}, u32[]{:S(2)}, u32[]{:S(2)}) collective-permute-start(bf16[8,24,768]{2,1,0:T(8,128)(2,1)} %get-tuple-element.206), channel_id=1, source_target_pairs={{0,24},{8,0},{16,8},{24,16},{1,25},{9,1},{17,9},{25,17},{2,26},{10... | collective-permute-start | bytes 884744 | tf_op jit(solution)/shard_map/ppermute | solution.py:1063
  602.5 40.6 %all-to-all-start.11 = ((bf16[8,24,768]{2,1,0:T(8,128)(2,1)}), bf16[8,24,768]{2,1,0:T(8,128)(2,1)S(1)}, u32[]{:S(2)}, u32[]{:S(2)}) async-start(bf16[8,24,768]{2,1,0:T(8,128)(2,1)} %add_convert_fusion), calls=%async_computation.12 | async-start | bytes 589824 | tf_op jit(solution)/shard_map/all_to_all | solution.py:1050
  (25 other events, 438.2 us)
Sparse Core Ops, SparseCore 0:
  445.6 64.3 reduce-scatter.1
  522.4 38.5 all-gather.6
